TPU v7x, 512 devices: a whole 4x8x8 slice. The times are simulated.
512 devices in a mesh: dp: 4 (over x), expert: 128 (over y, z, core).
Axes of the slice: x: 4, y: 8, z: 8, core: 2. Of those that a mesh axis runs over, the one named last changes fastest.
Arguments:
- tokens: bfloat16 [65536, 512], P(('dp', 'expert')), may hold values from -6 to 6
- codes: int32 [65536, 2], P(('dp', 'expert')), may hold values from 0 to 127, as said below
- cotangent: bfloat16 [65536, 512], P(('dp', 'expert')), may hold values from -6 to 6
- w_gate: bfloat16 [128, 512, 1024], P('expert'), may hold values from -0.25 to 0.25
- w_up: bfloat16 [128, 512, 1024], P('expert'), may hold values from -0.25 to 0.25
- w_down: bfloat16 [128, 1024, 512], P('expert'), may hold values from -0.1875 to 0.1875
Outputs:
- head_output: bfloat16 [65536, 512], P(('dp', 'expert'))
- grad_tokens: bfloat16 [65536, 512], P(('dp', 'expert'))
- grad_gate: bfloat16 [128, 512, 1024], P('expert', None, 'dp')
- grad_up: bfloat16 [128, 512, 1024], P('expert', None, 'dp')
- grad_down: bfloat16 [128, 1024, 512], P('expert', 'dp')
Inputs may be any that keep to these rules, and one draw needn't show every extreme that they name: A token's two codes differ. Within each device's 128 tokens (aligned blocks of 128 rows), each arm is named at most 4 times over both columns, and one arm, the same for every block, is named exactly 4 times in every block.
All inputs are finite; a program needn't handle non-finite values.
Results may differ from a plain program's by a relative error of at most 0.009.
Values may be sent and summed in bfloat16 or wider, within the bound.
A program may use at most 64 MiB of HBM per device.

v0:
```python
import jax
import jax.numpy as jnp
from jax import lax
from jax.sharding import PartitionSpec as P

fact_share = 0.7
counter_share = 0.3


def silu_parts(gate_pre):
    sigmoid_gate = jax.nn.sigmoid(gate_pre)
    return (gate_pre * sigmoid_gate, sigmoid_gate * (1.0 + gate_pre * (1.0 - sigmoid_gate)))


def arm_forward(rows_in, gate_w, up_w):
    gate_pre = jnp.einsum("arc,ach->arh", rows_in, gate_w, preferred_element_type=jnp.float32)
    up_pre = jnp.einsum("arc,ach->arh", rows_in, up_w, preferred_element_type=jnp.float32)
    activated, silu_slope = silu_parts(gate_pre)
    hidden = (activated * up_pre).astype(jnp.bfloat16)
    return (up_pre, activated, silu_slope, hidden)


def arm_backward(up_pre, activated, silu_slope, cot_in, down_w):
    d_hidden = jnp.einsum("arc,ahc->arh", cot_in, down_w, preferred_element_type=jnp.float32)
    d_up = (d_hidden * activated).astype(jnp.bfloat16)
    d_gate = (d_hidden * up_pre * silu_slope).astype(jnp.bfloat16)
    return (d_gate, d_up)


def on_device(tokens, codes, cotangent, w_gate, w_up, w_down):
    token_count, feature_width = tokens.shape
    local_arms = w_gate.shape[0]
    arm_count = local_arms * lax.axis_size("expert")
    capacity = 4 * token_count // arm_count
    flat_codes = codes.reshape(-1)
    arm_ids = jnp.arange(arm_count, dtype=jnp.int32)
    onehot = (flat_codes[:, None] == arm_ids[None, :]).astype(jnp.int32)
    earlier = jnp.cumsum(onehot, axis=0) - onehot
    destination = flat_codes * capacity + jnp.sum(earlier * onehot, axis=1)
    shares = jnp.tile(jnp.array([fact_share, counter_share], jnp.float32), token_count)
    token_rows = jnp.repeat(tokens, 2, axis=0)
    cot_rows = (jnp.repeat(cotangent.astype(jnp.float32), 2, axis=0) * shares[:, None]).astype(
        jnp.bfloat16
    )
    blank_rows = jnp.zeros((arm_count * capacity, feature_width), jnp.bfloat16)
    send_tokens = (
        blank_rows.at[destination].set(token_rows).reshape(arm_count, capacity, feature_width)
    )
    send_cot = blank_rows.at[destination].set(cot_rows).reshape(arm_count, capacity, feature_width)
    arm_tokens, arm_cot = (
        lax.all_to_all(send_tokens, "expert", split_axis=0, concat_axis=1, tiled=True),
        lax.all_to_all(send_cot, "expert", split_axis=0, concat_axis=1, tiled=True),
    )
    up_pre, activated, silu_slope, hidden = arm_forward(arm_tokens, w_gate, w_up)
    out_rows = jnp.einsum(
        "arh,ahc->arc", hidden, w_down, preferred_element_type=jnp.float32
    ).astype(jnp.bfloat16)
    d_gate, d_up = arm_backward(up_pre, activated, silu_slope, arm_cot, w_down)
    input_rows = (
        jnp.einsum("arh,ach->arc", d_gate, w_gate, preferred_element_type=jnp.float32)
        + jnp.einsum("arh,ach->arc", d_up, w_up, preferred_element_type=jnp.float32)
    ).astype(jnp.bfloat16)
    back_out, back_input = (
        lax.all_to_all(out_rows, "expert", split_axis=1, concat_axis=0, tiled=True),
        lax.all_to_all(input_rows, "expert", split_axis=1, concat_axis=0, tiled=True),
    )
    back_out = back_out.reshape(arm_count * capacity, feature_width)[destination]
    back_out = back_out.reshape(token_count, 2, feature_width).astype(jnp.float32)
    back_input = back_input.reshape(arm_count * capacity, feature_width)[destination]
    back_input = back_input.reshape(token_count, 2, feature_width).astype(jnp.float32)
    head_output = (fact_share * back_out[:, 0] + counter_share * back_out[:, 1]).astype(
        jnp.bfloat16
    )
    grad_tokens = (back_input[:, 0] + back_input[:, 1]).astype(jnp.bfloat16)
    partial_gate = jnp.einsum(
        "arc,arh->ach", arm_tokens, d_gate, preferred_element_type=jnp.float32
    )
    partial_up = jnp.einsum("arc,arh->ach", arm_tokens, d_up, preferred_element_type=jnp.float32)
    partial_down = jnp.einsum("arh,arc->ahc", hidden, arm_cot, preferred_element_type=jnp.float32)
    summed_gate, summed_up, summed_down = (
        lax.psum_scatter(
            partial_gate.astype(jnp.bfloat16), "dp", scatter_dimension=2, tiled=True
        ).astype(jnp.float32),
        lax.psum_scatter(
            partial_up.astype(jnp.bfloat16), "dp", scatter_dimension=2, tiled=True
        ).astype(jnp.float32),
        lax.psum_scatter(
            partial_down.astype(jnp.bfloat16), "dp", scatter_dimension=1, tiled=True
        ).astype(jnp.float32),
    )
    grad_gate = summed_gate.astype(jnp.bfloat16)
    grad_up = summed_up.astype(jnp.bfloat16)
    grad_down = summed_down.astype(jnp.bfloat16)
    return (head_output, grad_tokens, grad_gate, grad_up, grad_down)


def solution(mesh):
    return jax.shard_map(
        on_device,
        mesh=mesh,
        in_specs=(
            P(("dp", "expert"), None),
            P(("dp", "expert"), None),
            P(("dp", "expert"), None),
            P("expert", None, None),
            P("expert", None, None),
            P("expert", None, None),
        ),
        out_specs=(
            P(("dp", "expert"), None),
            P(("dp", "expert"), None),
            P("expert", None, "dp"),
            P("expert", None, "dp"),
            P("expert", "dp", None),
        ),
        check_vma=False,
    )
```

profile of v0, /device:TPU:1, one launch (start us, length us, event | category | flops | bytes accessed | tf_op | source)
XLA Modules:
  0.0 177.4 jit_solution(6236930548241239089)
XLA Ops:
  7.2 0.9 copy.37
  8.2 0.1 eq.25
  8.3 0.7 broadcast_multiply_fusion
  9.1 0.2 fusion.25
  9.6 0.1 mul.73
  9.7 1.0 broadcast_in_dim.7
  10.9 0.2 fusion.29
  11.1 1.7 scatter_custom_fusion
  12.7 0.9 reshape.177
  13.7 18.4 %all-to-all-start = ((bf16[128,4,512]{2,1,0:T(4,128)(2,1)}), bf16[128,4,512]{2,1,0:T(4,128)(2,1)S(1)}, u32[]{:S(2)}, u32[]{:S(2)}) async-start(bf16[128,4,512]{2,1,0:T(4,128)(2,1)} %reshape.177), calls=%async_computation | async-start | bytes 1048576 | tf_op jit(solution)/shard_map/all_to_all | solution.py:51
  32.2 0.4 reshape.183
  32.8 1.7 scatter_custom_fusion.1
  34.5 0.9 reshape.184
  35.4 16.1 %all-to-all-done = bf16[128,4,512]{2,1,0:T(4,128)(2,1)S(1)} async-done(((bf16[128,4,512]{2,1,0:T(4,128)(2,1)}), bf16[128,4,512]{2,1,0:T(4,128)(2,1)S(1)}, u32[]{:S(2)}, u32[]{:S(2)}) %all-to-all-start) | async-done | bytes 524320 | tf_op jit(solution)/shard_map/all_to_all | solution.py:51
  51.5 7.2 %all-to-all-start.2 = ((bf16[128,4,512]{2,1,0:T(4,128)(2,1)}), bf16[128,4,512]{2,1,0:T(4,128)(2,1)S(1)}, u32[]{:S(2)}, u32[]{:S(2)}) async-start(bf16[128,4,512]{2,1,0:T(4,128)(2,1)} %reshape.184), calls=%async_computation.2 | async-start | bytes 1048576 | tf_op jit(solution)/shard_map/all_to_all | solution.py:52
  59.0 3.3 %fusion.11 = f32[512,1024]{1,0:T(8,128)} fusion(bf16[512,512]{1,0:T(8,128)(2,1)S(1)} %reshape.178, bf16[1,512,1024]{2,1,0:T(8,128)(2,1)} %param.11), kind=kOutput, calls=%fused_computation.24 | convolution fusion | flops 536870912 | bytes 3670016 | tf_op jit(solution)/shard_map/arc,ach->arh/dot_general | solution.py:17
  62.3 2.0 %fusion.15 = f32[512,1024]{1,0:T(8,128)} fusion(bf16[512,512]{1,0:T(8,128)(2,1)S(1)} %reshape.178, bf16[1,512,1024]{2,1,0:T(8,128)(2,1)S(1)} %copy-done.2), kind=kOutput, calls=%fused_computation.28 | convolution fusion | flops 536870912 | bytes 3670016 | tf_op jit(solution)/shard_map/arc,ach->arh/dot_general | solution.py:16
  64.4 14.0 %all-to-all-done.2 = bf16[128,4,512]{2,1,0:T(4,128)(2,1)S(1)} async-done(((bf16[128,4,512]{2,1,0:T(4,128)(2,1)}), bf16[128,4,512]{2,1,0:T(4,128)(2,1)S(1)}, u32[]{:S(2)}, u32[]{:S(2)}) %all-to-all-start.2) | async-done | bytes 524320 | tf_op jit(solution)/shard_map/all_to_all | solution.py:52
  78.5 4.9 %multiply_convert_fusion = (bf16[512,1024]{1,0:T(8,128)(2,1)}, bf16[512,1024]{1,0:T(8,128)(2,1)S(1)}, bf16[512,1024]{1,0:T(8,128)(2,1)}) fusion(f32[512,1024]{1,0:T(8,128)} %fusion.15, f32[512,1024]{1,0:T(8,128)} %fusion.11, bf16[512,512]{1,0:T(8,128)(2,1)S(1)} %reshape.185, bf16[1,1024,512]{2,1,0:T(8,128)(2,1)S(1)} %copy-done), kind=kOutput, calls=%fused_computation.4 | convolution fusion | flops 544735232 | bytes 8912896 | tf_op jit(solution)/shard_map/arc,ahc->arh/dot_general | solution.py:24
  83.4 1.7 fusion.1
  85.2 0.2 reduce-scatter.6.cloned.1.call-start
  85.4 3.0 %fusion.2 = bf16[1,512,1024]{2,1,0:T(8,128)(2,1)} fusion(bf16[512,512]{1,0:T(8,128)(2,1)S(1)} %reshape.178, bf16[512,1024]{1,0:T(8,128)(2,1)} %get-tuple-element.5), kind=kOutput, calls=%fused_computation.14 | convolution fusion | flops 537395200 | bytes 2621440 | tf_op jit(solution)/shard_map/arc,arh->ach/dot_general | solution.py:78
  88.5 2.1 %fusion.13 = f32[512,512]{1,0:T(8,128)S(1)} fusion(bf16[512,1024]{1,0:T(8,128)(2,1)} %copy-done.8, bf16[1,512,1024]{2,1,0:T(8,128)(2,1)S(1)} %copy-done.3), kind=kOutput, calls=%fused_computation.26 | convolution fusion | flops 536870912 | bytes 3145728 | tf_op jit(solution)/shard_map/arh,ach->arc/dot_general | solution.py:60
  90.6 0.7 fusion.6
  91.4 0.8 copy.79
  92.2 0.5 broadcast.77
  92.7 3.8 %reduce.1 = bf16[512,512]{1,0:T(8,128)(2,1)S(1)} reduce(bf16[512,1,512]{2,1,0:T(2,128)(2,1)S(1)} %bitcast.76, bf16[]{:T(256)} %broadcast.77), dimensions={1}, to_apply=%bitcast.67.reduce_sub_computation | reduce | bytes 1048578
  96.6 1.1 reshape.227
  97.7 7.1 %all-to-all-start.3 = ((bf16[128,2,1024]{2,1,0:T(2,128)(2,1)}), bf16[128,2,1024]{2,1,0:T(2,128)(2,1)S(1)}, u32[]{:S(2)}, u32[]{:S(2)}) async-start(bf16[128,2,1024]{2,1,0:T(2,128)(2,1)} %reshape.227), calls=%async_computation.3 | async-start | bytes 1048576 | tf_op jit(solution)/shard_map/all_to_all | solution.py:65
  104.8 0.3 reduce-scatter.8.cloned.1.call-start
  105.1 3.0 %fusion.3 = bf16[1,1024,512]{2,1,0:T(8,128)(2,1)} fusion(bf16[512,1024]{1,0:T(8,128)(2,1)} %get-tuple-element.7, bf16[512,512]{1,0:T(8,128)(2,1)S(1)} %reshape.185), kind=kOutput, calls=%fused_computation.15 | convolution fusion | flops 537395200 | bytes 2621440 | tf_op jit(solution)/shard_map/arh,arc->ahc/dot_general | solution.py:79
  108.1 0.7 fusion.5
  108.9 0.8 copy.80
  109.7 3.8 %reduce = bf16[512,512]{1,0:T(8,128)(2,1)S(1)} reduce(bf16[512,1,512]{2,1,0:T(2,128)(2,1)S(1)} %bitcast.77, bf16[]{:T(256)} %broadcast.77), dimensions={1}, to_apply=%bitcast.68.reduce_sub_computation | reduce | bytes 1048578
  113.5 1.1 reshape.225
  114.6 9.8 %all-to-all-done.3 = bf16[128,2,1024]{2,1,0:T(2,128)(2,1)S(1)} async-done(((bf16[128,2,1024]{2,1,0:T(2,128)(2,1)}), bf16[128,2,1024]{2,1,0:T(2,128)(2,1)S(1)}, u32[]{:S(2)}, u32[]{:S(2)}) %all-to-all-start.3) | async-done | bytes 524320 | tf_op jit(solution)/shard_map/all_to_all | solution.py:65
  124.4 7.1 %all-to-all-start.1 = ((bf16[128,2,1024]{2,1,0:T(2,128)(2,1)}), bf16[128,2,1024]{2,1,0:T(2,128)(2,1)S(1)}, u32[]{:S(2)}, u32[]{:S(2)}) async-start(bf16[128,2,1024]{2,1,0:T(2,128)(2,1)} %reshape.225), calls=%async_computation.1 | async-start | bytes 1048576 | tf_op jit(solution)/shard_map/all_to_all | solution.py:64
  131.5 0.5 reshape.228
  132.1 1.2 gather_fusion.1
  133.3 1.1 reshape.188
  134.4 16.7 %all-to-all-done.1 = bf16[128,2,1024]{2,1,0:T(2,128)(2,1)S(1)} async-done(((bf16[128,2,1024]{2,1,0:T(2,128)(2,1)}), bf16[128,2,1024]{2,1,0:T(2,128)(2,1)S(1)}, u32[]{:S(2)}, u32[]{:S(2)}) %all-to-all-start.1) | async-done | bytes 524320 | tf_op jit(solution)/shard_map/all_to_all | solution.py:64
  151.1 0.4 reshape.226
  151.7 1.2 gather_fusion
  152.8 0.3 reshape.187
  153.2 0.4 fusion.32
  153.6 0.4 fusion.33
  154.0 0.8 fusion.26
  154.8 16.1 %reduce-scatter.8.cloned.1.call-done = bf16[1,256,512]{2,1,0:T(8,128)(2,1)} async-done(((bf16[1,1024,512]{2,1,0:T(8,128)(2,1)}), bf16[1,256,512]{2,1,0:T(8,128)(2,1)}) %reduce-scatter.8.cloned.1.call-update) | async-done | bytes 262160 | tf_op jit(solution)/shard_map/reduce_scatter | solution.py:87
  (45 shorter events, 1.5 us)
Async XLA Ops:
  7.2 71.3 %copy-start = (bf16[1,1024,512]{2,1,0:T(8,128)(2,1)S(1)}, bf16[1,1024,512]{2,1,0:T(8,128)(2,1)}, u32[]{:S(2)}) copy-start(bf16[1,1024,512]{2,1,0:T(8,128)(2,1)} %param.12) | copy-start | bytes 3145732
  9.4 22.7 %copy-start.5 = (bf16[128,512]{1,0:T(8,128)(2,1)S(1)}, bf16[128,512]{1,0:T(8,128)(2,1)}, u32[]{:S(2)}) copy-start(bf16[128,512]{1,0:T(8,128)(2,1)} %param.9) | copy-start | bytes 393220
  11.1 21.6 %copy-start.6 = (f32[2]{0:T(128)S(1)}, f32[2]{0:T(128)}, u32[]{:S(2)}) copy-start(f32[2]{0:T(128)} %constant.21.clone) | copy-start | bytes 28
  13.7 37.9 %all-to-all-start = ((bf16[128,4,512]{2,1,0:T(4,128)(2,1)}), bf16[128,4,512]{2,1,0:T(4,128)(2,1)S(1)}, u32[]{:S(2)}, u32[]{:S(2)}) async-start(bf16[128,4,512]{2,1,0:T(4,128)(2,1)} %reshape.177), calls=%async_computation | async-start | bytes 1048576 | tf_op jit(solution)/shard_map/all_to_all | solution.py:51
  51.5 26.8 %all-to-all-start.2 = ((bf16[128,4,512]{2,1,0:T(4,128)(2,1)}), bf16[128,4,512]{2,1,0:T(4,128)(2,1)S(1)}, u32[]{:S(2)}, u32[]{:S(2)}) async-start(bf16[128,4,512]{2,1,0:T(4,128)(2,1)} %reshape.184), calls=%async_computation.2 | async-start | bytes 1048576 | tf_op jit(solution)/shard_map/all_to_all | solution.py:52
  58.8 96.0 %reduce-scatter.4.cloned.1.call-start = ((), (), s32[]{:S(2)}) async-start(), calls=%async_computation.7 | async-start | bytes 1310720 | tf_op jit(solution)/shard_map/reduce_scatter | solution.py:81
  59.0 3.4 %copy-start.2 = (bf16[1,512,1024]{2,1,0:T(8,128)(2,1)S(1)}, bf16[1,512,1024]{2,1,0:T(8,128)(2,1)}, u32[]{:S(2)}) copy-start(bf16[1,512,1024]{2,1,0:T(8,128)(2,1)} %param.10) | copy-start | bytes 3145732
  83.4 1.7 copy-start.8
  85.2 3.3 %copy-start.3 = (bf16[1,512,1024]{2,1,0:T(8,128)(2,1)S(1)}, bf16[1,512,1024]{2,1,0:T(8,128)(2,1)}, u32[]{:S(2)}) copy-start(bf16[1,512,1024]{2,1,0:T(8,128)(2,1)} %param.10) | copy-start | bytes 3145732
  85.2 69.6 %reduce-scatter.6.cloned.1.call-start = ((), (), s32[]{:S(2)}) async-start(), calls=%async_computation.8 | async-start | bytes 1310720 | tf_op jit(solution)/shard_map/reduce_scatter | solution.py:84
  88.5 2.1 %copy-start.4 = (bf16[1,512,1024]{2,1,0:T(8,128)(2,1)S(1)}, bf16[1,512,1024]{2,1,0:T(8,128)(2,1)}, u32[]{:S(2)}) copy-start(bf16[1,512,1024]{2,1,0:T(8,128)(2,1)} %param.11) | copy-start | bytes 3145732
  88.5 2.1 %copy-start.7 = (bf16[512,1024]{1,0:T(8,128)(2,1)S(1)}, bf16[512,1024]{1,0:T(8,128)(2,1)}, u32[]{:S(2)}) copy-start(bf16[512,1024]{1,0:T(8,128)(2,1)} %get-tuple-element.5) | copy-start | bytes 3145732
  97.7 26.7 %all-to-all-start.3 = ((bf16[128,2,1024]{2,1,0:T(2,128)(2,1)}), bf16[128,2,1024]{2,1,0:T(2,128)(2,1)S(1)}, u32[]{:S(2)}, u32[]{:S(2)}) async-start(bf16[128,2,1024]{2,1,0:T(2,128)(2,1)} %reshape.227), calls=%async_computation.3 | async-start | bytes 1048576 | tf_op jit(solution)/shard_map/all_to_all | solution.py:65
  104.8 3.3 %copy-start.9 = (bf16[512,1024]{1,0:T(8,128)(2,1)S(1)}, bf16[512,1024]{1,0:T(8,128)(2,1)}, u32[]{:S(2)}) copy-start(bf16[512,1024]{1,0:T(8,128)(2,1)} %get-tuple-element.7) | copy-start | bytes 3145732
  104.8 66.0 %reduce-scatter.8.cloned.1.call-start = ((), (), s32[]{:S(2)}) async-start(), calls=%async_computation.9 | async-start | bytes 1310720 | tf_op jit(solution)/shard_map/reduce_scatter | solution.py:87
  124.4 26.7 %all-to-all-start.1 = ((bf16[128,2,1024]{2,1,0:T(2,128)(2,1)}), bf16[128,2,1024]{2,1,0:T(2,128)(2,1)S(1)}, u32[]{:S(2)}, u32[]{:S(2)}) async-start(bf16[128,2,1024]{2,1,0:T(2,128)(2,1)} %reshape.225), calls=%async_computation.1 | async-start | bytes 1048576 | tf_op jit(solution)/shard_map/all_to_all | solution.py:64
  151.5 1.6 copy-start.1
Sparse Core Ops, SparseCore 0:
  85.3 20.6 reduce-scatter.3
  109.6 29.1 reduce-scatter.5
  142.2 28.5 reduce-scatter.7
where the time goes:
time: 178 us; the launch traced here: 177 us
  waiting for transfers between devices  72.7 us (41%)
  starting transfers between devices  40.4 us (23%)
  matrix products  21.6 us (12%)
  local copies, waits for them, and re-layouts  17.2 us (10%)
  between operations  14.1 us (8%)
  other arithmetic  11.3 us (6%)
    all_to_all x1, starting transfers between devices, on_device(): lax.all_to_all(send_tokens, 'expert', split_axis=0, concat_axis=1, tiled=...  18.4 us
    all_to_all x1, waiting for transfers between devices, on_device(): lax.all_to_all(out_rows, 'expert', split_axis=1, concat_axis=0, tiled=True)  16.7 us
    all_to_all x1, waiting for transfers between devices, on_device(): lax.all_to_all(send_tokens, 'expert', split_axis=0, concat_axis=1, tiled=...  16.1 us
    reduce_scatter x1, waiting for transfers between devices, on_device(): lax.psum_scatter(partial_down.astype(jnp.bfloat16), 'dp', scatter_dimensi...  16.1 us
    all_to_all x1, waiting for transfers between devices, on_device(): lax.all_to_all(send_cot, 'expert', split_axis=0, concat_axis=1, tiled=True)  14 us
    all_to_all x1, waiting for transfers between devices, on_device(): lax.all_to_all(input_rows, 'expert', split_axis=1, concat_axis=0, tiled=T...  9.75 us
    unnamed x2, other arithmetic  7.65 us
    all_to_all x1, starting transfers between devices, on_device(): lax.all_to_all(send_cot, 'expert', split_axis=0, concat_axis=1, tiled=True)  7.23 us
  transfers between devices with their start and end apart: 7, of which 5 were waited for; matrix products, arithmetic and copies ran while one was open for 21% of the time, Pallas kernels for 0%

commit v1 on v0

v1 whole, which is shorter than its diff:
```python
import functools

import jax
import jax.numpy as jnp
from jax import lax
from jax.experimental import pallas as pl
from jax.experimental.pallas import tpu as pltpu
from jax.sharding import PartitionSpec as P

fact_share = 0.7
counter_share = 0.3
MESH_ID = pl.DeviceIdType.MESH


def silu_parts(gate_pre):
    sigmoid_gate = jax.nn.sigmoid(gate_pre)
    return (gate_pre * sigmoid_gate, sigmoid_gate * (1.0 + gate_pre * (1.0 - sigmoid_gate)))


def exchange_kernel(n, send_hbm, recv_hbm, send_sem, recv_sem, local_sem):
    me = lax.axis_index("expert")
    row = lax.axis_index("dp")

    def copy_to(i):
        j = lax.rem(me + i, n)
        return pltpu.make_async_remote_copy(
            src_ref=send_hbm.at[j],
            dst_ref=recv_hbm.at[me],
            send_sem=send_sem.at[j],
            recv_sem=recv_sem.at[me],
            device_id=(row, j),
            device_id_type=MESH_ID,
        )

    def start(i, carry):
        copy_to(i).start()
        return carry

    lax.fori_loop(1, n, start, 0)
    local = pltpu.make_async_copy(send_hbm.at[me], recv_hbm.at[me], local_sem)
    local.start()
    local.wait()

    def finish(i, carry):
        j = lax.rem(me + i, n)
        copy_to(i).wait_send()
        pltpu.make_async_remote_copy(
            src_ref=send_hbm.at[j],
            dst_ref=recv_hbm.at[j],
            send_sem=send_sem.at[j],
            recv_sem=recv_sem.at[j],
            device_id=(row, j),
            device_id_type=MESH_ID,
        ).wait_recv()
        return carry

    lax.fori_loop(1, n, finish, 0)


def exchange(send):
    n = send.shape[0]
    nbytes = send.size * send.dtype.itemsize
    return pl.pallas_call(
        functools.partial(exchange_kernel, n),
        out_shape=jax.ShapeDtypeStruct(send.shape, send.dtype),
        in_specs=[pl.BlockSpec(memory_space=pl.ANY)],
        out_specs=pl.BlockSpec(memory_space=pl.ANY),
        scratch_shapes=[
            pltpu.SemaphoreType.DMA((n,)),
            pltpu.SemaphoreType.DMA((n,)),
            pltpu.SemaphoreType.DMA,
        ],
        compiler_params=pltpu.CompilerParams(has_side_effects=True),
        cost_estimate=pl.CostEstimate(flops=0, bytes_accessed=2 * nbytes, transcendentals=0),
    )(send)


def on_device(tokens, codes, cotangent, w_gate, w_up, w_down):
    token_count, feature_width = tokens.shape
    local_arms = w_gate.shape[0]
    arm_count = local_arms * lax.axis_size("expert")
    capacity = 4 * token_count // arm_count
    flat_codes = codes.reshape(-1)
    arm_ids = jnp.arange(arm_count, dtype=jnp.int32)
    onehot = (flat_codes[:, None] == arm_ids[None, :]).astype(jnp.int32)
    earlier = jnp.cumsum(onehot, axis=0) - onehot
    slot = jnp.sum(earlier * onehot, axis=1)
    tok_dest = flat_codes * (2 * capacity) + slot
    cot_dest = tok_dest + capacity
    shares = jnp.tile(jnp.array([fact_share, counter_share], jnp.float32), token_count)
    token_rows = jnp.repeat(tokens, 2, axis=0)
    cot_rows = (jnp.repeat(cotangent.astype(jnp.float32), 2, axis=0) * shares[:, None]).astype(
        jnp.bfloat16
    )
    send = (
        jnp.zeros((arm_count * 2 * capacity, feature_width), jnp.bfloat16)
        .at[jnp.concatenate([tok_dest, cot_dest])]
        .set(jnp.concatenate([token_rows, cot_rows]))
        .reshape(arm_count, 2 * capacity, feature_width)
    )
    got = exchange(send)
    arm_tokens = got[:, :capacity].reshape(1, -1, feature_width)
    arm_cot = got[:, capacity:].reshape(1, -1, feature_width)

    gate_pre = jnp.einsum("arc,ach->arh", arm_tokens, w_gate, preferred_element_type=jnp.float32)
    up_pre = jnp.einsum("arc,ach->arh", arm_tokens, w_up, preferred_element_type=jnp.float32)
    activated, silu_slope = silu_parts(gate_pre)
    hidden = (activated * up_pre).astype(jnp.bfloat16)
    out_rows = jnp.einsum(
        "arh,ahc->arc", hidden, w_down, preferred_element_type=jnp.float32
    ).astype(jnp.bfloat16)
    d_hidden = jnp.einsum("arc,ahc->arh", arm_cot, w_down, preferred_element_type=jnp.float32)
    d_up = (d_hidden * activated).astype(jnp.bfloat16)
    d_gate = (d_hidden * up_pre * silu_slope).astype(jnp.bfloat16)
    input_rows = (
        jnp.einsum("arh,ach->arc", d_gate, w_gate, preferred_element_type=jnp.float32)
        + jnp.einsum("arh,ach->arc", d_up, w_up, preferred_element_type=jnp.float32)
    ).astype(jnp.bfloat16)

    ret = jnp.concatenate(
        [
            out_rows.reshape(-1, capacity, feature_width),
            input_rows.reshape(-1, capacity, feature_width),
        ],
        axis=1,
    )
    back = exchange(ret).reshape(arm_count * 2 * capacity, feature_width)
    back_out = back[tok_dest].reshape(token_count, 2, feature_width).astype(jnp.float32)
    back_input = back[cot_dest].reshape(token_count, 2, feature_width).astype(jnp.float32)
    head_output = (fact_share * back_out[:, 0] + counter_share * back_out[:, 1]).astype(
        jnp.bfloat16
    )
    grad_tokens = (back_input[:, 0] + back_input[:, 1]).astype(jnp.bfloat16)

    partial_gate = jnp.einsum(
        "arc,arh->ach", arm_tokens, d_gate, preferred_element_type=jnp.float32
    )
    partial_up = jnp.einsum("arc,arh->ach", arm_tokens, d_up, preferred_element_type=jnp.float32)
    partial_down = jnp.einsum("arh,arc->ahc", hidden, arm_cot, preferred_element_type=jnp.float32)
    summed_gate, summed_up, summed_down = (
        lax.psum_scatter(
            partial_gate.astype(jnp.bfloat16), "dp", scatter_dimension=2, tiled=True
        ).astype(jnp.float32),
        lax.psum_scatter(
            partial_up.astype(jnp.bfloat16), "dp", scatter_dimension=2, tiled=True
        ).astype(jnp.float32),
        lax.psum_scatter(
            partial_down.astype(jnp.bfloat16), "dp", scatter_dimension=1, tiled=True
        ).astype(jnp.float32),
    )
    grad_gate = summed_gate.astype(jnp.bfloat16)
    grad_up = summed_up.astype(jnp.bfloat16)
    grad_down = summed_down.astype(jnp.bfloat16)
    return (head_output, grad_tokens, grad_gate, grad_up, grad_down)


def solution(mesh):
    return jax.shard_map(
        on_device,
        mesh=mesh,
        in_specs=(
            P(("dp", "expert"), None),
            P(("dp", "expert"), None),
            P(("dp", "expert"), None),
            P("expert", None, None),
            P("expert", None, None),
            P("expert", None, None),
        ),
        out_specs=(
            P(("dp", "expert"), None),
            P(("dp", "expert"), None),
            P("expert", None, "dp"),
            P("expert", None, "dp"),
            P("expert", "dp", None),
        ),
        check_vma=False,
    )
```

time: 178 us -> 179 us (level)
  Pallas kernels: 0 us -> 105 us
  waiting for transfers between devices: 72.7 us -> 22.2 us
  starting transfers between devices: 40.4 us -> 0.3 us
  matrix products: 21.6 us -> 16.4 us
  other arithmetic: 11.3 us -> 6.33 us
  local copies, waits for them, and re-layouts: 17.2 us -> 12.5 us
    pallas_call x0 -> x2, Pallas kernels: none -> 105 us  [exchange(): pl.pallas_call(functools.partial(exchange_kernel, n), out_shape=jax.Shape...]
    all_to_all x4 -> x0, waiting for transfers between devices: 56.5 us -> none  [the longest x1 16.7 us: on_device(): lax.all_to_all(out_rows, 'expert', split_axis=1, concat_axis=0, tiled=True)]
    all_to_all x4 -> x0, starting transfers between devices: 39.9 us -> none  [the longest x1 18.4 us: on_device(): lax.all_to_all(send_tokens, 'expert', split_axis=0, concat_axis=1, tiled=...]
    unnamed x2 -> x0, other arithmetic: 7.65 us -> none
    reduce_scatter x1, waiting for transfers between devices: 16.1 us -> 22.1 us  [on_device(): lax.psum_scatter(partial_down.astype(jnp.bfloat16), 'dp', scatter_dimensi...]
    dot_general x3, matrix products: 10.3 us -> 5.2 us  [the longest x1 2.42 us: on_device(): jnp.einsum('arc,ach->arh', arm_tokens, w_up, preferred_element_type=jnp.f...]
    unnamed x29 -> x24, local copies, waits for them, and re-layouts: 4.83 us -> 2.23 us
    convert_element_type x4 -> x2, local copies, waits for them, and re-layouts: 3.09 us -> 0.68 us  [the longest x1 0.34 us: on_device(): back[tok_dest].reshape(token_count, 2, feature_width).astype(jnp.float32)]
  transfers between devices with their start and end apart: 7 -> 3, of which waited for: 5 -> 1; matrix products, arithmetic and copies ran while one was open for 21% -> 10% of each run, Pallas kernels for 0% -> 28%
where the time goes in v1:
time: 179 us; the launch traced here: 177 us
  Pallas kernels  105 us (59%)
  waiting for transfers between devices  22.2 us (12%)
  matrix products  16.4 us (9%)
  between operations  14.1 us (8%)
  local copies, waits for them, and re-layouts  12.5 us (7%)
  other arithmetic  6.33 us (4%)
    pallas_call x2, Pallas kernels, exchange(): pl.pallas_call(functools.partial(exchange_kernel, n), out_shape=jax.Shape...  105 us
    reduce_scatter x1, waiting for transfers between devices, on_device(): lax.psum_scatter(partial_down.astype(jnp.bfloat16), 'dp', scatter_dimensi...  22.1 us
  transfers between devices with their start and end apart: 3, of which 1 were waited for; matrix products, arithmetic and copies ran while one was open for 10% of the time, Pallas kernels for 28%

profile of v1, /device:TPU:1, one launch (start us, length us, event | category | flops | bytes accessed | tf_op | source)
XLA Modules:
  0.0 177.1 jit_solution(8280556324036916450)
XLA Ops:
  7.2 0.0 reduce-scatter.4.cloned.1.call-start
  7.2 0.9 copy.16
  8.1 0.1 eq.26
  8.3 0.1 reshape.264
  8.4 0.1 copy.18
  8.5 0.2 fusion.23
  8.8 0.2 fusion.27
  9.0 1.0 broadcast_in_dim.15
  10.1 0.4 reshape.267
  10.5 0.1 mul.106
  10.6 0.1 broadcast_in_dim.14
  10.7 0.1 reshape.266
  10.9 0.1 multiply_convert_fusion.3
  11.0 3.5 %scatter_custom_fusion = bf16[1024,512]{1,0:T(8,128)(2,1)} fusion(s32[512]{0:T(512)S(1)} %bitcast.71, bf16[256,512]{1,0:T(8,128)(2,1)S(1)} %multiply_convert_fusion.3, bf16[]{:T(256)} %constant.34, bf16[256,512]{1,0:T(8,128)(2,1)S(1)} %reshape.266, bf16[]{:T(256)} %constant.10.clone.1), kind=kCustom, calls=%fused_computation.28 | custom fusion | flops 1048576 | bytes 1572868 | tf_op jit(solution)/shard_map/scatter | solution.py:98
  14.4 56.2 %shard_map.110 = bf16[128,8,512]{2,1,0:T(8,128)(2,1)} custom-call(bf16[128,8,512]{2,1,0:T(8,128)(2,1)} %bitcast.62), custom_call_target="tpu_custom_call" | custom-call | bytes 2097152 | tf_op jit(solution)/shard_map/pallas_call | solution.py:63
  70.7 2.0 %fusion.30 = (bf16[128,4,512]{2,1,0:T(4,128)(2,1)S(1)}, bf16[128,4,512]{2,1,0:T(4,128)(2,1)S(1)}) fusion(bf16[128,8,512]{2,1,0:T(8,128)(2,1)} %shard_map.110), kind=kLoop, calls=%fused_computation.60 | loop fusion | bytes 2097152 | tf_op jit(solution)/shard_map/slice | solution.py:103
  72.7 0.1 reshape.269
  72.9 0.1 reshape.274
  73.0 2.0 %fusion.13 = f32[512,1024]{1,0:T(8,128)S(1)} fusion(bf16[512,512]{1,0:T(8,128)(2,1)S(1)} %reshape.269, bf16[1,512,1024]{2,1,0:T(8,128)(2,1)} %param.10), kind=kOutput, calls=%fused_computation.26 | convolution fusion | flops 536870912 | bytes 3670016 | tf_op jit(solution)/shard_map/arc,ach->arh/dot_general | solution.py:105
  75.1 0.7 fusion.5
  75.8 2.4 %multiply_convert_fusion.2 = (bf16[512,1024]{1,0:T(8,128)(2,1)}, bf16[512,1024]{1,0:T(8,128)(2,1)S(1)}, bf16[512,1024]{1,0:T(8,128)(2,1)S(1)}) fusion(f32[512,1024]{1,0:T(8,128)S(1)} %fusion.13, f32[512,1024]{1,0:T(8,128)S(1)} %fusion.5, bf16[512,512]{1,0:T(8,128)(2,1)S(1)} %reshape.269, bf16[1,512,1024]{2,1,0:T(8,128)(2,1)S(1)} %copy-done), kind=kOutput, calls=%fused_computation.5 | convolution fusion | flops 544735232 | bytes 8912896 | tf_op jit(solution)/shard_map/arc,ach->arh/dot_general | solution.py:106
  78.2 1.0 copy-done.10
  79.2 1.7 fusion.1
  80.9 0.0 reduce-scatter.4.cloned.1.call-update
  80.9 0.0 reduce-scatter.6.cloned.1.call-start
  81.0 1.8 fusion.2
  82.7 0.0 reduce-scatter.6.cloned.1.call-update
  82.8 0.2 reduce-scatter.8.cloned.1.call-start
  83.0 3.0 %fusion.3 = bf16[1,1024,512]{2,1,0:T(8,128)(2,1)} fusion(bf16[512,1024]{1,0:T(8,128)(2,1)} %get-tuple-element.7, bf16[512,512]{1,0:T(8,128)(2,1)S(1)} %reshape.274), kind=kOutput, calls=%fused_computation.14 | convolution fusion | flops 537395200 | bytes 2621440 | tf_op jit(solution)/shard_map/arh,arc->ahc/dot_general | solution.py:139
  86.0 0.0 reduce-scatter.8.cloned.1.call-update
  86.1 2.1 %fusion.11 = f32[512,512]{1,0:T(8,128)S(1)} fusion(bf16[512,1024]{1,0:T(8,128)(2,1)} %copy-done.10, bf16[1,512,1024]{2,1,0:T(8,128)(2,1)S(1)} %copy-done.2), kind=kOutput, calls=%fused_computation.24 | convolution fusion | flops 536870912 | bytes 3145728 | tf_op jit(solution)/shard_map/arh,ach->arc/dot_general | solution.py:116
  88.2 0.7 fusion.4
  88.9 0.1 reshape.275
  89.1 0.3 copy-done.4
  89.4 1.9 %convolution_convert_fusion.3 = bf16[512,512]{1,0:T(8,128)(2,1)S(1)} fusion(bf16[512,1024]{1,0:T(8,128)(2,1)} %get-tuple-element.7, bf16[1,1024,512]{2,1,0:T(8,128)(2,1)S(1)} %copy-done.4), kind=kOutput, calls=%fused_computation.16 | convolution fusion | flops 537133056 | bytes 2621440 | tf_op jit(solution)/shard_map/arh,ahc->arc/dot_general | solution.py:109
  91.3 0.1 reshape.273
  91.5 1.5 pad_maximum_fusion.send_hbm
  93.0 49.0 %shard_map.111 = bf16[128,8,512]{2,1,0:T(8,128)(2,1)} custom-call(bf16[128,8,512]{2,1,0:T(8,128)(2,1)} %pad_maximum_fusion.send_hbm), custom_call_target="tpu_custom_call" | custom-call | bytes 2097152 | tf_op jit(solution)/shard_map/pallas_call | solution.py:63
  142.1 0.1 copy.20
  142.2 0.1 mul.118
  142.4 2.6 %gather_fusion.1 = bf16[256,512]{1,0:T(8,128)(2,1)S(1)} fusion(bf16[1024,512]{1,0:T(8,128)(2,1)} %bitcast.60, s32[1024]{0:T(1024)S(1)} %pad_clamp_fusion), kind=kCustom, calls=%fused_computation.1 | custom fusion | bytes 525312 | tf_op jit(solution)/shard_map/gather | solution.py:129
  145.0 0.3 reshape.278
  145.3 1.2 gather_fusion
  146.5 0.3 reshape.277
  146.8 0.4 fusion.31
  147.2 0.4 fusion.32
  147.6 0.8 fusion.24
  148.4 22.1 %reduce-scatter.8.cloned.1.call-done = bf16[1,256,512]{2,1,0:T(8,128)(2,1)} async-done(((bf16[1,1024,512]{2,1,0:T(8,128)(2,1)}), bf16[1,256,512]{2,1,0:T(8,128)(2,1)}) %reduce-scatter.8.cloned.1.call-update) | async-done | bytes 262160 | tf_op jit(solution)/shard_map/reduce_scatter | solution.py:147
  (35 shorter events, 0.2 us)
Async XLA Ops:
  7.2 68.6 %copy-start = (bf16[1,512,1024]{2,1,0:T(8,128)(2,1)S(1)}, bf16[1,512,1024]{2,1,0:T(8,128)(2,1)}, u32[]{:S(2)}) copy-start(bf16[1,512,1024]{2,1,0:T(8,128)(2,1)} %param.11) | copy-start | bytes 3145732
  7.2 3.3 %copy-start.7 = (f32[2]{0:T(128)S(1)}, f32[2]{0:T(128)}, u32[]{:S(2)}) copy-start(f32[2]{0:T(128)} %constant.27.clone) | copy-start | bytes 28
  7.2 3.4 %copy-start.5 = (bf16[128,512]{1,0:T(8,128)(2,1)S(1)}, bf16[128,512]{1,0:T(8,128)(2,1)}, u32[]{:S(2)}) copy-start(bf16[128,512]{1,0:T(8,128)(2,1)} %param.7) | copy-start | bytes 393220
  7.2 141.2 %reduce-scatter.4.cloned.1.call-start = ((), (), s32[]{:S(2)}) async-start(), calls=%async_computation.3 | async-start | bytes 1310720 | tf_op jit(solution)/shard_map/reduce_scatter | solution.py:141
  73.0 2.1 %copy-start.3 = (bf16[1,1024,512]{2,1,0:T(8,128)(2,1)S(1)}, bf16[1,1024,512]{2,1,0:T(8,128)(2,1)}, u32[]{:S(2)}) copy-start(bf16[1,1024,512]{2,1,0:T(8,128)(2,1)} %param.12) | copy-start | bytes 3145732
  78.2 1.0 copy-start.10
  78.2 4.5 %copy-start.8 = (bf16[512,1024]{1,0:T(8,128)(2,1)}, bf16[512,1024]{1,0:T(8,128)(2,1)S(1)}, u32[]{:S(2)}) copy-start(bf16[512,1024]{1,0:T(8,128)(2,1)S(1)} %get-tuple-element.9) | copy-start | bytes 3145732
  80.9 67.5 %reduce-scatter.6.cloned.1.call-start = ((), (), s32[]{:S(2)}) async-start(), calls=%async_computation.4 | async-start | bytes 1310720 | tf_op jit(solution)/shard_map/reduce_scatter | solution.py:144
  82.8 3.3 %copy-start.2 = (bf16[1,512,1024]{2,1,0:T(8,128)(2,1)S(1)}, bf16[1,512,1024]{2,1,0:T(8,128)(2,1)}, u32[]{:S(2)}) copy-start(bf16[1,512,1024]{2,1,0:T(8,128)(2,1)} %param.10) | copy-start | bytes 3145732
  82.8 87.8 %reduce-scatter.8.cloned.1.call-start = ((), (), s32[]{:S(2)}) async-start(), calls=%async_computation.5 | async-start | bytes 1310720 | tf_op jit(solution)/shard_map/reduce_scatter | solution.py:147
  86.1 2.1 %copy-start.9 = (bf16[512,1024]{1,0:T(8,128)(2,1)S(1)}, bf16[512,1024]{1,0:T(8,128)(2,1)}, u32[]{:S(2)}) copy-start(bf16[512,1024]{1,0:T(8,128)(2,1)} %copy-done.8) | copy-start | bytes 3145732
  88.2 1.2 copy-start.4
  91.5 50.6 %copy-start.6 = (s32[128,2]{0,1:T(2,128)S(1)}, s32[128,2]{0,1:T(2,128)}, u32[]{:S(2)}) copy-start(s32[128,2]{0,1:T(2,128)} %param.8) | copy-start | bytes 3076
  142.0 3.3 %copy-start.1 = (bf16[128,8,512]{2,1,0:T(8,128)(2,1)S(1)}, bf16[128,8,512]{2,1,0:T(8,128)(2,1)}, u32[]{:S(2)}) copy-start(bf16[128,8,512]{2,1,0:T(8,128)(2,1)} %shard_map.111) | copy-start | bytes 3145732
Sparse Core Ops, SparseCore 0:
  81.0 25.0 reduce-scatter.3
  109.8 29.3 reduce-scatter.5
  142.6 27.8 reduce-scatter.7

commit v2 on v1

--- a/solution.py
+++ b/solution.py
@@ -98,7 +98,7 @@
         .set(jnp.concatenate([token_rows, cot_rows]))
         .reshape(arm_count, 2 * capacity, feature_width)
     )
-    got = exchange(send)
+    got = lax.all_to_all(send, "expert", 0, 0, tiled=True)
     arm_tokens = got[:, :capacity].reshape(1, -1, feature_width)
     arm_cot = got[:, capacity:].reshape(1, -1, feature_width)
 
@@ -124,7 +124,7 @@
         ],
         axis=1,
     )
-    back = exchange(ret).reshape(arm_count * 2 * capacity, feature_width)
+    back = lax.all_to_all(ret, "expert", 0, 0, tiled=True).reshape(arm_count * 2 * capacity, feature_width)
     back_out = back[tok_dest].reshape(token_count, 2, feature_width).astype(jnp.float32)
     back_input = back[cot_dest].reshape(token_count, 2, feature_width).astype(jnp.float32)
     head_output = (fact_share * back_out[:, 0] + counter_share * back_out[:, 1]).astype(
@@ -132,25 +132,18 @@
     )
     grad_tokens = (back_input[:, 0] + back_input[:, 1]).astype(jnp.bfloat16)
 
-    partial_gate = jnp.einsum(
-        "arc,arh->ach", arm_tokens, d_gate, preferred_element_type=jnp.float32
-    )
-    partial_up = jnp.einsum("arc,arh->ach", arm_tokens, d_up, preferred_element_type=jnp.float32)
-    partial_down = jnp.einsum("arh,arc->ahc", hidden, arm_cot, preferred_element_type=jnp.float32)
-    summed_gate, summed_up, summed_down = (
-        lax.psum_scatter(
-            partial_gate.astype(jnp.bfloat16), "dp", scatter_dimension=2, tiled=True
-        ).astype(jnp.float32),
-        lax.psum_scatter(
-            partial_up.astype(jnp.bfloat16), "dp", scatter_dimension=2, tiled=True
-        ).astype(jnp.float32),
-        lax.psum_scatter(
-            partial_down.astype(jnp.bfloat16), "dp", scatter_dimension=1, tiled=True
-        ).astype(jnp.float32),
-    )
-    grad_gate = summed_gate.astype(jnp.bfloat16)
-    grad_up = summed_up.astype(jnp.bfloat16)
-    grad_down = summed_down.astype(jnp.bfloat16)
+    partials = jnp.stack(
+        [
+            jnp.einsum("arh,arc->hc", d_gate, arm_tokens, preferred_element_type=jnp.float32),
+            jnp.einsum("arh,arc->hc", d_up, arm_tokens, preferred_element_type=jnp.float32),
+            jnp.einsum("arh,arc->hc", hidden, arm_cot, preferred_element_type=jnp.float32),
+        ],
+        axis=1,
+    ).astype(jnp.bfloat16)
+    summed = lax.psum_scatter(partials, "dp", scatter_dimension=0, tiled=True)
+    grad_gate = summed[:, 0, :].T[None]
+    grad_up = summed[:, 1, :].T[None]
+    grad_down = summed[:, 2, :][None]
     return (head_output, grad_tokens, grad_gate, grad_up, grad_down)
 
 

time: 179 us -> 132 us (0.74); the launches traced: 177 us -> 132 us
  Pallas kernels: 105 us -> 0 us
  blocking collectives: 0 us -> 48.7 us
  waiting for transfers between devices: 22.2 us -> 30.1 us
  starting transfers between devices: 0.3 us -> 6.97 us
  matrix products: 16.4 us -> 11.2 us
    pallas_call x2 -> x0, Pallas kernels: 105 us -> none  [exchange(): pl.pallas_call(functools.partial(exchange_kernel, n), out_shape=jax.Shape...]
    all_to_all x0 -> x1, blocking collectives: none -> 48.7 us  [on_device(): got = lax.all_to_all(send, 'expert', 0, 0, tiled=True)]
    all_to_all x0 -> x1, waiting for transfers between devices: none -> 30.1 us  [on_device(): lax.all_to_all(ret, 'expert', 0, 0, tiled=True)]
    reduce_scatter x3 -> x1, waiting for transfers between devices: 22.1 us -> 0.01 us  [on_device(): summed = lax.psum_scatter(partials, 'dp', scatter_dimension=0, tiled=True)]
    all_to_all x0 -> x1, starting transfers between devices: none -> 6.94 us  [on_device(): lax.all_to_all(ret, 'expert', 0, 0, tiled=True)]
    dot_general x3, matrix products: 6.49 us -> 2.26 us  [the longest x1 0.76 us: on_device(): jnp.einsum('arh,arc->hc', hidden, arm_cot, preferred_element_type=jnp.flo...]
    another operation x3 -> x4, other arithmetic: 0.26 us -> 2.23 us  [the longest x1 1.98 us: on_device(): jnp.stack([jnp.einsum('arh,arc->hc', d_gate, arm_tokens, preferred_elemen...]
    another operation x5 -> x6, local copies, waits for them, and re-layouts: 0.27 us -> 2.13 us  [the longest x1 1.86 us: on_device(): grad_down = summed[:, 2, :][None]]
  transfers between devices with their start and end apart: 3 -> 2, of which waited for: 1 -> 1; matrix products, arithmetic and copies ran while one was open for 10% -> 9% of each run, Pallas kernels for 28% -> 0%
where the time goes in v2:
time: 132 us
  blocking collectives  48.7 us (37%)
  waiting for transfers between devices  30.1 us (23%)
  between operations  14.4 us (11%)
  local copies, waits for them, and re-layouts  13 us (10%)
  matrix products  11.2 us (8%)
  other arithmetic  7.63 us (6%)
  starting transfers between devices  6.97 us (5%)
    all_to_all x1, blocking collectives, on_device(): got = lax.all_to_all(send, 'expert', 0, 0, tiled=True)  48.7 us
    all_to_all x1, waiting for transfers between devices, on_device(): lax.all_to_all(ret, 'expert', 0, 0, tiled=True)  30.1 us
    all_to_all x1, starting transfers between devices, on_device(): lax.all_to_all(ret, 'expert', 0, 0, tiled=True)  6.94 us
    unnamed x24, local copies, waits for them, and re-layouts  4 us
    scatter x1, other arithmetic, on_device(): send = jnp.zeros((arm_count * 2 * capacity, feature_width), jnp.bfloat16)...  2.74 us
  transfers between devices with their start and end apart: 2, of which 1 were waited for; matrix products, arithmetic and copies ran while one was open for 9% of the time, Pallas kernels for 0%

profile of v2, /device:TPU:1, one launch (start us, length us, event | category | flops | bytes accessed | tf_op | source)
XLA Modules:
  0.0 132.0 jit_solution(5081128406059705690)
XLA Ops:
  7.2 0.0 reduce-scatter.2.cloned.1.call-start
  7.2 0.9 copy.18
  8.1 0.1 eq.26
  8.3 0.1 reshape.258
  8.4 0.1 copy.20
  8.5 0.2 fusion.23
  8.8 0.2 fusion.27
  9.0 1.0 broadcast_in_dim.21
  10.1 0.4 reshape.261
  10.5 0.1 mul.106
  10.6 0.1 broadcast_in_dim.20
  10.7 0.1 reshape.260
  10.9 0.1 multiply_convert_fusion.3
  11.0 2.7 %scatter_custom_fusion = bf16[1024,512]{1,0:T(8,128)(2,1)S(1)} fusion(s32[512]{0:T(512)S(1)} %bitcast.85, bf16[256,512]{1,0:T(8,128)(2,1)S(1)} %multiply_convert_fusion.3, bf16[]{:T(256)} %constant.34, bf16[256,512]{1,0:T(8,128)(2,1)S(1)} %reshape.260, bf16[]{:T(256)} %constant.10.clone.1), kind=kCustom, calls=%fused_computation.29 | custom fusion | flops 1048576 | bytes 1572868 | tf_op jit(solution)/shard_map/scatter | solution.py:98
  13.7 48.7 %all_to_all.10 = bf16[128,8,512]{2,1,0:T(8,128)(2,1)S(1)} all-to-all(bf16[128,8,512]{2,1,0:T(8,128)(2,1)S(1)} %bitcast.76), channel_id=1, replica_groups=mesh['dp'=4,'expert'=128] {'expert'}, dimensions={0} | all-to-all | bytes 2097152 | tf_op jit(solution)/shard_map/all_to_all | solution.py:101
  62.4 0.3 fusion.30
  62.7 0.1 reshape.263
  62.9 0.1 reshape.268
  63.0 2.0 %fusion.13 = f32[512,1024]{1,0:T(8,128)S(1)} fusion(bf16[512,512]{1,0:T(8,128)(2,1)S(1)} %reshape.263, bf16[1,512,1024]{2,1,0:T(8,128)(2,1)} %param.10), kind=kOutput, calls=%fused_computation.27 | convolution fusion | flops 536870912 | bytes 3670016 | tf_op jit(solution)/shard_map/arc,ach->arh/dot_general | solution.py:105
  65.1 0.7 fusion.5
  65.8 1.4 %multiply_convert_fusion.2 = (bf16[512,1024]{1,0:T(8,128)(2,1)S(1)}, bf16[512,1024]{1,0:T(8,128)(2,1)S(1)}, bf16[512,1024]{1,0:T(8,128)(2,1)S(1)}) fusion(f32[512,1024]{1,0:T(8,128)S(1)} %fusion.13, f32[512,1024]{1,0:T(8,128)S(1)} %fusion.5, bf16[512,512]{1,0:T(8,128)(2,1)S(1)} %reshape.263, bf16[1,512,1024]{2,1,0:T(8,128)(2,1)S(1)} %copy-done), kind=kOutput, calls=%fused_computation.6 | convolution fusion | flops 544735232 | bytes 8912896 | tf_op jit(solution)/shard_map/arc,ach->arh/dot_general | solution.py:106
  67.3 0.8 fusion.3
  68.0 0.2 copy-done.9
  68.3 0.8 fusion.2
  69.0 0.8 fusion.1
  69.8 2.0 %pad_maximum_fusion = bf16[1024,3,512]{2,0,1:T(8,128)(2,1)} fusion(bf16[1024,1,512]{2,0,1:T(8,128)(2,1)S(1)} %fusion.3, bf16[1024,1,512]{2,0,1:T(8,128)(2,1)S(1)} %fusion.2, bf16[1024,1,512]{2,0,1:T(8,128)(2,1)S(1)} %fusion.1), kind=kLoop, calls=%fused_computation.3 | loop fusion | flops 3145728 | bytes 6291456 | tf_op jit(solution)/shard_map/stack | solution.py:135
  71.8 0.0 reduce-scatter.2.cloned.1.call-update
  71.8 1.2 copy-done.1
  73.0 2.1 %fusion.11 = f32[512,512]{1,0:T(8,128)S(1)} fusion(bf16[512,1024]{1,0:T(8,128)(2,1)} %copy-done.8, bf16[1,512,1024]{2,1,0:T(8,128)(2,1)S(1)} %copy-done.1), kind=kOutput, calls=%fused_computation.25 | convolution fusion | flops 536870912 | bytes 3145728 | tf_op jit(solution)/shard_map/arh,ach->arc/dot_general | solution.py:116
  75.1 0.7 fusion.4
  75.8 0.1 reshape.269
  75.9 1.9 %convolution_convert_fusion.3 = bf16[512,512]{1,0:T(8,128)(2,1)S(1)} fusion(bf16[512,1024]{1,0:T(8,128)(2,1)} %copy-done.9, bf16[1,1024,512]{2,1,0:T(8,128)(2,1)S(1)} %copy-done.2), kind=kOutput, calls=%fused_computation.17 | convolution fusion | flops 537133056 | bytes 2621440 | tf_op jit(solution)/shard_map/arh,ahc->arc/dot_general | solution.py:109
  77.9 0.1 reshape.267
  78.0 1.6 %pad_maximum_fusion.1 = bf16[128,8,512]{2,1,0:T(8,128)(2,1)} fusion(bf16[128,4,512]{2,1,0:T(4,128)(2,1)S(1)} %reshape.269, bf16[128,4,512]{2,1,0:T(4,128)(2,1)S(1)} %reshape.267), kind=kLoop, calls=%fused_computation.18 | loop fusion | flops 2097152 | bytes 2097152 | tf_op jit(solution)/shard_map/concatenate | solution.py:120
  79.6 6.9 %all-to-all-start.1 = ((bf16[128,8,512]{2,1,0:T(8,128)(2,1)}), bf16[128,8,512]{2,1,0:T(8,128)(2,1)S(1)}, u32[]{:S(2)}, u32[]{:S(2)}) async-start(bf16[128,8,512]{2,1,0:T(8,128)(2,1)} %pad_maximum_fusion.1), calls=%async_computation.1 | async-start | bytes 2097152 | tf_op jit(solution)/shard_map/all_to_all | solution.py:127
  86.6 0.1 copy.22
  86.7 0.1 mul.118
  86.8 30.1 %all-to-all-done.1 = bf16[128,8,512]{2,1,0:T(8,128)(2,1)S(1)} async-done(((bf16[128,8,512]{2,1,0:T(8,128)(2,1)}), bf16[128,8,512]{2,1,0:T(8,128)(2,1)S(1)}, u32[]{:S(2)}, u32[]{:S(2)}) %all-to-all-start.1) | async-done | bytes 1048608 | tf_op jit(solution)/shard_map/all_to_all | solution.py:127
  117.0 1.2 gather_fusion
  118.1 0.3 reshape.271
  118.5 1.2 gather_fusion.1
  119.6 0.3 reshape.272
  120.0 0.4 fusion.32
  120.4 0.4 fusion.31
  120.8 0.8 fusion.24
  121.6 1.9 %slice_bitcast_fusion = (bf16[1,256,512]{2,1,0:T(8,128)(2,1)}, bf16[1,512,256]{1,2,0:T(8,128)(2,1)S(1)}, bf16[1,512,256]{1,2,0:T(8,128)(2,1)S(1)}) fusion(bf16[256,3,512]{2,0,1:T(8,128)(2,1)} %reduce-scatter.2.cloned.1.call-done), kind=kLoop, calls=%fused_computation.35 | loop fusion | bytes 1572864 | tf_op jit(solution)/shard_map/broadcast_in_dim;squeeze | solution.py:146
  123.4 0.8 copy.27
  124.3 0.8 copy.28
  (32 shorter events, 0.2 us)
Async XLA Ops:
  7.2 58.6 %copy-start = (bf16[1,512,1024]{2,1,0:T(8,128)(2,1)S(1)}, bf16[1,512,1024]{2,1,0:T(8,128)(2,1)}, u32[]{:S(2)}) copy-start(bf16[1,512,1024]{2,1,0:T(8,128)(2,1)} %param.11) | copy-start | bytes 3145732
  7.2 3.3 %copy-start.5 = (f32[2]{0:T(128)S(1)}, f32[2]{0:T(128)}, u32[]{:S(2)}) copy-start(f32[2]{0:T(128)} %constant.27.clone) | copy-start | bytes 28
  7.2 3.4 %copy-start.3 = (bf16[128,512]{1,0:T(8,128)(2,1)S(1)}, bf16[128,512]{1,0:T(8,128)(2,1)}, u32[]{:S(2)}) copy-start(bf16[128,512]{1,0:T(8,128)(2,1)} %param.7) | copy-start | bytes 393220
  7.2 114.4 %reduce-scatter.2.cloned.1.call-start = ((), (), s32[]{:S(2)}) async-start(), calls=%async_computation.3 | async-start | bytes 3932160 | tf_op jit(solution)/shard_map/reduce_scatter | solution.py:143
  63.0 2.1 %copy-start.2 = (bf16[1,1024,512]{2,1,0:T(8,128)(2,1)S(1)}, bf16[1,1024,512]{2,1,0:T(8,128)(2,1)}, u32[]{:S(2)}) copy-start(bf16[1,1024,512]{2,1,0:T(8,128)(2,1)} %param.12) | copy-start | bytes 3145732
  67.3 1.0 copy-start.9
  67.3 1.7 %copy-start.6 = (bf16[512,1024]{1,0:T(8,128)(2,1)}, bf16[512,1024]{1,0:T(8,128)(2,1)S(1)}, u32[]{:S(2)}) copy-start(bf16[512,1024]{1,0:T(8,128)(2,1)S(1)} %get-tuple-element.19) | copy-start | bytes 3145732
  67.3 1.7 %copy-start.8 = (bf16[512,1024]{1,0:T(8,128)(2,1)}, bf16[512,1024]{1,0:T(8,128)(2,1)S(1)}, u32[]{:S(2)}) copy-start(bf16[512,1024]{1,0:T(8,128)(2,1)S(1)} %get-tuple-element.18) | copy-start | bytes 3145732
  71.8 1.2 copy-start.1
  73.0 2.1 %copy-start.7 = (bf16[512,1024]{1,0:T(8,128)(2,1)S(1)}, bf16[512,1024]{1,0:T(8,128)(2,1)}, u32[]{:S(2)}) copy-start(bf16[512,1024]{1,0:T(8,128)(2,1)} %copy-done.6) | copy-start | bytes 3145732
  78.0 8.5 %copy-start.4 = (s32[128,2]{0,1:T(2,128)S(1)}, s32[128,2]{0,1:T(2,128)}, u32[]{:S(2)}) copy-start(s32[128,2]{0,1:T(2,128)} %param.8) | copy-start | bytes 3076
  79.6 37.4 %all-to-all-start.1 = ((bf16[128,8,512]{2,1,0:T(8,128)(2,1)}), bf16[128,8,512]{2,1,0:T(8,128)(2,1)S(1)}, u32[]{:S(2)}, u32[]{:S(2)}) async-start(bf16[128,8,512]{2,1,0:T(8,128)(2,1)} %pad_maximum_fusion.1), calls=%async_computation.1 | async-start | bytes 2097152 | tf_op jit(solution)/shard_map/all_to_all | solution.py:127
Sparse Core Ops, SparseCore 0:
  71.9 37.6 reduce-scatter.1

commit v3 on v2

--- a/solution.py
+++ b/solution.py
@@ -73,6 +73,81 @@
         compiler_params=pltpu.CompilerParams(has_side_effects=True),
         cost_estimate=pl.CostEstimate(flops=0, bytes_accessed=2 * nbytes, transcendentals=0),
     )(send)
+
+
+def contract_rows(a, b):
+    return lax.dot_general(a, b, (((0,), (0,)), ((), ())), preferred_element_type=jnp.float32)
+
+
+def contract_cols(a, b):
+    return lax.dot_general(a, b, (((1,), (1,)), ((), ())), preferred_element_type=jnp.float32)
+
+
+def arm_kernel(tok_ref, cot_ref, wg_ref, wu_ref, wd_ref, out_ref, inp_ref, gu_ref, down_ref, acc_g, acc_u, acc_d):
+    step = pl.program_id(0)
+    hidden_width = wg_ref.shape[1]
+
+    @pl.when(step == 0)
+    def _():
+        acc_g[...] = jnp.zeros_like(acc_g)
+        acc_u[...] = jnp.zeros_like(acc_u)
+        acc_d[...] = jnp.zeros_like(acc_d)
+
+    x = tok_ref[...]
+    c = cot_ref[...]
+    wg = wg_ref[...]
+    wu = wu_ref[...]
+    wd = wd_ref[...]
+    gate_pre = jnp.dot(x, wg, preferred_element_type=jnp.float32)
+    up_pre = jnp.dot(x, wu, preferred_element_type=jnp.float32)
+    activated, silu_slope = silu_parts(gate_pre)
+    hidden = (activated * up_pre).astype(jnp.bfloat16)
+    out_ref[...] = jnp.dot(hidden, wd, preferred_element_type=jnp.float32).astype(out_ref.dtype)
+    d_hidden = contract_cols(c, wd)
+    d_up = (d_hidden * activated).astype(jnp.bfloat16)
+    d_gate = (d_hidden * up_pre * silu_slope).astype(jnp.bfloat16)
+    inp_ref[...] = (contract_cols(d_gate, wg) + contract_cols(d_up, wu)).astype(inp_ref.dtype)
+    acc_g[...] += contract_rows(x, d_gate)
+    acc_u[...] += contract_rows(x, d_up)
+    acc_d[...] += contract_rows(hidden, c)
+
+    @pl.when(step == pl.num_programs(0) - 1)
+    def _():
+        gu_ref[:, :hidden_width] = acc_g[...].astype(gu_ref.dtype)
+        gu_ref[:, hidden_width:] = acc_u[...].astype(gu_ref.dtype)
+        down_ref[...] = acc_d[...].astype(down_ref.dtype)
+
+
+def arm_math(tokens, cot, wg, wu, wd):
+    rows, width = tokens.shape
+    hidden_width = wg.shape[1]
+    block = 128
+    row_spec = pl.BlockSpec((block, width), lambda i: (i, 0))
+    whole = lambda shape: pl.BlockSpec(shape, lambda i: (0, 0))
+    flops = 2 * rows * width * hidden_width * 9
+    return pl.pallas_call(
+        arm_kernel,
+        grid=(rows // block,),
+        in_specs=[row_spec, row_spec, whole(wg.shape), whole(wu.shape), whole(wd.shape)],
+        out_specs=[row_spec, row_spec, whole((width, 2 * hidden_width)), whole((hidden_width, width))],
+        out_shape=[
+            jax.ShapeDtypeStruct((rows, width), jnp.bfloat16),
+            jax.ShapeDtypeStruct((rows, width), jnp.bfloat16),
+            jax.ShapeDtypeStruct((width, 2 * hidden_width), jnp.bfloat16),
+            jax.ShapeDtypeStruct((hidden_width, width), jnp.bfloat16),
+        ],
+        scratch_shapes=[
+            pltpu.VMEM((width, hidden_width), jnp.float32),
+            pltpu.VMEM((width, hidden_width), jnp.float32),
+            pltpu.VMEM((hidden_width, width), jnp.float32),
+        ],
+        compiler_params=pltpu.CompilerParams(
+            dimension_semantics=("arbitrary",), vmem_limit_bytes=48 * 1024 * 1024
+        ),
+        cost_estimate=pl.CostEstimate(
+            flops=flops, bytes_accessed=2 * (4 * rows * width + 6 * width * hidden_width), transcendentals=rows * hidden_width
+        ),
+    )(tokens, cot, wg, wu, wd)
 
 
 def on_device(tokens, codes, cotangent, w_gate, w_up, w_down):
@@ -102,21 +177,9 @@
     arm_tokens = got[:, :capacity].reshape(1, -1, feature_width)
     arm_cot = got[:, capacity:].reshape(1, -1, feature_width)
 
-    gate_pre = jnp.einsum("arc,ach->arh", arm_tokens, w_gate, preferred_element_type=jnp.float32)
-    up_pre = jnp.einsum("arc,ach->arh", arm_tokens, w_up, preferred_element_type=jnp.float32)
-    activated, silu_slope = silu_parts(gate_pre)
-    hidden = (activated * up_pre).astype(jnp.bfloat16)
-    out_rows = jnp.einsum(
-        "arh,ahc->arc", hidden, w_down, preferred_element_type=jnp.float32
-    ).astype(jnp.bfloat16)
-    d_hidden = jnp.einsum("arc,ahc->arh", arm_cot, w_down, preferred_element_type=jnp.float32)
-    d_up = (d_hidden * activated).astype(jnp.bfloat16)
-    d_gate = (d_hidden * up_pre * silu_slope).astype(jnp.bfloat16)
-    input_rows = (
-        jnp.einsum("arh,ach->arc", d_gate, w_gate, preferred_element_type=jnp.float32)
-        + jnp.einsum("arh,ach->arc", d_up, w_up, preferred_element_type=jnp.float32)
-    ).astype(jnp.bfloat16)
-
+    out_rows, input_rows, part_gu, part_down = arm_math(
+        arm_tokens[0], arm_cot[0], w_gate[0], w_up[0], w_down[0]
+    )
     ret = jnp.concatenate(
         [
             out_rows.reshape(-1, capacity, feature_width),
@@ -132,18 +195,14 @@
     )
     grad_tokens = (back_input[:, 0] + back_input[:, 1]).astype(jnp.bfloat16)
 
-    partials = jnp.stack(
-        [
-            jnp.einsum("arh,arc->hc", d_gate, arm_tokens, preferred_element_type=jnp.float32),
-            jnp.einsum("arh,arc->hc", d_up, arm_tokens, preferred_element_type=jnp.float32),
-            jnp.einsum("arh,arc->hc", hidden, arm_cot, preferred_element_type=jnp.float32),
-        ],
-        axis=1,
-    ).astype(jnp.bfloat16)
-    summed = lax.psum_scatter(partials, "dp", scatter_dimension=0, tiled=True)
-    grad_gate = summed[:, 0, :].T[None]
-    grad_up = summed[:, 1, :].T[None]
-    grad_down = summed[:, 2, :][None]
+    hidden_width = w_gate.shape[2]
+    summed_gu = lax.psum_scatter(
+        part_gu.reshape(feature_width, 2, hidden_width), "dp", scatter_dimension=2, tiled=True
+    )
+    summed_down = lax.psum_scatter(part_down, "dp", scatter_dimension=0, tiled=True)
+    grad_gate = summed_gu[None, :, 0, :]
+    grad_up = summed_gu[None, :, 1, :]
+    grad_down = summed_down[None]
     return (head_output, grad_tokens, grad_gate, grad_up, grad_down)
 
 

time: 132 us -> 150 us (1.14)
  Pallas kernels: 0 us -> 13.7 us
  waiting for transfers between devices: 30.1 us -> 43.7 us
  matrix products: 11.2 us -> 0 us
  local copies, waits for them, and re-layouts: 13 us -> 15.4 us
  other arithmetic: 7.63 us -> 5.61 us
    pallas_call x0 -> x1, Pallas kernels: none -> 13.7 us  [arm_math(): pl.pallas_call(arm_kernel, grid=(rows // block,), in_specs=[row_spec, row...]
    reduce_scatter x1 -> x2, waiting for transfers between devices: 0.01 us -> 13.7 us  [the longest x1 13.7 us: on_device(): lax.psum_scatter(part_down, 'dp', scatter_dimension=0, tiled=True)]
    dot_general x9 -> x0, matrix products: 11.2 us -> none  [the longest x1 2.05 us: on_device(): jnp.einsum('arh,ach->arc', d_gate, w_gate, preferred_element_type=jnp.flo...]
    reshape x0 -> x1, local copies, waits for them, and re-layouts: none -> 3.13 us  [on_device(): part_gu.reshape(feature_width, 2, hidden_width)]
    another operation x4 -> x3, other arithmetic: 2.23 us -> 0.26 us  [the longest x1 1.98 us: on_device(): jnp.stack([jnp.einsum('arh,arc->hc', d_gate, arm_tokens, preferred_elemen...]
    unnamed x24 -> x10, local copies, waits for them, and re-layouts: 4 us -> 2.67 us
  transfers between devices with their start and end apart: 2 -> 3, of which waited for: 1 -> 2; matrix products, arithmetic and copies ran while one was open for 9% -> 6% of each run, Pallas kernels for 0% -> 0%
where the time goes in v3:
time: 150 us; the launch traced here: 149 us
  blocking collectives  48.7 us (32%)
  waiting for transfers between devices  43.7 us (29%)
  local copies, waits for them, and re-layouts  15.4 us (10%)
  between operations  14.2 us (9%)
  Pallas kernels  13.7 us (9%)
  starting transfers between devices  7.14 us (5%)
  other arithmetic  5.61 us (4%)
    all_to_all x1, blocking collectives, on_device(): got = lax.all_to_all(send, 'expert', 0, 0, tiled=True)  48.7 us
    all_to_all x1, waiting for transfers between devices, on_device(): lax.all_to_all(ret, 'expert', 0, 0, tiled=True)  29.4 us
    pallas_call x1, Pallas kernels, arm_math(): pl.pallas_call(arm_kernel, grid=(rows // block,), in_specs=[row_spec, row...  13.7 us
    reduce_scatter x1, waiting for transfers between devices, on_device(): lax.psum_scatter(part_down, 'dp', scatter_dimension=0, tiled=True)  13.7 us
    all_to_all x1, starting transfers between devices, on_device(): lax.all_to_all(ret, 'expert', 0, 0, tiled=True)  7.06 us
    reshape x1, local copies, waits for them, and re-layouts, on_device(): part_gu.reshape(feature_width, 2, hidden_width)  3.13 us
  transfers between devices with their start and end apart: 3, of which 2 were waited for; matrix products, arithmetic and copies ran while one was open for 6% of the time, Pallas kernels for 0%

profile of v3, /device:TPU:1, one launch (start us, length us, event | category | flops | bytes accessed | tf_op | source)
XLA Modules:
  0.0 148.5 jit_solution(15452114888548958348)
XLA Ops:
  7.2 0.0 copy-start.2
  7.2 0.0 reduce-scatter.3.cloned.1.call-start
  7.2 0.8 copy.17
  8.0 0.1 reshape.192
  8.2 0.1 eq.26
  8.3 0.1 copy.19
  8.4 0.2 fusion.8
  8.7 0.2 fusion.12
  8.9 0.7 tile.2
  9.6 0.1 mul.78
  9.7 1.0 broadcast_in_dim.17
  10.8 0.1 reshape.194
  10.9 0.0 copy-done.2
  10.9 0.1 broadcast_in_dim.18
  11.1 0.4 reshape.195
  11.4 0.1 multiply_convert_fusion
  11.5 2.7 %scatter_custom_fusion = bf16[1024,512]{1,0:T(8,128)(2,1)S(1)} fusion(s32[512]{0:T(512)S(1)} %bitcast.53, bf16[256,512]{1,0:T(8,128)(2,1)S(1)} %multiply_convert_fusion, bf16[]{:T(256)} %constant.32, bf16[256,512]{1,0:T(8,128)(2,1)S(1)} %reshape.194, bf16[]{:T(256)} %constant.9.clone.1), kind=kCustom, calls=%fused_computation.5 | custom fusion | flops 1048576 | bytes 1572868 | tf_op jit(solution)/shard_map/scatter | solution.py:173
  14.3 48.7 %all_to_all.10 = bf16[128,8,512]{2,1,0:T(8,128)(2,1)S(1)} all-to-all(bf16[128,8,512]{2,1,0:T(8,128)(2,1)S(1)} %bitcast.43), channel_id=1, replica_groups=mesh['dp'=4,'expert'=128] {'expert'}, dimensions={0} | all-to-all | bytes 2097152 | tf_op jit(solution)/shard_map/all_to_all | solution.py:176
  62.9 0.0 copy-start
  62.9 0.3 fusion.15
  63.3 0.1 squeeze_reshape.7.cot_ref
  63.4 0.1 squeeze_reshape.6.tok_ref
  63.6 0.6 copy-done
  64.2 0.0 copy-start.1
  64.2 1.2 copy-done.1
  65.4 13.7 %shard_map.110 = (bf16[512,512]{1,0:T(8,128)(2,1)S(1)}, bf16[512,512]{1,0:T(8,128)(2,1)S(1)}, bf16[512,2048]{1,0:T(8,128)(2,1)}, bf16[1024,512]{1,0:T(8,128)(2,1)}) custom-call(bf16[512,512]{1,0:T(8,128)(2,1)S(1)} %squeeze_reshape.6.tok_ref, bf16[512,512]{1,0:T(8,128)(2,1)S(1)} %squeeze_reshape.7.cot_ref, bf16[512,1024]{1,0:T(8,128)(2,1)S(1)} %bitcast.38, ...), custom_call_target="tpu_custom_call" | custom-call | flops 4831838208 | bytes 8388608 | tf_op jit(solution)/shard_map/pallas_call | solution.py:128
  79.1 3.1 %copy.53 = bf16[64,2,8,1024]{3,2,0,1:T(8,128)(2,1)} copy(bf16[64,2,8,1024]{3,2,1,0:T(8,128)(2,1)} %bitcast.44) | data formatting | bytes 4194304 | tf_op jit(solution)/shard_map/reshape | solution.py:200
  82.3 0.0 reduce-scatter.3.cloned.1.call-update
  82.3 0.1 reshape.197
  82.4 0.1 reshape.198
  82.6 1.5 %pad_maximum_fusion = bf16[128,8,512]{2,1,0:T(8,128)(2,1)} fusion(bf16[128,4,512]{2,1,0:T(4,128)(2,1)S(1)} %reshape.198, bf16[128,4,512]{2,1,0:T(4,128)(2,1)S(1)} %reshape.197), kind=kLoop, calls=%fused_computation.4 | loop fusion | flops 2097152 | bytes 2097152 | tf_op jit(solution)/shard_map/concatenate | solution.py:183
  84.1 0.0 copy-start.3
  84.1 7.1 %all-to-all-start.1 = ((bf16[128,8,512]{2,1,0:T(8,128)(2,1)}), bf16[128,8,512]{2,1,0:T(8,128)(2,1)S(1)}, u32[]{:S(2)}, u32[]{:S(2)}) async-start(bf16[128,8,512]{2,1,0:T(8,128)(2,1)} %pad_maximum_fusion), calls=%async_computation.1 | async-start | bytes 2097152 | tf_op jit(solution)/shard_map/all_to_all | solution.py:190
  91.1 0.0 reduce-scatter.5.cloned.1.call-start
  91.2 0.7 reduce-scatter.5.cloned.1.call-update
  91.9 0.0 copy-done.3
  91.9 0.1 copy.21
  92.0 0.1 mul.83
  92.2 29.4 %all-to-all-done.1 = bf16[128,8,512]{2,1,0:T(8,128)(2,1)S(1)} async-done(((bf16[128,8,512]{2,1,0:T(8,128)(2,1)}), bf16[128,8,512]{2,1,0:T(8,128)(2,1)S(1)}, u32[]{:S(2)}, u32[]{:S(2)}) %all-to-all-start.1) | async-done | bytes 1048608 | tf_op jit(solution)/shard_map/all_to_all | solution.py:190
  121.6 1.2 gather_fusion.1
  122.7 1.2 gather_fusion
  123.9 0.3 reshape.201
  124.2 0.3 reshape.202
  124.6 0.4 fusion.17
  125.0 0.4 fusion.16
  125.4 0.8 fusion.9
  126.2 1.9 %slice_bitcast_fusion = (bf16[1,512,256]{2,1,0:T(8,128)(2,1)}, bf16[1,512,256]{2,1,0:T(8,128)(2,1)}) fusion(bf16[512,2,256]{2,0,1:T(8,128)(2,1)} %reduce-scatter.3.cloned.1.call-done), kind=kLoop, calls=%fused_computation.11 | loop fusion | bytes 1048576 | tf_op jit(solution)/shard_map/broadcast_in_dim;squeeze | solution.py:204
  128.0 13.7 %reduce-scatter.5.cloned.1.call-done = bf16[256,512]{1,0:T(8,128)(2,1)} async-done(((bf16[1024,512]{1,0:T(8,128)(2,1)}), bf16[256,512]{1,0:T(8,128)(2,1)}) %reduce-scatter.5.cloned.1.call-update) | async-done | bytes 262160 | tf_op jit(solution)/shard_map/reduce_scatter | solution.py:202
  (13 shorter events, 0.1 us)
Async XLA Ops:
  7.2 3.7 %copy-start.2 = (bf16[128,512]{1,0:T(8,128)(2,1)S(1)}, bf16[128,512]{1,0:T(8,128)(2,1)}, u32[]{:S(2)}) copy-start(bf16[128,512]{1,0:T(8,128)(2,1)} %param.9) | copy-start | bytes 393220
  7.2 119.0 %reduce-scatter.3.cloned.1.call-start = ((), (), s32[]{:S(2)}) async-start(), calls=%async_computation.4 | async-start | bytes 2621440 | tf_op jit(solution)/shard_map/reduce_scatter | solution.py:199
  62.9 1.2 copy-start
  64.2 1.2 copy-start.1
  84.1 7.8 %copy-start.3 = (s32[128,2]{0,1:T(2,128)S(1)}, s32[128,2]{0,1:T(2,128)}, u32[]{:S(2)}) copy-start(s32[128,2]{0,1:T(2,128)} %param.8) | copy-start | bytes 3076
  84.1 37.5 %all-to-all-start.1 = ((bf16[128,8,512]{2,1,0:T(8,128)(2,1)}), bf16[128,8,512]{2,1,0:T(8,128)(2,1)S(1)}, u32[]{:S(2)}, u32[]{:S(2)}) async-start(bf16[128,8,512]{2,1,0:T(8,128)(2,1)} %pad_maximum_fusion), calls=%async_computation.1 | async-start | bytes 2097152 | tf_op jit(solution)/shard_map/all_to_all | solution.py:190
  91.1 50.6 %reduce-scatter.5.cloned.1.call-start = ((), (), s32[]{:S(2)}) async-start(), calls=%async_computation.5 | async-start | bytes 1310720 | tf_op jit(solution)/shard_map/reduce_scatter | solution.py:202
Sparse Core Ops, SparseCore 0:
  82.4 29.0 reduce-scatter.2
  115.1 26.5 reduce-scatter.4

commit v4 on v3

--- a/solution.py
+++ b/solution.py
@@ -83,7 +83,7 @@
     return lax.dot_general(a, b, (((1,), (1,)), ((), ())), preferred_element_type=jnp.float32)
 
 
-def arm_kernel(tok_ref, cot_ref, wg_ref, wu_ref, wd_ref, out_ref, inp_ref, gu_ref, down_ref, acc_g, acc_u, acc_d):
+def arm_kernel(tok_ref, cot_ref, wg_ref, wu_ref, wd_ref, out_ref, inp_ref, part_ref, acc_g, acc_u, acc_d):
     step = pl.program_id(0)
     hidden_width = wg_ref.shape[1]
 
@@ -109,19 +109,19 @@
     inp_ref[...] = (contract_cols(d_gate, wg) + contract_cols(d_up, wu)).astype(inp_ref.dtype)
     acc_g[...] += contract_rows(x, d_gate)
     acc_u[...] += contract_rows(x, d_up)
-    acc_d[...] += contract_rows(hidden, c)
+    acc_d[...] += contract_rows(c, hidden)
 
     @pl.when(step == pl.num_programs(0) - 1)
     def _():
-        gu_ref[:, :hidden_width] = acc_g[...].astype(gu_ref.dtype)
-        gu_ref[:, hidden_width:] = acc_u[...].astype(gu_ref.dtype)
-        down_ref[...] = acc_d[...].astype(down_ref.dtype)
+        part_ref[0] = acc_g[...].astype(part_ref.dtype)
+        part_ref[1] = acc_u[...].astype(part_ref.dtype)
+        part_ref[2] = acc_d[...].astype(part_ref.dtype)
 
 
 def arm_math(tokens, cot, wg, wu, wd):
     rows, width = tokens.shape
     hidden_width = wg.shape[1]
-    block = 128
+    block = 256
     row_spec = pl.BlockSpec((block, width), lambda i: (i, 0))
     whole = lambda shape: pl.BlockSpec(shape, lambda i: (0, 0))
     flops = 2 * rows * width * hidden_width * 9
@@ -129,17 +129,20 @@
         arm_kernel,
         grid=(rows // block,),
         in_specs=[row_spec, row_spec, whole(wg.shape), whole(wu.shape), whole(wd.shape)],
-        out_specs=[row_spec, row_spec, whole((width, 2 * hidden_width)), whole((hidden_width, width))],
+        out_specs=[
+            row_spec,
+            row_spec,
+            pl.BlockSpec((3, width, hidden_width), lambda i: (0, 0, 0)),
+        ],
         out_shape=[
             jax.ShapeDtypeStruct((rows, width), jnp.bfloat16),
             jax.ShapeDtypeStruct((rows, width), jnp.bfloat16),
-            jax.ShapeDtypeStruct((width, 2 * hidden_width), jnp.bfloat16),
-            jax.ShapeDtypeStruct((hidden_width, width), jnp.bfloat16),
+            jax.ShapeDtypeStruct((3, width, hidden_width), jnp.bfloat16),
         ],
         scratch_shapes=[
             pltpu.VMEM((width, hidden_width), jnp.float32),
             pltpu.VMEM((width, hidden_width), jnp.float32),
-            pltpu.VMEM((hidden_width, width), jnp.float32),
+            pltpu.VMEM((width, hidden_width), jnp.float32),
         ],
         compiler_params=pltpu.CompilerParams(
             dimension_semantics=("arbitrary",), vmem_limit_bytes=48 * 1024 * 1024
@@ -177,7 +180,7 @@
     arm_tokens = got[:, :capacity].reshape(1, -1, feature_width)
     arm_cot = got[:, capacity:].reshape(1, -1, feature_width)
 
-    out_rows, input_rows, part_gu, part_down = arm_math(
+    out_rows, input_rows, partials = arm_math(
         arm_tokens[0], arm_cot[0], w_gate[0], w_up[0], w_down[0]
     )
     ret = jnp.concatenate(
@@ -195,14 +198,10 @@
     )
     grad_tokens = (back_input[:, 0] + back_input[:, 1]).astype(jnp.bfloat16)
 
-    hidden_width = w_gate.shape[2]
-    summed_gu = lax.psum_scatter(
-        part_gu.reshape(feature_width, 2, hidden_width), "dp", scatter_dimension=2, tiled=True
-    )
-    summed_down = lax.psum_scatter(part_down, "dp", scatter_dimension=0, tiled=True)
-    grad_gate = summed_gu[None, :, 0, :]
-    grad_up = summed_gu[None, :, 1, :]
-    grad_down = summed_down[None]
+    summed = lax.psum_scatter(partials, "dp", scatter_dimension=2, tiled=True)
+    grad_gate = summed[0:1]
+    grad_up = summed[1:2]
+    grad_down = summed[2].T[None]
     return (head_output, grad_tokens, grad_gate, grad_up, grad_down)
 
 

time: 150 us -> 128 us (0.85)
  waiting for transfers between devices: 43.7 us -> 30.1 us
  Pallas kernels: 13.7 us -> 7.93 us
    reduce_scatter x2 -> x1, waiting for transfers between devices: 13.7 us -> 0.01 us  [on_device(): summed = lax.psum_scatter(partials, 'dp', scatter_dimension=2, tiled=True)]
    pallas_call x1, Pallas kernels: 13.7 us -> 7.93 us  [arm_math(): pl.pallas_call(arm_kernel, grid=(rows // block,), in_specs=[row_spec, row...]
    reshape x1 -> x0, local copies, waits for them, and re-layouts: 3.13 us -> none  [on_device(): part_gu.reshape(feature_width, 2, hidden_width)]
    unnamed x10 -> x13, local copies, waits for them, and re-layouts: 2.67 us -> 4.74 us
    broadcast_in_dim x0 -> x1, local copies, waits for them, and re-layouts: none -> 1.95 us  [on_device(): grad_down = summed[2].T[None]]
    another operation x4 -> x3, local copies, waits for them, and re-layouts: 1.87 us -> 0.02 us  [the longest x1 1.85 us: on_device(): grad_up = summed_gu[None, :, 1, :]]
  transfers between devices with their start and end apart: 3 -> 2, of which waited for: 2 -> 1; matrix products, arithmetic and copies ran while one was open for 6% -> 5% of each run, Pallas kernels for 0% -> 0%
where the time goes in v4:
time: 128 us
  blocking collectives  48.7 us (38%)
  waiting for transfers between devices  30.1 us (24%)
  local copies, waits for them, and re-layouts  14.4 us (11%)
  between operations  14.2 us (11%)
  Pallas kernels  7.93 us (6%)
  starting transfers between devices  6.96 us (5%)
  other arithmetic  5.59 us (4%)
    all_to_all x1, blocking collectives, on_device(): got = lax.all_to_all(send, 'expert', 0, 0, tiled=True)  48.7 us
    all_to_all x1, waiting for transfers between devices, on_device(): lax.all_to_all(ret, 'expert', 0, 0, tiled=True)  30.1 us
    pallas_call x1, Pallas kernels, arm_math(): pl.pallas_call(arm_kernel, grid=(rows // block,), in_specs=[row_spec, row...  7.93 us
    all_to_all x1, starting transfers between devices, on_device(): lax.all_to_all(ret, 'expert', 0, 0, tiled=True)  6.92 us
    unnamed x13, local copies, waits for them, and re-layouts  4.74 us
    scatter x1, other arithmetic, on_device(): send = jnp.zeros((arm_count * 2 * capacity, feature_width), jnp.bfloat16)...  2.74 us
  transfers between devices with their start and end apart: 2, of which 1 were waited for; matrix products, arithmetic and copies ran while one was open for 5% of the time, Pallas kernels for 0%

profile of v4, /device:TPU:1, one launch (start us, length us, event | category | flops | bytes accessed | tf_op | source)
XLA Modules:
  0.0 128.0 jit_solution(90419961524556713)
XLA Ops:
  7.2 0.0 copy-start.3
  7.2 0.0 reduce-scatter.2.cloned.1.call-start
  7.2 0.8 copy.17
  8.0 0.1 reshape.189
  8.2 0.1 eq.26
  8.3 0.1 copy.19
  8.4 0.2 fusion.8
  8.7 0.2 fusion.12
  8.9 0.7 tile.2
  9.6 0.1 mul.78
  9.7 1.0 broadcast_in_dim.17
  10.8 0.1 reshape.191
  10.9 0.0 copy-done.3
  10.9 0.1 broadcast_in_dim.18
  11.1 0.4 reshape.192
  11.4 0.1 multiply_convert_fusion
  11.5 2.7 %scatter_custom_fusion = bf16[1024,512]{1,0:T(8,128)(2,1)S(1)} fusion(s32[512]{0:T(512)S(1)} %bitcast.49, bf16[256,512]{1,0:T(8,128)(2,1)S(1)} %multiply_convert_fusion, bf16[]{:T(256)} %constant.32, bf16[256,512]{1,0:T(8,128)(2,1)S(1)} %reshape.191, bf16[]{:T(256)} %constant.9.clone.1), kind=kCustom, calls=%fused_computation.4 | custom fusion | flops 1048576 | bytes 1572868 | tf_op jit(solution)/shard_map/scatter | solution.py:176
  14.3 48.7 %all_to_all.10 = bf16[128,8,512]{2,1,0:T(8,128)(2,1)S(1)} all-to-all(bf16[128,8,512]{2,1,0:T(8,128)(2,1)S(1)} %bitcast.40), channel_id=1, replica_groups=mesh['dp'=4,'expert'=128] {'expert'}, dimensions={0} | all-to-all | bytes 2097152 | tf_op jit(solution)/shard_map/all_to_all | solution.py:179
  62.9 0.0 copy-start
  63.0 0.3 fusion.15
  63.3 0.1 squeeze_reshape.7.cot_ref
  63.4 0.1 squeeze_reshape.6.tok_ref
  63.6 0.6 copy-done
  64.2 0.0 copy-start.1
  64.2 1.2 copy-done.1
  65.4 0.0 copy-start.2
  65.4 1.2 copy-done.2
  66.6 7.9 %shard_map.110 = (bf16[512,512]{1,0:T(8,128)(2,1)S(1)}, bf16[512,512]{1,0:T(8,128)(2,1)S(1)}, bf16[3,512,1024]{2,1,0:T(8,128)(2,1)}) custom-call(bf16[512,512]{1,0:T(8,128)(2,1)S(1)} %squeeze_reshape.6.tok_ref, bf16[512,512]{1,0:T(8,128)(2,1)S(1)} %squeeze_reshape.7.cot_ref, bf16[512,1024]{1,0:T(8,128)(2,1)S(1)} %bitcast.35, bf16[512,1024]{1,0:T(8,128)(2,1)S(1)} %bitcast.36, ...), custom_call_target="tpu_custom_call" | custom-call | flops 4831838208 | bytes 8388608 | tf_op jit(solution)/shard_map/pallas_call | solution.py:128
  74.6 0.0 reduce-scatter.2.cloned.1.call-update
  74.6 0.1 reshape.194
  74.7 0.1 reshape.195
  74.8 0.0 copy-start.4
  74.9 1.5 %pad_maximum_fusion = bf16[128,8,512]{2,1,0:T(8,128)(2,1)} fusion(bf16[128,4,512]{2,1,0:T(4,128)(2,1)S(1)} %reshape.195, bf16[128,4,512]{2,1,0:T(4,128)(2,1)S(1)} %reshape.194), kind=kLoop, calls=%fused_computation.3 | loop fusion | flops 2097152 | bytes 2097152 | tf_op jit(solution)/shard_map/concatenate | solution.py:186
  76.3 6.9 %all-to-all-start.1 = ((bf16[128,8,512]{2,1,0:T(8,128)(2,1)}), bf16[128,8,512]{2,1,0:T(8,128)(2,1)S(1)}, u32[]{:S(2)}, u32[]{:S(2)}) async-start(bf16[128,8,512]{2,1,0:T(8,128)(2,1)} %pad_maximum_fusion), calls=%async_computation.1 | async-start | bytes 2097152 | tf_op jit(solution)/shard_map/all_to_all | solution.py:193
  83.3 0.0 copy-done.4
  83.3 0.1 copy.21
  83.4 0.1 mul.83
  83.6 30.1 %all-to-all-done.1 = bf16[128,8,512]{2,1,0:T(8,128)(2,1)S(1)} async-done(((bf16[128,8,512]{2,1,0:T(8,128)(2,1)}), bf16[128,8,512]{2,1,0:T(8,128)(2,1)S(1)}, u32[]{:S(2)}, u32[]{:S(2)}) %all-to-all-start.1) | async-done | bytes 1048608 | tf_op jit(solution)/shard_map/all_to_all | solution.py:193
  113.7 1.2 gather_fusion.1
  114.9 1.2 gather_fusion
  116.0 0.3 reshape.197
  116.4 0.3 reshape.198
  116.7 0.4 fusion.17
  117.1 0.4 fusion.16
  117.5 0.8 fusion.9
  118.3 0.0 reduce-scatter.2.cloned.1.call-done
  118.3 1.9 %slice_bitcast_fusion = (bf16[1,256,512]{1,2,0:T(8,128)(2,1)S(1)}, bf16[1,512,256]{2,1,0:T(8,128)(2,1)}, bf16[1,512,256]{2,1,0:T(8,128)(2,1)}) fusion(bf16[3,512,256]{2,1,0:T(8,128)(2,1)} %reduce-scatter.2.cloned.1.call-done), kind=kLoop, calls=%fused_computation.10 | loop fusion | bytes 1572864 | tf_op jit(solution)/shard_map/broadcast_in_dim | solution.py:204
  120.3 0.8 copy.26
  (12 shorter events, 0.1 us)
Async XLA Ops:
  7.2 3.7 %copy-start.3 = (bf16[128,512]{1,0:T(8,128)(2,1)S(1)}, bf16[128,512]{1,0:T(8,128)(2,1)}, u32[]{:S(2)}) copy-start(bf16[128,512]{1,0:T(8,128)(2,1)} %param.9) | copy-start | bytes 393220
  7.2 111.1 %reduce-scatter.2.cloned.1.call-start = ((), (), s32[]{:S(2)}) async-start(), calls=%async_computation.3 | async-start | bytes 3932160 | tf_op jit(solution)/shard_map/reduce_scatter | solution.py:201
  62.9 1.2 copy-start
  64.2 1.2 copy-start.1
  65.4 1.2 copy-start.2
  74.8 8.4 %copy-start.4 = (s32[128,2]{0,1:T(2,128)S(1)}, s32[128,2]{0,1:T(2,128)}, u32[]{:S(2)}) copy-start(s32[128,2]{0,1:T(2,128)} %param.8) | copy-start | bytes 3076
  76.3 37.4 %all-to-all-start.1 = ((bf16[128,8,512]{2,1,0:T(8,128)(2,1)}), bf16[128,8,512]{2,1,0:T(8,128)(2,1)S(1)}, u32[]{:S(2)}, u32[]{:S(2)}) async-start(bf16[128,8,512]{2,1,0:T(8,128)(2,1)} %pad_maximum_fusion), calls=%async_computation.1 | async-start | bytes 2097152 | tf_op jit(solution)/shard_map/all_to_all | solution.py:193
Sparse Core Ops, SparseCore 0:
  74.7 37.5 reduce-scatter.1

commit v5 on v4

--- a/solution.py
+++ b/solution.py
@@ -83,25 +83,41 @@
     return lax.dot_general(a, b, (((1,), (1,)), ((), ())), preferred_element_type=jnp.float32)
 
 
-def arm_kernel(tok_ref, cot_ref, wg_ref, wu_ref, wd_ref, out_ref, inp_ref, part_ref, acc_g, acc_u, acc_d):
+def arm_kernel(
+    tok_ref, cot_ref, wg_hbm, wu_hbm, wd_hbm, out_ref, inp_ref, part_ref,
+    wg_ref, wu_ref, wd_ref, acc_g, acc_u, acc_d, sems,
+):
     step = pl.program_id(0)
     hidden_width = wg_ref.shape[1]
+    loads = [
+        pltpu.make_async_copy(src, dst, sems.at[k])
+        for k, (src, dst) in enumerate(((wg_hbm, wg_ref), (wu_hbm, wu_ref), (wd_hbm, wd_ref)))
+    ]
 
     @pl.when(step == 0)
     def _():
+        for load in loads:
+            load.start()
         acc_g[...] = jnp.zeros_like(acc_g)
         acc_u[...] = jnp.zeros_like(acc_u)
         acc_d[...] = jnp.zeros_like(acc_d)
+        loads[0].wait()
+        loads[1].wait()
 
     x = tok_ref[...]
     c = cot_ref[...]
     wg = wg_ref[...]
     wu = wu_ref[...]
-    wd = wd_ref[...]
     gate_pre = jnp.dot(x, wg, preferred_element_type=jnp.float32)
     up_pre = jnp.dot(x, wu, preferred_element_type=jnp.float32)
     activated, silu_slope = silu_parts(gate_pre)
     hidden = (activated * up_pre).astype(jnp.bfloat16)
+
+    @pl.when(step == 0)
+    def _():
+        loads[2].wait()
+
+    wd = wd_ref[...]
     out_ref[...] = jnp.dot(hidden, wd, preferred_element_type=jnp.float32).astype(out_ref.dtype)
     d_hidden = contract_cols(c, wd)
     d_up = (d_hidden * activated).astype(jnp.bfloat16)
@@ -123,12 +139,11 @@
     hidden_width = wg.shape[1]
     block = 256
     row_spec = pl.BlockSpec((block, width), lambda i: (i, 0))
-    whole = lambda shape: pl.BlockSpec(shape, lambda i: (0, 0))
     flops = 2 * rows * width * hidden_width * 9
     return pl.pallas_call(
         arm_kernel,
         grid=(rows // block,),
-        in_specs=[row_spec, row_spec, whole(wg.shape), whole(wu.shape), whole(wd.shape)],
+        in_specs=[row_spec, row_spec] + [pl.BlockSpec(memory_space=pl.ANY)] * 3,
         out_specs=[
             row_spec,
             row_spec,
@@ -140,9 +155,13 @@
             jax.ShapeDtypeStruct((3, width, hidden_width), jnp.bfloat16),
         ],
         scratch_shapes=[
+            pltpu.VMEM(wg.shape, wg.dtype),
+            pltpu.VMEM(wu.shape, wu.dtype),
+            pltpu.VMEM(wd.shape, wd.dtype),
             pltpu.VMEM((width, hidden_width), jnp.float32),
             pltpu.VMEM((width, hidden_width), jnp.float32),
             pltpu.VMEM((width, hidden_width), jnp.float32),
+            pltpu.SemaphoreType.DMA((3,)),
         ],
         compiler_params=pltpu.CompilerParams(
             dimension_semantics=("arbitrary",), vmem_limit_bytes=48 * 1024 * 1024

time: 128 us -> 129 us (level)
  no operation moved by 1% of the time
where the time goes in v5:
time: 129 us; the launch traced here: 128 us
  blocking collectives  48.7 us (38%)
  waiting for transfers between devices  30.1 us (23%)
  local copies, waits for them, and re-layouts  14.4 us (11%)
  between operations  14.3 us (11%)
  Pallas kernels  8.44 us (7%)
  starting transfers between devices  6.97 us (5%)
  other arithmetic  5.59 us (4%)
    all_to_all x1, blocking collectives, on_device(): got = lax.all_to_all(send, 'expert', 0, 0, tiled=True)  48.7 us
    all_to_all x1, waiting for transfers between devices, on_device(): lax.all_to_all(ret, 'expert', 0, 0, tiled=True)  30.1 us
    pallas_call x1, Pallas kernels, arm_math(): pl.pallas_call(arm_kernel, grid=(rows // block,), in_specs=[row_spec, row...  8.44 us
    all_to_all x1, starting transfers between devices, on_device(): lax.all_to_all(ret, 'expert', 0, 0, tiled=True)  6.93 us
    unnamed x13, local copies, waits for them, and re-layouts  4.74 us
    scatter x1, other arithmetic, on_device(): send = jnp.zeros((arm_count * 2 * capacity, feature_width), jnp.bfloat16)...  2.74 us
  transfers between devices with their start and end apart: 2, of which 1 were waited for; matrix products, arithmetic and copies ran while one was open for 5% of the time, Pallas kernels for 0%

profile of v5, /device:TPU:1, one launch (start us, length us, event | category | flops | bytes accessed | tf_op | source)
XLA Modules:
  0.0 128.5 jit_solution(13993422030919202048)
XLA Ops:
  7.2 0.0 copy-start.3
  7.2 0.0 reduce-scatter.2.cloned.1.call-start
  7.2 0.8 copy.17
  8.0 0.1 reshape.189
  8.2 0.1 eq.26
  8.3 0.1 copy.19
  8.4 0.2 fusion.8
  8.7 0.2 fusion.12
  8.9 0.7 tile.2
  9.6 0.1 mul.78
  9.7 1.0 broadcast_in_dim.17
  10.8 0.1 reshape.191
  10.9 0.0 copy-done.3
  10.9 0.1 broadcast_in_dim.18
  11.1 0.4 reshape.192
  11.4 0.1 multiply_convert_fusion
  11.5 2.7 %scatter_custom_fusion = bf16[1024,512]{1,0:T(8,128)(2,1)S(1)} fusion(s32[512]{0:T(512)S(1)} %bitcast.49, bf16[256,512]{1,0:T(8,128)(2,1)S(1)} %multiply_convert_fusion, bf16[]{:T(256)} %constant.32, bf16[256,512]{1,0:T(8,128)(2,1)S(1)} %reshape.191, bf16[]{:T(256)} %constant.9.clone.1), kind=kCustom, calls=%fused_computation.4 | custom fusion | flops 1048576 | bytes 1572868 | tf_op jit(solution)/shard_map/scatter | solution.py:195
  14.3 48.7 %all_to_all.10 = bf16[128,8,512]{2,1,0:T(8,128)(2,1)S(1)} all-to-all(bf16[128,8,512]{2,1,0:T(8,128)(2,1)S(1)} %bitcast.40), channel_id=1, replica_groups=mesh['dp'=4,'expert'=128] {'expert'}, dimensions={0} | all-to-all | bytes 2097152 | tf_op jit(solution)/shard_map/all_to_all | solution.py:198
  62.9 0.0 copy-start
  63.0 0.3 fusion.15
  63.3 0.1 squeeze_reshape.7.cot_ref
  63.4 0.1 squeeze_reshape.6.tok_ref
  63.6 0.6 copy-done
  64.2 0.0 copy-start.1
  64.2 1.2 copy-done.1
  65.4 0.0 copy-start.2
  65.4 1.2 copy-done.2
  66.6 8.4 %shard_map.110 = (bf16[512,512]{1,0:T(8,128)(2,1)S(1)}, bf16[512,512]{1,0:T(8,128)(2,1)S(1)}, bf16[3,512,1024]{2,1,0:T(8,128)(2,1)}) custom-call(bf16[512,512]{1,0:T(8,128)(2,1)S(1)} %squeeze_reshape.6.tok_ref, bf16[512,512]{1,0:T(8,128)(2,1)S(1)} %squeeze_reshape.7.cot_ref, bf16[512,1024]{1,0:T(8,128)(2,1)S(1)} %bitcast.35, bf16[512,1024]{1,0:T(8,128)(2,1)S(1)} %bitcast.36, ...), custom_call_target="tpu_custom_call" | custom-call | flops 4831838208 | bytes 8388608 | tf_op jit(solution)/shard_map/pallas_call | solution.py:143
  75.1 0.0 reduce-scatter.2.cloned.1.call-update
  75.1 0.1 reshape.194
  75.2 0.1 reshape.195
  75.4 0.0 copy-start.4
  75.4 1.5 %pad_maximum_fusion = bf16[128,8,512]{2,1,0:T(8,128)(2,1)} fusion(bf16[128,4,512]{2,1,0:T(4,128)(2,1)S(1)} %reshape.195, bf16[128,4,512]{2,1,0:T(4,128)(2,1)S(1)} %reshape.194), kind=kLoop, calls=%fused_computation.3 | loop fusion | flops 2097152 | bytes 2097152 | tf_op jit(solution)/shard_map/concatenate | solution.py:205
  76.9 6.9 %all-to-all-start.1 = ((bf16[128,8,512]{2,1,0:T(8,128)(2,1)}), bf16[128,8,512]{2,1,0:T(8,128)(2,1)S(1)}, u32[]{:S(2)}, u32[]{:S(2)}) async-start(bf16[128,8,512]{2,1,0:T(8,128)(2,1)} %pad_maximum_fusion), calls=%async_computation.1 | async-start | bytes 2097152 | tf_op jit(solution)/shard_map/all_to_all | solution.py:212
  83.8 0.0 copy-done.4
  83.8 0.1 copy.21
  83.9 0.1 mul.83
  84.1 30.1 %all-to-all-done.1 = bf16[128,8,512]{2,1,0:T(8,128)(2,1)S(1)} async-done(((bf16[128,8,512]{2,1,0:T(8,128)(2,1)}), bf16[128,8,512]{2,1,0:T(8,128)(2,1)S(1)}, u32[]{:S(2)}, u32[]{:S(2)}) %all-to-all-start.1) | async-done | bytes 1048608 | tf_op jit(solution)/shard_map/all_to_all | solution.py:212
  114.2 1.2 gather_fusion.1
  115.4 1.2 gather_fusion
  116.5 0.3 reshape.197
  116.9 0.3 reshape.198
  117.2 0.4 fusion.17
  117.6 0.4 fusion.16
  118.1 0.8 fusion.9
  118.8 0.0 reduce-scatter.2.cloned.1.call-done
  118.8 1.9 %slice_bitcast_fusion = (bf16[1,256,512]{1,2,0:T(8,128)(2,1)S(1)}, bf16[1,512,256]{2,1,0:T(8,128)(2,1)}, bf16[1,512,256]{2,1,0:T(8,128)(2,1)}) fusion(bf16[3,512,256]{2,1,0:T(8,128)(2,1)} %reduce-scatter.2.cloned.1.call-done), kind=kLoop, calls=%fused_computation.10 | loop fusion | bytes 1572864 | tf_op jit(solution)/shard_map/broadcast_in_dim | solution.py:223
  120.8 0.8 copy.26
  (12 shorter events, 0.1 us)
Async XLA Ops:
  7.2 3.7 %copy-start.3 = (bf16[128,512]{1,0:T(8,128)(2,1)S(1)}, bf16[128,512]{1,0:T(8,128)(2,1)}, u32[]{:S(2)}) copy-start(bf16[128,512]{1,0:T(8,128)(2,1)} %param.9) | copy-start | bytes 393220
  7.2 111.7 %reduce-scatter.2.cloned.1.call-start = ((), (), s32[]{:S(2)}) async-start(), calls=%async_computation.3 | async-start | bytes 3932160 | tf_op jit(solution)/shard_map/reduce_scatter | solution.py:220
  62.9 1.2 copy-start
  64.2 1.2 copy-start.1
  65.4 1.2 copy-start.2
  75.4 8.4 %copy-start.4 = (s32[128,2]{0,1:T(2,128)S(1)}, s32[128,2]{0,1:T(2,128)}, u32[]{:S(2)}) copy-start(s32[128,2]{0,1:T(2,128)} %param.8) | copy-start | bytes 3076
  76.9 37.4 %all-to-all-start.1 = ((bf16[128,8,512]{2,1,0:T(8,128)(2,1)}), bf16[128,8,512]{2,1,0:T(8,128)(2,1)S(1)}, u32[]{:S(2)}, u32[]{:S(2)}) async-start(bf16[128,8,512]{2,1,0:T(8,128)(2,1)} %pad_maximum_fusion), calls=%async_computation.1 | async-start | bytes 2097152 | tf_op jit(solution)/shard_map/all_to_all | solution.py:212
Sparse Core Ops, SparseCore 0:
  75.2 37.6 reduce-scatter.1

commit v6 on v5

--- a/solution.py
+++ b/solution.py
@@ -143,7 +143,7 @@
     return pl.pallas_call(
         arm_kernel,
         grid=(rows // block,),
-        in_specs=[row_spec, row_spec] + [pl.BlockSpec(memory_space=pl.ANY)] * 3,
+        in_specs=[row_spec, row_spec] + [pl.BlockSpec(memory_space=pltpu.HBM)] * 3,
         out_specs=[
             row_spec,
             row_spec,
@@ -164,7 +164,7 @@
             pltpu.SemaphoreType.DMA((3,)),
         ],
         compiler_params=pltpu.CompilerParams(
-            dimension_semantics=("arbitrary",), vmem_limit_bytes=48 * 1024 * 1024
+            dimension_semantics=("arbitrary",), vmem_limit_bytes=67043328
         ),
         cost_estimate=pl.CostEstimate(
             flops=flops, bytes_accessed=2 * (4 * rows * width + 6 * width * hidden_width), transcendentals=rows * hidden_width

time: 129 us -> 131 us (1.016)
  Pallas kernels: 8.44 us -> 10.6 us
    pallas_call x1, Pallas kernels: 8.44 us -> 10.6 us  [arm_math(): pl.pallas_call(arm_kernel, grid=(rows // block,), in_specs=[row_spec, row...]
    unnamed x13 -> x15, local copies, waits for them, and re-layouts: 4.74 us -> 3.27 us
where the time goes in v6:
time: 131 us
  blocking collectives  48.7 us (37%)
  waiting for transfers between devices  30.1 us (23%)
  local copies, waits for them, and re-layouts  14.6 us (11%)
  between operations  14.3 us (11%)
  Pallas kernels  10.6 us (8%)
  starting transfers between devices  6.97 us (5%)
  other arithmetic  5.59 us (4%)
    all_to_all x1, blocking collectives, on_device(): got = lax.all_to_all(send, 'expert', 0, 0, tiled=True)  48.7 us
    all_to_all x1, waiting for transfers between devices, on_device(): lax.all_to_all(ret, 'expert', 0, 0, tiled=True)  30.1 us
    pallas_call x1, Pallas kernels, arm_math(): pl.pallas_call(arm_kernel, grid=(rows // block,), in_specs=[row_spec, row...  10.6 us
    all_to_all x1, starting transfers between devices, on_device(): lax.all_to_all(ret, 'expert', 0, 0, tiled=True)  6.93 us
    unnamed x15, local copies, waits for them, and re-layouts  3.27 us
    scatter x1, other arithmetic, on_device(): send = jnp.zeros((arm_count * 2 * capacity, feature_width), jnp.bfloat16)...  2.74 us
  transfers between devices with their start and end apart: 2, of which 1 were waited for; matrix products, arithmetic and copies ran while one was open for 5% of the time, Pallas kernels for 0%

profile of v6, /device:TPU:1, one launch (start us, length us, event | category | flops | bytes accessed | tf_op | source)
XLA Modules:
  0.0 130.8 jit_solution(7197662555439815313)
XLA Ops:
  7.2 0.0 copy-start.2
  7.2 0.0 reduce-scatter.2.cloned.1.call-start
  7.2 0.8 copy.17
  8.0 0.1 reshape.189
  8.2 0.1 eq.26
  8.3 0.1 copy.19
  8.4 0.2 fusion.8
  8.7 0.2 fusion.12
  8.9 0.0 copy-start.3
  8.9 0.5 copy-done.3
  9.5 0.7 tile.2
  10.2 0.1 mul.78
  10.3 1.0 broadcast_in_dim.17
  11.3 0.1 reshape.191
  11.5 0.0 copy-done.2
  11.5 0.1 broadcast_in_dim.18
  11.6 0.4 reshape.192
  12.0 0.1 multiply_convert_fusion
  12.1 2.7 %scatter_custom_fusion = bf16[1024,512]{1,0:T(8,128)(2,1)S(1)} fusion(s32[512]{0:T(512)S(1)} %bitcast.46, bf16[256,512]{1,0:T(8,128)(2,1)S(1)} %multiply_convert_fusion, bf16[]{:T(256)} %constant.32, bf16[256,512]{1,0:T(8,128)(2,1)S(1)} %reshape.191, bf16[]{:T(256)} %constant.9.clone.1), kind=kCustom, calls=%fused_computation.4 | custom fusion | flops 1048576 | bytes 1572868 | tf_op jit(solution)/shard_map/scatter | solution.py:195
  14.8 48.7 %all_to_all.10 = bf16[128,8,512]{2,1,0:T(8,128)(2,1)S(1)} all-to-all(bf16[128,8,512]{2,1,0:T(8,128)(2,1)S(1)} %bitcast.37), channel_id=1, replica_groups=mesh['dp'=4,'expert'=128] {'expert'}, dimensions={0} | all-to-all | bytes 2097152 | tf_op jit(solution)/shard_map/all_to_all | solution.py:198
  63.5 0.3 fusion.15
  63.8 0.9 squeeze_reshape.7.cot_ref
  64.8 0.9 squeeze_reshape.6.tok_ref
  65.7 10.6 %shard_map.110 = (bf16[512,512]{1,0:T(8,128)(2,1)}, bf16[512,512]{1,0:T(8,128)(2,1)}, bf16[3,512,1024]{2,1,0:T(8,128)(2,1)}) custom-call(bf16[512,512]{1,0:T(8,128)(2,1)} %squeeze_reshape.6.tok_ref, bf16[512,512]{1,0:T(8,128)(2,1)} %squeeze_reshape.7.cot_ref, bf16[512,1024]{1,0:T(8,128)(2,1)} %bitcast.47, bf16[512,1024]{1,0:T(8,128)(2,1)} %bitcast.48, ...), custom_call_target="tpu_custom_call" | custom-call | flops 4831838208 | bytes 8388608 | tf_op jit(solution)/shard_map/pallas_call | solution.py:143
  76.3 0.0 copy-start.1
  76.4 0.0 copy-start
  76.4 0.0 reduce-scatter.2.cloned.1.call-update
  76.4 1.0 copy-done.1
  77.4 0.1 reshape.194
  77.5 0.0 copy-done
  77.6 0.1 reshape.195
  77.7 0.0 copy-start.5
  77.7 0.0 copy-start.4
  77.7 1.5 %pad_maximum_fusion = bf16[128,8,512]{2,1,0:T(8,128)(2,1)} fusion(bf16[128,4,512]{2,1,0:T(4,128)(2,1)S(1)} %reshape.195, bf16[128,4,512]{2,1,0:T(4,128)(2,1)S(1)} %reshape.194), kind=kLoop, calls=%fused_computation.3 | loop fusion | flops 2097152 | bytes 2097152 | tf_op jit(solution)/shard_map/concatenate | solution.py:205
  79.2 6.9 %all-to-all-start.1 = ((bf16[128,8,512]{2,1,0:T(8,128)(2,1)}), bf16[128,8,512]{2,1,0:T(8,128)(2,1)S(1)}, u32[]{:S(2)}, u32[]{:S(2)}) async-start(bf16[128,8,512]{2,1,0:T(8,128)(2,1)} %pad_maximum_fusion), calls=%async_computation.1 | async-start | bytes 2097152 | tf_op jit(solution)/shard_map/all_to_all | solution.py:212
  86.1 0.0 copy-done.5
  86.2 0.1 copy.21
  86.3 0.1 mul.83
  86.5 30.1 %all-to-all-done.1 = bf16[128,8,512]{2,1,0:T(8,128)(2,1)S(1)} async-done(((bf16[128,8,512]{2,1,0:T(8,128)(2,1)}), bf16[128,8,512]{2,1,0:T(8,128)(2,1)S(1)}, u32[]{:S(2)}, u32[]{:S(2)}) %all-to-all-start.1) | async-done | bytes 1048608 | tf_op jit(solution)/shard_map/all_to_all | solution.py:212
  116.6 1.2 gather_fusion.1
  117.7 1.2 gather_fusion
  118.9 0.3 reshape.197
  119.2 0.3 reshape.198
  119.6 0.4 fusion.17
  120.0 0.4 fusion.16
  120.4 0.8 fusion.9
  121.2 1.9 %slice_bitcast_fusion = (bf16[1,256,512]{1,2,0:T(8,128)(2,1)S(1)}, bf16[1,512,256]{2,1,0:T(8,128)(2,1)}, bf16[1,512,256]{2,1,0:T(8,128)(2,1)}) fusion(bf16[3,512,256]{2,1,0:T(8,128)(2,1)} %reduce-scatter.2.cloned.1.call-done), kind=kLoop, calls=%fused_computation.10 | loop fusion | bytes 1572864 | tf_op jit(solution)/shard_map/broadcast_in_dim | solution.py:223
  123.1 0.8 copy.26
  (14 shorter events, 0.1 us)
Async XLA Ops:
  7.2 4.3 %copy-start.2 = (bf16[128,512]{1,0:T(8,128)(2,1)S(1)}, bf16[128,512]{1,0:T(8,128)(2,1)}, u32[]{:S(2)}) copy-start(bf16[128,512]{1,0:T(8,128)(2,1)} %param.9) | copy-start | bytes 393220
  7.2 114.0 %reduce-scatter.2.cloned.1.call-start = ((), (), s32[]{:S(2)}) async-start(), calls=%async_computation.3 | async-start | bytes 3932160 | tf_op jit(solution)/shard_map/reduce_scatter | solution.py:220
  8.9 0.6 copy-start.3
  76.3 1.0 copy-start.1
  76.4 1.2 copy-start
  77.7 8.5 %copy-start.5 = (s32[128,2]{0,1:T(2,128)S(1)}, s32[128,2]{0,1:T(2,128)}, u32[]{:S(2)}) copy-start(s32[128,2]{0,1:T(2,128)} %param.8) | copy-start | bytes 3076
  77.7 8.7 %copy-start.4 = (s32[256]{0:T(256)S(1)}, s32[256]{0:T(256)}, u32[]{:S(2)}) copy-start(s32[256]{0:T(256)} %copy-done.3) | copy-start | bytes 3076
  79.2 37.4 %all-to-all-start.1 = ((bf16[128,8,512]{2,1,0:T(8,128)(2,1)}), bf16[128,8,512]{2,1,0:T(8,128)(2,1)S(1)}, u32[]{:S(2)}, u32[]{:S(2)}) async-start(bf16[128,8,512]{2,1,0:T(8,128)(2,1)} %pad_maximum_fusion), calls=%async_computation.1 | async-start | bytes 2097152 | tf_op jit(solution)/shard_map/all_to_all | solution.py:212
Sparse Core Ops, SparseCore 0:
  76.5 37.6 reduce-scatter.1

commit v7 on v4

--- a/solution.py
+++ b/solution.py
@@ -165,15 +165,17 @@
     slot = jnp.sum(earlier * onehot, axis=1)
     tok_dest = flat_codes * (2 * capacity) + slot
     cot_dest = tok_dest + capacity
-    shares = jnp.tile(jnp.array([fact_share, counter_share], jnp.float32), token_count)
-    token_rows = jnp.repeat(tokens, 2, axis=0)
-    cot_rows = (jnp.repeat(cotangent.astype(jnp.float32), 2, axis=0) * shares[:, None]).astype(
-        jnp.bfloat16
-    )
+    cot_f = cotangent.astype(jnp.float32)
+    sources = jnp.concatenate(
+        [tokens, tokens, (cot_f * fact_share).astype(jnp.bfloat16), (cot_f * counter_share).astype(jnp.bfloat16)]
+    )
+    dest = jnp.concatenate([tok_dest[0::2], tok_dest[1::2], cot_dest[0::2], cot_dest[1::2]])
+    place = (
+        lax.broadcasted_iota(jnp.int32, (arm_count * 2 * capacity, dest.shape[0]), 0) == dest[None, :]
+    ).astype(jnp.bfloat16)
     send = (
-        jnp.zeros((arm_count * 2 * capacity, feature_width), jnp.bfloat16)
-        .at[jnp.concatenate([tok_dest, cot_dest])]
-        .set(jnp.concatenate([token_rows, cot_rows]))
+        jnp.dot(place, sources, preferred_element_type=jnp.float32)
+        .astype(jnp.bfloat16)
         .reshape(arm_count, 2 * capacity, feature_width)
     )
     got = lax.all_to_all(send, "expert", 0, 0, tiled=True)
@@ -190,13 +192,12 @@
         ],
         axis=1,
     )
-    back = lax.all_to_all(ret, "expert", 0, 0, tiled=True).reshape(arm_count * 2 * capacity, feature_width)
-    back_out = back[tok_dest].reshape(token_count, 2, feature_width).astype(jnp.float32)
-    back_input = back[cot_dest].reshape(token_count, 2, feature_width).astype(jnp.float32)
-    head_output = (fact_share * back_out[:, 0] + counter_share * back_out[:, 1]).astype(
-        jnp.bfloat16
-    )
-    grad_tokens = (back_input[:, 0] + back_input[:, 1]).astype(jnp.bfloat16)
+    back = lax.all_to_all(ret, "expert", 0, 0, tiled=True).reshape(-1, feature_width)
+    picked = lax.dot_general(
+        place, back, (((0,), (0,)), ((), ())), preferred_element_type=jnp.float32
+    ).reshape(4, token_count, feature_width)
+    head_output = (fact_share * picked[0] + counter_share * picked[1]).astype(jnp.bfloat16)
+    grad_tokens = (picked[2] + picked[3]).astype(jnp.bfloat16)
 
     summed = lax.psum_scatter(partials, "dp", scatter_dimension=2, tiled=True)
     grad_gate = summed[0:1]

time: 128 us -> 122 us (0.953)
  blocking collectives: 48.7 us -> 85.8 us
  waiting for transfers between devices: 30.1 us -> 0.02 us
  starting transfers between devices: 6.96 us -> 0.04 us
  local copies, waits for them, and re-layouts: 14.4 us -> 8.8 us
  other arithmetic: 5.59 us -> 2.71 us
  matrix products: 0 us -> 2.45 us
    all_to_all x0 -> x1, blocking collectives: none -> 37.2 us  [on_device(): lax.all_to_all(ret, 'expert', 0, 0, tiled=True).reshape(-1, feature_width)]
    all_to_all x1 -> x0, waiting for transfers between devices: 30.1 us -> none  [on_device(): lax.all_to_all(ret, 'expert', 0, 0, tiled=True)]
    all_to_all x1 -> x0, starting transfers between devices: 6.92 us -> none  [on_device(): lax.all_to_all(ret, 'expert', 0, 0, tiled=True)]
    scatter x1 -> x0, other arithmetic: 2.74 us -> none  [on_device(): send = jnp.zeros((arm_count * 2 * capacity, feature_width), jnp.bfloat16)...]
    dot_general x0 -> x2, matrix products: none -> 2.45 us  [the longest x1 1.7 us: on_device(): jnp.dot(place, sources, preferred_element_type=jnp.float32)]
    gather x2 -> x0, local copies, waits for them, and re-layouts: 2.3 us -> none  [the longest x1 1.15 us: on_device(): back[cot_dest].reshape(token_count, 2, feature_width).astype(jnp.float32)]
    unnamed x13 -> x9, local copies, waits for them, and re-layouts: 4.74 us -> 4.7 us
  transfers between devices with their start and end apart: 2 -> 1, of which waited for: 1 -> 0; matrix products, arithmetic and copies ran while one was open for 5% -> 2% of each run, Pallas kernels for 0% -> 0%
where the time goes in v7:
time: 122 us
  blocking collectives  85.8 us (70%)
  between operations  14.1 us (12%)
  local copies, waits for them, and re-layouts  8.8 us (7%)
  Pallas kernels  7.94 us (7%)
  other arithmetic  2.71 us (2%)
  matrix products  2.45 us (2%)
    all_to_all x1, blocking collectives, on_device(): got = lax.all_to_all(send, 'expert', 0, 0, tiled=True)  48.7 us
    all_to_all x1, blocking collectives, on_device(): lax.all_to_all(ret, 'expert', 0, 0, tiled=True).reshape(-1, feature_width)  37.2 us
    pallas_call x1, Pallas kernels, arm_math(): pl.pallas_call(arm_kernel, grid=(rows // block,), in_specs=[row_spec, row...  7.94 us
    unnamed x9, local copies, waits for them, and re-layouts  4.7 us
  transfers between devices with their start and end apart: 1, of which 0 were waited for; matrix products, arithmetic and copies ran while one was open for 2% of the time, Pallas kernels for 0%

profile of v7, /device:TPU:1, one launch (start us, length us, event | category | flops | bytes accessed | tf_op | source)
XLA Modules:
  0.0 121.9 jit_solution(5243513218253950690)
XLA Ops:
  7.2 0.0 reduce-scatter.2.cloned.1.call-start
  7.2 0.8 copy.12
  8.0 0.1 reshape.52
  8.1 0.1 eq.34
  8.3 0.1 copy.14
  8.4 0.2 fusion.19
  8.7 0.2 fusion.21
  8.9 0.2 slice.54
  9.1 0.2 slice.53
  9.3 0.2 slice.52
  9.6 0.2 slice.51
  9.8 0.9 fusion.14
  10.8 1.7 %fusion.3 = bf16[128,8,512]{2,1,0:T(8,128)(2,1)S(1)} fusion(s32[512]{0:T(512)S(1)} %pad_add_fusion, bf16[128,512]{1,0:T(8,128)(2,1)S(1)} %get-tuple-element.31, bf16[128,512]{1,0:T(8,128)(2,1)S(1)} %get-tuple-element.30, bf16[128,512]{1,0:T(8,128)(2,1)} %param.6), kind=kOutput, calls=%fused_computation.4 | convolution fusion | flops 540016640 | bytes 1443840 | tf_op jit(solution)/shard_map/dot_general | solution.py:177
  12.5 48.7 %all_to_all.10 = bf16[128,8,512]{2,1,0:T(8,128)(2,1)S(1)} all-to-all(bf16[128,8,512]{2,1,0:T(8,128)(2,1)S(1)} %fusion.3), channel_id=1, replica_groups=mesh['dp'=4,'expert'=128] {'expert'}, dimensions={0} | all-to-all | bytes 2097152 | tf_op jit(solution)/shard_map/all_to_all | solution.py:181
  61.1 0.0 copy-start
  61.1 0.3 fusion.25
  61.5 0.1 squeeze_reshape.7.cot_ref
  61.6 0.1 squeeze_reshape.6.tok_ref
  61.7 0.6 copy-done
  62.4 0.0 copy-start.1
  62.4 1.2 %copy-done.1 = bf16[1,512,1024]{2,1,0:T(8,128)(2,1)S(1)} copy-done((bf16[1,512,1024]{2,1,0:T(8,128)(2,1)S(1)}, bf16[1,512,1024]{2,1,0:T(8,128)(2,1)}, u32[]{:S(2)}) %copy-start.1) | copy-done | bytes 1048600
  63.6 0.0 copy-start.2
  63.6 1.2 %copy-done.2 = bf16[1,1024,512]{2,1,0:T(8,128)(2,1)S(1)} copy-done((bf16[1,1024,512]{2,1,0:T(8,128)(2,1)S(1)}, bf16[1,1024,512]{2,1,0:T(8,128)(2,1)}, u32[]{:S(2)}) %copy-start.2) | copy-done | bytes 1048600
  64.8 7.9 %shard_map.101 = (bf16[512,512]{1,0:T(8,128)(2,1)S(1)}, bf16[512,512]{1,0:T(8,128)(2,1)S(1)}, bf16[3,512,1024]{2,1,0:T(8,128)(2,1)}) custom-call(bf16[512,512]{1,0:T(8,128)(2,1)S(1)} %squeeze_reshape.6.tok_ref, bf16[512,512]{1,0:T(8,128)(2,1)S(1)} %squeeze_reshape.7.cot_ref, bf16[512,1024]{1,0:T(8,128)(2,1)S(1)} %bitcast.27, bf16[512,1024]{1,0:T(8,128)(2,1)S(1)} %bitcast.28, ...), custom_call_target="tpu_custom_call" | custom-call | flops 4831838208 | bytes 8388608 | tf_op jit(solution)/shard_map/pallas_call | solution.py:128
  72.7 0.0 reduce-scatter.2.cloned.1.call-update
  72.8 0.1 reshape.55
  72.9 0.1 reshape.56
  73.0 0.5 pad_maximum_fusion
  73.6 37.2 %all_to_all.11 = bf16[128,8,512]{2,1,0:T(8,128)(2,1)S(1)} all-to-all(bf16[128,8,512]{2,1,0:T(8,128)(2,1)S(1)} %pad_maximum_fusion), channel_id=1, replica_groups=mesh['dp'=4,'expert'=128] {'expert'}, dimensions={0} | all-to-all | bytes 2097152 | tf_op jit(solution)/shard_map/all_to_all | solution.py:195
  110.7 0.8 fusion
  111.5 0.8 fusion.16
  112.3 0.0 reduce-scatter.2.cloned.1.call-done
  112.3 1.9 %slice_bitcast_fusion = (bf16[1,256,512]{1,2,0:T(8,128)(2,1)S(1)}, bf16[1,512,256]{2,1,0:T(8,128)(2,1)}, bf16[1,512,256]{2,1,0:T(8,128)(2,1)}) fusion(bf16[3,512,256]{2,1,0:T(8,128)(2,1)} %reduce-scatter.2.cloned.1.call-done), kind=kLoop, calls=%fused_computation.20 | loop fusion | bytes 1572864 | tf_op jit(solution)/shard_map/broadcast_in_dim | solution.py:205
  114.2 0.8 copy.16
  (8 shorter events, 0.1 us)
Async XLA Ops:
  7.2 105.1 %reduce-scatter.2.cloned.1.call-start = ((), (), s32[]{:S(2)}) async-start(), calls=%async_computation.3 | async-start | bytes 3932160 | tf_op jit(solution)/shard_map/reduce_scatter | solution.py:202
  61.1 1.2 %copy-start = (bf16[1,512,1024]{2,1,0:T(8,128)(2,1)S(1)}, bf16[1,512,1024]{2,1,0:T(8,128)(2,1)}, u32[]{:S(2)}) copy-start(bf16[1,512,1024]{2,1,0:T(8,128)(2,1)} %param.9) | copy-start | bytes 3145732
  62.4 1.2 %copy-start.1 = (bf16[1,512,1024]{2,1,0:T(8,128)(2,1)S(1)}, bf16[1,512,1024]{2,1,0:T(8,128)(2,1)}, u32[]{:S(2)}) copy-start(bf16[1,512,1024]{2,1,0:T(8,128)(2,1)} %param.10) | copy-start | bytes 3145732
  63.6 1.2 %copy-start.2 = (bf16[1,1024,512]{2,1,0:T(8,128)(2,1)S(1)}, bf16[1,1024,512]{2,1,0:T(8,128)(2,1)}, u32[]{:S(2)}) copy-start(bf16[1,1024,512]{2,1,0:T(8,128)(2,1)} %param.11) | copy-start | bytes 3145732
Sparse Core Ops, SparseCore 0:
  72.9 37.6 reduce-scatter.1

commit v8 on v7

--- a/solution.py
+++ b/solution.py
@@ -121,7 +121,7 @@
 def arm_math(tokens, cot, wg, wu, wd):
     rows, width = tokens.shape
     hidden_width = wg.shape[1]
-    block = 256
+    block = 512
     row_spec = pl.BlockSpec((block, width), lambda i: (i, 0))
     whole = lambda shape: pl.BlockSpec(shape, lambda i: (0, 0))
     flops = 2 * rows * width * hidden_width * 9

time: 122 us -> 121 us (level)
  no operation moved by 1% of the time
where the time goes in v8:
time: 121 us
  blocking collectives  85.8 us (71%)
  between operations  14.1 us (12%)
  local copies, waits for them, and re-layouts  8.8 us (7%)
  Pallas kernels  7.01 us (6%)
  other arithmetic  2.71 us (2%)
  matrix products  2.45 us (2%)
    all_to_all x1, blocking collectives, on_device(): got = lax.all_to_all(send, 'expert', 0, 0, tiled=True)  48.7 us
    all_to_all x1, blocking collectives, on_device(): lax.all_to_all(ret, 'expert', 0, 0, tiled=True).reshape(-1, feature_width)  37.2 us
    pallas_call x1, Pallas kernels, arm_math(): pl.pallas_call(arm_kernel, grid=(rows // block,), in_specs=[row_spec, row...  7.01 us
    unnamed x9, local copies, waits for them, and re-layouts  4.7 us
  transfers between devices with their start and end apart: 1, of which 0 were waited for; matrix products, arithmetic and copies ran while one was open for 2% of the time, Pallas kernels for 0%

profile of v8, /device:TPU:1, one launch (start us, length us, event | category | flops | bytes accessed | tf_op | source)
XLA Modules:
  0.0 121.0 jit_solution(2655489625047367248)
XLA Ops:
  7.2 0.0 reduce-scatter.2.cloned.1.call-start
  7.2 0.8 copy.12
  8.0 0.1 reshape.52
  8.1 0.1 eq.34
  8.3 0.1 copy.14
  8.4 0.2 fusion.19
  8.7 0.2 fusion.21
  8.9 0.2 slice.54
  9.1 0.2 slice.53
  9.3 0.2 slice.52
  9.6 0.2 slice.51
  9.8 0.9 fusion.14
  10.8 1.7 %fusion.3 = bf16[128,8,512]{2,1,0:T(8,128)(2,1)S(1)} fusion(s32[512]{0:T(512)S(1)} %pad_add_fusion, bf16[128,512]{1,0:T(8,128)(2,1)S(1)} %get-tuple-element.31, bf16[128,512]{1,0:T(8,128)(2,1)S(1)} %get-tuple-element.30, bf16[128,512]{1,0:T(8,128)(2,1)} %param.6), kind=kOutput, calls=%fused_computation.4 | convolution fusion | flops 540016640 | bytes 1443840 | tf_op jit(solution)/shard_map/dot_general | solution.py:177
  12.5 48.7 %all_to_all.10 = bf16[128,8,512]{2,1,0:T(8,128)(2,1)S(1)} all-to-all(bf16[128,8,512]{2,1,0:T(8,128)(2,1)S(1)} %fusion.3), channel_id=1, replica_groups=mesh['dp'=4,'expert'=128] {'expert'}, dimensions={0} | all-to-all | bytes 2097152 | tf_op jit(solution)/shard_map/all_to_all | solution.py:181
  61.1 0.0 copy-start
  61.1 0.3 fusion.25
  61.5 0.1 squeeze_reshape.7.cot_ref
  61.6 0.1 squeeze_reshape.6.tok_ref
  61.7 0.6 copy-done
  62.4 0.0 copy-start.1
  62.4 1.2 %copy-done.1 = bf16[1,512,1024]{2,1,0:T(8,128)(2,1)S(1)} copy-done((bf16[1,512,1024]{2,1,0:T(8,128)(2,1)S(1)}, bf16[1,512,1024]{2,1,0:T(8,128)(2,1)}, u32[]{:S(2)}) %copy-start.1) | copy-done | bytes 1048600
  63.6 0.0 copy-start.2
  63.6 1.2 %copy-done.2 = bf16[1,1024,512]{2,1,0:T(8,128)(2,1)S(1)} copy-done((bf16[1,1024,512]{2,1,0:T(8,128)(2,1)S(1)}, bf16[1,1024,512]{2,1,0:T(8,128)(2,1)}, u32[]{:S(2)}) %copy-start.2) | copy-done | bytes 1048600
  64.8 7.0 %shard_map.101 = (bf16[512,512]{1,0:T(8,128)(2,1)S(1)}, bf16[512,512]{1,0:T(8,128)(2,1)S(1)}, bf16[3,512,1024]{2,1,0:T(8,128)(2,1)}) custom-call(bf16[512,512]{1,0:T(8,128)(2,1)S(1)} %squeeze_reshape.6.tok_ref, bf16[512,512]{1,0:T(8,128)(2,1)S(1)} %squeeze_reshape.7.cot_ref, bf16[512,1024]{1,0:T(8,128)(2,1)S(1)} %bitcast.27, bf16[512,1024]{1,0:T(8,128)(2,1)S(1)} %bitcast.28, ...), custom_call_target="tpu_custom_call" | custom-call | flops 4831838208 | bytes 8388608 | tf_op jit(solution)/shard_map/pallas_call | solution.py:128
  71.8 0.0 reduce-scatter.2.cloned.1.call-update
  71.8 0.1 reshape.55
  72.0 0.1 reshape.56
  72.1 0.5 pad_maximum_fusion
  72.6 37.2 %all_to_all.11 = bf16[128,8,512]{2,1,0:T(8,128)(2,1)S(1)} all-to-all(bf16[128,8,512]{2,1,0:T(8,128)(2,1)S(1)} %pad_maximum_fusion), channel_id=1, replica_groups=mesh['dp'=4,'expert'=128] {'expert'}, dimensions={0} | all-to-all | bytes 2097152 | tf_op jit(solution)/shard_map/all_to_all | solution.py:195
  109.8 0.8 fusion
  110.6 0.8 fusion.16
  111.3 0.0 reduce-scatter.2.cloned.1.call-done
  111.3 1.9 %slice_bitcast_fusion = (bf16[1,256,512]{1,2,0:T(8,128)(2,1)S(1)}, bf16[1,512,256]{2,1,0:T(8,128)(2,1)}, bf16[1,512,256]{2,1,0:T(8,128)(2,1)}) fusion(bf16[3,512,256]{2,1,0:T(8,128)(2,1)} %reduce-scatter.2.cloned.1.call-done), kind=kLoop, calls=%fused_computation.20 | loop fusion | bytes 1572864 | tf_op jit(solution)/shard_map/broadcast_in_dim | solution.py:205
  113.3 0.8 copy.16
  (8 shorter events, 0.1 us)
Async XLA Ops:
  7.2 104.2 %reduce-scatter.2.cloned.1.call-start = ((), (), s32[]{:S(2)}) async-start(), calls=%async_computation.3 | async-start | bytes 3932160 | tf_op jit(solution)/shard_map/reduce_scatter | solution.py:202
  61.1 1.2 %copy-start = (bf16[1,512,1024]{2,1,0:T(8,128)(2,1)S(1)}, bf16[1,512,1024]{2,1,0:T(8,128)(2,1)}, u32[]{:S(2)}) copy-start(bf16[1,512,1024]{2,1,0:T(8,128)(2,1)} %param.9) | copy-start | bytes 3145732
  62.4 1.2 %copy-start.1 = (bf16[1,512,1024]{2,1,0:T(8,128)(2,1)S(1)}, bf16[1,512,1024]{2,1,0:T(8,128)(2,1)}, u32[]{:S(2)}) copy-start(bf16[1,512,1024]{2,1,0:T(8,128)(2,1)} %param.10) | copy-start | bytes 3145732
  63.6 1.2 %copy-start.2 = (bf16[1,1024,512]{2,1,0:T(8,128)(2,1)S(1)}, bf16[1,1024,512]{2,1,0:T(8,128)(2,1)}, u32[]{:S(2)}) copy-start(bf16[1,1024,512]{2,1,0:T(8,128)(2,1)} %param.11) | copy-start | bytes 3145732
Sparse Core Ops, SparseCore 0:
  72.0 37.6 reduce-scatter.1

commit v9 on v8

--- a/solution.py
+++ b/solution.py
@@ -153,6 +153,34 @@
     )(tokens, cot, wg, wu, wd)
 
 
+def reduce_over_dp(partials):
+    n = lax.axis_size("dp")
+    if n != 4:
+        return lax.psum_scatter(partials, "dp", scatter_dimension=2, tiled=True)
+    me = lax.axis_index("dp")
+    width = partials.shape[2] // n
+    rows = partials.shape[1]
+    half = rows // 2
+
+    def quarter(offset):
+        return lax.dynamic_slice_in_dim(partials, lax.rem(me + offset, n) * width, width, axis=2)
+
+    right = [(i, (i + 1) % n) for i in range(n)]
+    left = [(i, (i - 1) % n) for i in range(n)]
+    across = quarter(2)
+    from_left = lax.ppermute(jnp.concatenate([quarter(1), across[:, :half]], axis=1), "dp", right)
+    from_right = lax.ppermute(jnp.concatenate([quarter(n - 1), across[:, half:]], axis=1), "dp", left)
+    far_first = lax.ppermute(from_left[:, rows:], "dp", right)
+    far_second = lax.ppermute(from_right[:, rows:], "dp", left)
+    total = (
+        quarter(0).astype(jnp.float32)
+        + from_left[:, :rows].astype(jnp.float32)
+        + from_right[:, :rows].astype(jnp.float32)
+        + jnp.concatenate([far_first, far_second], axis=1).astype(jnp.float32)
+    )
+    return total.astype(jnp.bfloat16)
+
+
 def on_device(tokens, codes, cotangent, w_gate, w_up, w_down):
     token_count, feature_width = tokens.shape
     local_arms = w_gate.shape[0]
@@ -199,7 +227,7 @@
     head_output = (fact_share * picked[0] + counter_share * picked[1]).astype(jnp.bfloat16)
     grad_tokens = (picked[2] + picked[3]).astype(jnp.bfloat16)
 
-    summed = lax.psum_scatter(partials, "dp", scatter_dimension=2, tiled=True)
+    summed = reduce_over_dp(partials)
     grad_gate = summed[0:1]
     grad_up = summed[1:2]
     grad_down = summed[2].T[None]

time: 121 us -> 127 us (1.050)
  the two profiles are of different devices: /device:TPU:1 before, /device:TPU:24 now
where the time goes in v9:
time: 127 us; the launch traced here: 126 us
  waiting for transfers between devices  54.9 us (43%)
  starting transfers between devices  40.2 us (32%)
  local copies, waits for them, and re-layouts  12.8 us (10%)
  Pallas kernels  6.99 us (6%)
  other arithmetic  6.84 us (5%)
  matrix products  3.43 us (3%)
    all_to_all x1, waiting for transfers between devices, on_device(): got = lax.all_to_all(send, 'expert', 0, 0, tiled=True)  28.6 us
    all_to_all x1, starting transfers between devices, on_device(): got = lax.all_to_all(send, 'expert', 0, 0, tiled=True)  17.3 us
    ppermute x1, waiting for transfers between devices, reduce_over_dp(): lax.ppermute(jnp.concatenate([quarter(n - 1), across[:, half:]], axis=1),...  14.2 us
    all_to_all x1, starting transfers between devices, on_device(): lax.all_to_all(ret, 'expert', 0, 0, tiled=True).reshape(-1, feature_width)  8.78 us
    pallas_call x1, Pallas kernels, arm_math(): pl.pallas_call(arm_kernel, grid=(rows // block,), in_specs=[row_spec, row...  6.99 us
    ppermute x1, waiting for transfers between devices, reduce_over_dp(): far_first = lax.ppermute(from_left[:, rows:], 'dp', right)  6.37 us
    ppermute x1, waiting for transfers between devices, reduce_over_dp(): far_second = lax.ppermute(from_right[:, rows:], 'dp', left)  5.71 us
    ppermute x1, starting transfers between devices, reduce_over_dp(): far_second = lax.ppermute(from_right[:, rows:], 'dp', left)  5.6 us
  transfers between devices with their start and end apart: 6, of which 4 were waited for; matrix products, arithmetic and copies ran while one was open for 6% of the time, Pallas kernels for 0%

profile of v9, /device:TPU:24, one launch (start us, length us, event | category | flops | bytes accessed | tf_op | source)
XLA Modules:
  0.0 126.0 jit_solution(14612200628382044600)
XLA Ops:
  0.6 0.8 copy.12
  1.4 0.1 eq.34
  1.6 0.1 reshape.52
  1.7 0.1 copy.14
  1.8 0.2 fusion.19
  2.1 0.2 fusion.21
  2.3 0.2 slice.72
  2.5 0.2 slice.71
  2.8 0.2 slice.70
  3.0 0.2 slice.69
  3.2 0.9 fusion.14
  4.2 2.7 %fusion.3 = bf16[128,8,512]{2,1,0:T(8,128)(2,1)} fusion(s32[512]{0:T(512)S(1)} %pad_add_fusion, bf16[128,512]{1,0:T(8,128)(2,1)S(1)} %get-tuple-element.35, bf16[128,512]{1,0:T(8,128)(2,1)S(1)} %get-tuple-element.34, bf16[128,512]{1,0:T(8,128)(2,1)} %param.6), kind=kOutput, calls=%fused_computation.5 | convolution fusion | flops 540016640 | bytes 1443840 | tf_op jit(solution)/shard_map/dot_general | solution.py:205
  6.9 17.3 %all-to-all-start = ((bf16[128,8,512]{2,1,0:T(8,128)(2,1)}), bf16[128,8,512]{2,1,0:T(8,128)(2,1)S(1)}, u32[]{:S(2)}, u32[]{:S(2)}) async-start(bf16[128,8,512]{2,1,0:T(8,128)(2,1)} %fusion.3), calls=%async_computation | async-start | bytes 2097152 | tf_op jit(solution)/shard_map/all_to_all | solution.py:209
  24.2 28.6 %all-to-all-done = bf16[128,8,512]{2,1,0:T(8,128)(2,1)S(1)} async-done(((bf16[128,8,512]{2,1,0:T(8,128)(2,1)}), bf16[128,8,512]{2,1,0:T(8,128)(2,1)S(1)}, u32[]{:S(2)}, u32[]{:S(2)}) %all-to-all-start) | async-done | bytes 1048608 | tf_op jit(solution)/shard_map/all_to_all | solution.py:209
  52.8 0.3 fusion.25
  53.2 0.0 copy-start
  53.2 0.1 squeeze_reshape.6.tok_ref
  53.3 0.1 squeeze_reshape.7.cot_ref
  53.4 1.0 copy-done
  54.4 0.0 copy-start.1
  54.4 1.2 copy-done.1
  55.6 0.0 copy-start.2
  55.6 1.2 copy-done.2
  56.8 7.0 %shard_map.101 = (bf16[512,512]{1,0:T(8,128)(2,1)S(1)}, bf16[512,512]{1,0:T(8,128)(2,1)S(1)}, bf16[3,512,1024]{2,1,0:T(8,128)(2,1)}) custom-call(bf16[512,512]{1,0:T(8,128)(2,1)S(1)} %squeeze_reshape.6.tok_ref, bf16[512,512]{1,0:T(8,128)(2,1)S(1)} %squeeze_reshape.7.cot_ref, bf16[512,1024]{1,0:T(8,128)(2,1)S(1)} %bitcast.27, bf16[512,1024]{1,0:T(8,128)(2,1)S(1)} %bitcast.28, ...), custom_call_target="tpu_custom_call" | custom-call | flops 4831838208 | bytes 8388608 | tf_op jit(solution)/shard_map/pallas_call | solution.py:128
  63.8 0.1 reshape.56
  63.9 0.1 reshape.55
  64.1 1.2 constant_dynamic-slice_fusion
  65.3 1.5 %constant_dynamic-slice_fusion.3 = (bf16[3,512,256]{2,1,0:T(8,128)(2,1)S(1)}, bf16[3,512,256]{2,1,0:T(8,128)(2,1)S(1)}) fusion(bf16[3,512,1024]{2,1,0:T(8,128)(2,1)} %get-tuple-element.10, s32[]{:T(128)S(6)} %select_n.13, s32[]{:T(128)S(6)} %select_n.15), kind=kLoop, calls=%fused_computation.43 | loop fusion | bytes 3145736 | tf_op jit(solution)/shard_map/dynamic_slice | solution.py:166
  66.8 1.1 pad_maximum_fusion.1
  67.9 4.7 %collective-permute-start.1 = (bf16[3,768,256]{2,1,0:T(8,128)(2,1)}, bf16[3,768,256]{2,1,0:T(8,128)(2,1)}, u32[]{:S(2)}, u32[]{:S(2)}) collective-permute-start(bf16[3,768,256]{2,1,0:T(8,128)(2,1)} %pad_maximum_fusion.1), channel_id=1, source_target_pairs={{0,384},{128,0},{256,128},{384,256},{1,385},{129,1},{257,129},{385... | collective-permute-start | bytes 3538952 | tf_op jit(solution)/shard_map/ppermute | solution.py:172
  72.5 0.1 pad_maximum_fusion
  72.6 1.9 %collective-permute-start = (bf16[3,768,256]{2,1,0:T(8,128)(2,1)S(1)}, bf16[3,768,256]{2,1,0:T(8,128)(2,1)}, u32[]{:S(2)}, u32[]{:S(2)}) collective-permute-start(bf16[3,768,256]{2,1,0:T(8,128)(2,1)S(1)} %pad_maximum_fusion), channel_id=1, source_target_pairs={{0,128},{128,256},{256,384},{384,0},{1,129},{129,257},{257,385},{3... | collective-permute-start | bytes 3538952 | tf_op jit(solution)/shard_map/ppermute | solution.py:171
  74.6 1.5 %pad_maximum_fusion.2 = bf16[128,8,512]{2,1,0:T(8,128)(2,1)} fusion(bf16[128,4,512]{2,1,0:T(4,128)(2,1)S(1)} %reshape.56, bf16[128,4,512]{2,1,0:T(4,128)(2,1)S(1)} %reshape.55), kind=kLoop, calls=%fused_computation.8 | loop fusion | flops 2097152 | bytes 2097152 | tf_op jit(solution)/shard_map/concatenate | solution.py:216
  76.0 8.8 %all-to-all-start.1 = ((bf16[128,8,512]{2,1,0:T(8,128)(2,1)}), bf16[128,8,512]{2,1,0:T(8,128)(2,1)S(1)}, u32[]{:S(2)}, u32[]{:S(2)}) async-start(bf16[128,8,512]{2,1,0:T(8,128)(2,1)} %pad_maximum_fusion.2), calls=%async_computation.1 | async-start | bytes 2097152 | tf_op jit(solution)/shard_map/all_to_all | solution.py:223
  84.8 14.2 %collective-permute-done.1 = bf16[3,768,256]{2,1,0:T(8,128)(2,1)} collective-permute-done((bf16[3,768,256]{2,1,0:T(8,128)(2,1)}, bf16[3,768,256]{2,1,0:T(8,128)(2,1)}, u32[]{:S(2)}, u32[]{:S(2)}) %collective-permute-start.1) | collective-permute-done | bytes 1179680 | tf_op jit(solution)/shard_map/ppermute | solution.py:172
  99.0 1.0 slice.98
  100.1 5.6 %collective-permute-start.3 = (bf16[3,256,256]{2,1,0:T(8,128)(2,1)S(1)}, bf16[3,256,256]{2,1,0:T(8,128)(2,1)S(1)}, u32[]{:S(2)}, u32[]{:S(2)}) collective-permute-start(bf16[3,256,256]{2,1,0:T(8,128)(2,1)S(1)} %slice.98), channel_id=1, source_target_pairs={{0,384},{128,0},{256,128},{384,256},{1,385},{129,1},{257,129},{385... | collective-permute-start | bytes 1179656 | tf_op jit(solution)/shard_map/ppermute | solution.py:174
  105.7 0.0 collective-permute-done
  105.7 1.0 slice.97
  106.7 1.9 %collective-permute-start.2 = (bf16[3,256,256]{2,1,0:T(8,128)(2,1)S(1)}, bf16[3,256,256]{2,1,0:T(8,128)(2,1)S(1)}, u32[]{:S(2)}, u32[]{:S(2)}) collective-permute-start(bf16[3,256,256]{2,1,0:T(8,128)(2,1)S(1)} %slice.97), channel_id=1, source_target_pairs={{0,128},{128,256},{256,384},{384,0},{1,129},{129,257},{257,385},{3... | collective-permute-start | bytes 1179656 | tf_op jit(solution)/shard_map/ppermute | solution.py:173
  108.6 5.7 %collective-permute-done.3 = bf16[3,256,256]{2,1,0:T(8,128)(2,1)S(1)} collective-permute-done((bf16[3,256,256]{2,1,0:T(8,128)(2,1)S(1)}, bf16[3,256,256]{2,1,0:T(8,128)(2,1)S(1)}, u32[]{:S(2)}, u32[]{:S(2)}) %collective-permute-start.3) | collective-permute-done | bytes 393248 | tf_op jit(solution)/shard_map/ppermute | solution.py:174
  114.4 6.4 %collective-permute-done.2 = bf16[3,256,256]{2,1,0:T(8,128)(2,1)S(1)} collective-permute-done((bf16[3,256,256]{2,1,0:T(8,128)(2,1)S(1)}, bf16[3,256,256]{2,1,0:T(8,128)(2,1)S(1)}, u32[]{:S(2)}, u32[]{:S(2)}) %collective-permute-start.2) | collective-permute-done | bytes 393248 | tf_op jit(solution)/shard_map/ppermute | solution.py:173
  120.7 2.0 %add_convert_fusion = bf16[3,512,256]{2,1,0:T(8,128)(2,1)S(1)} fusion(bf16[3,768,256]{2,1,0:T(8,128)(2,1)} %collective-permute-done.1, bf16[3,768,256]{2,1,0:T(8,128)(2,1)} %collective-permute-done, bf16[3,256,256]{2,1,0:T(8,128)(2,1)S(1)} %collective-permute-done.3, bf16[3,256,256]{2,1,0:T(8,128)(2,1)S(1)} %collective-permute-done.2, ...), kind=kLoop, calls=%fused_computation.3 | loop fusion | flops 4325376 | bytes 3932164 | tf_op jit(solution)/shard_map/convert_element_type | solution.py:181
  122.7 0.8 slice_bitcast_fusion
  123.6 0.8 copy.16
  124.4 0.0 all-to-all-done.1
  124.4 0.8 fusion
  125.2 0.8 fusion.16
  (8 shorter events, 0.1 us)
Async XLA Ops:
  6.9 45.9 %all-to-all-start = ((bf16[128,8,512]{2,1,0:T(8,128)(2,1)}), bf16[128,8,512]{2,1,0:T(8,128)(2,1)S(1)}, u32[]{:S(2)}, u32[]{:S(2)}) async-start(bf16[128,8,512]{2,1,0:T(8,128)(2,1)} %fusion.3), calls=%async_computation | async-start | bytes 2097152 | tf_op jit(solution)/shard_map/all_to_all | solution.py:209
  53.2 1.2 copy-start
  54.4 1.2 copy-start.1
  55.6 1.2 copy-start.2
  67.9 31.2 %collective-permute-start.1 = (bf16[3,768,256]{2,1,0:T(8,128)(2,1)}, bf16[3,768,256]{2,1,0:T(8,128)(2,1)}, u32[]{:S(2)}, u32[]{:S(2)}) collective-permute-start(bf16[3,768,256]{2,1,0:T(8,128)(2,1)} %pad_maximum_fusion.1), channel_id=1, source_target_pairs={{0,384},{128,0},{256,128},{384,256},{1,385},{129,1},{257,129},{385... | collective-permute-start | bytes 3538952 | tf_op jit(solution)/shard_map/ppermute | solution.py:172
  72.6 33.0 %collective-permute-start = (bf16[3,768,256]{2,1,0:T(8,128)(2,1)S(1)}, bf16[3,768,256]{2,1,0:T(8,128)(2,1)}, u32[]{:S(2)}, u32[]{:S(2)}) collective-permute-start(bf16[3,768,256]{2,1,0:T(8,128)(2,1)S(1)} %pad_maximum_fusion), channel_id=1, source_target_pairs={{0,128},{128,256},{256,384},{384,0},{1,129},{129,257},{257,385},{3... | collective-permute-start | bytes 3538952 | tf_op jit(solution)/shard_map/ppermute | solution.py:171
  76.0 48.4 %all-to-all-start.1 = ((bf16[128,8,512]{2,1,0:T(8,128)(2,1)}), bf16[128,8,512]{2,1,0:T(8,128)(2,1)S(1)}, u32[]{:S(2)}, u32[]{:S(2)}) async-start(bf16[128,8,512]{2,1,0:T(8,128)(2,1)} %pad_maximum_fusion.2), calls=%async_computation.1 | async-start | bytes 2097152 | tf_op jit(solution)/shard_map/all_to_all | solution.py:223
  100.1 14.3 %collective-permute-start.3 = (bf16[3,256,256]{2,1,0:T(8,128)(2,1)S(1)}, bf16[3,256,256]{2,1,0:T(8,128)(2,1)S(1)}, u32[]{:S(2)}, u32[]{:S(2)}) collective-permute-start(bf16[3,256,256]{2,1,0:T(8,128)(2,1)S(1)} %slice.98), channel_id=1, source_target_pairs={{0,384},{128,0},{256,128},{384,256},{1,385},{129,1},{257,129},{385... | collective-permute-start | bytes 1179656 | tf_op jit(solution)/shard_map/ppermute | solution.py:174
  106.7 14.0 %collective-permute-start.2 = (bf16[3,256,256]{2,1,0:T(8,128)(2,1)S(1)}, bf16[3,256,256]{2,1,0:T(8,128)(2,1)S(1)}, u32[]{:S(2)}, u32[]{:S(2)}) collective-permute-start(bf16[3,256,256]{2,1,0:T(8,128)(2,1)S(1)} %slice.97), channel_id=1, source_target_pairs={{0,128},{128,256},{256,384},{384,0},{1,129},{129,257},{257,385},{3... | collective-permute-start | bytes 1179656 | tf_op jit(solution)/shard_map/ppermute | solution.py:173

commit v10 on v8

--- a/solution.py
+++ b/solution.py
@@ -83,15 +83,13 @@
     return lax.dot_general(a, b, (((1,), (1,)), ((), ())), preferred_element_type=jnp.float32)
 
 
-def arm_kernel(tok_ref, cot_ref, wg_ref, wu_ref, wd_ref, out_ref, inp_ref, part_ref, acc_g, acc_u, acc_d):
+def arm_kernel(tok_ref, cot_ref, wg_ref, wu_ref, wd_ref, out_ref, inp_ref, part_ref, acc_out, acc_inp):
     step = pl.program_id(0)
-    hidden_width = wg_ref.shape[1]
 
     @pl.when(step == 0)
     def _():
-        acc_g[...] = jnp.zeros_like(acc_g)
-        acc_u[...] = jnp.zeros_like(acc_u)
-        acc_d[...] = jnp.zeros_like(acc_d)
+        acc_out[...] = jnp.zeros_like(acc_out)
+        acc_inp[...] = jnp.zeros_like(acc_inp)
 
     x = tok_ref[...]
     c = cot_ref[...]
@@ -102,47 +100,46 @@
     up_pre = jnp.dot(x, wu, preferred_element_type=jnp.float32)
     activated, silu_slope = silu_parts(gate_pre)
     hidden = (activated * up_pre).astype(jnp.bfloat16)
-    out_ref[...] = jnp.dot(hidden, wd, preferred_element_type=jnp.float32).astype(out_ref.dtype)
+    acc_out[...] += jnp.dot(hidden, wd, preferred_element_type=jnp.float32)
     d_hidden = contract_cols(c, wd)
     d_up = (d_hidden * activated).astype(jnp.bfloat16)
     d_gate = (d_hidden * up_pre * silu_slope).astype(jnp.bfloat16)
-    inp_ref[...] = (contract_cols(d_gate, wg) + contract_cols(d_up, wu)).astype(inp_ref.dtype)
-    acc_g[...] += contract_rows(x, d_gate)
-    acc_u[...] += contract_rows(x, d_up)
-    acc_d[...] += contract_rows(c, hidden)
+    acc_inp[...] += contract_cols(d_gate, wg) + contract_cols(d_up, wu)
+    part_ref[0] = contract_rows(x, d_gate).astype(part_ref.dtype)
+    part_ref[1] = contract_rows(x, d_up).astype(part_ref.dtype)
+    part_ref[2] = contract_rows(c, hidden).astype(part_ref.dtype)
 
     @pl.when(step == pl.num_programs(0) - 1)
     def _():
-        part_ref[0] = acc_g[...].astype(part_ref.dtype)
-        part_ref[1] = acc_u[...].astype(part_ref.dtype)
-        part_ref[2] = acc_d[...].astype(part_ref.dtype)
+        out_ref[...] = acc_out[...].astype(out_ref.dtype)
+        inp_ref[...] = acc_inp[...].astype(inp_ref.dtype)
 
 
 def arm_math(tokens, cot, wg, wu, wd):
     rows, width = tokens.shape
     hidden_width = wg.shape[1]
-    block = 512
-    row_spec = pl.BlockSpec((block, width), lambda i: (i, 0))
-    whole = lambda shape: pl.BlockSpec(shape, lambda i: (0, 0))
+    chunk = 256
+    rows_spec = pl.BlockSpec((rows, width), lambda j: (0, 0))
     flops = 2 * rows * width * hidden_width * 9
     return pl.pallas_call(
         arm_kernel,
-        grid=(rows // block,),
-        in_specs=[row_spec, row_spec, whole(wg.shape), whole(wu.shape), whole(wd.shape)],
-        out_specs=[
-            row_spec,
-            row_spec,
-            pl.BlockSpec((3, width, hidden_width), lambda i: (0, 0, 0)),
-        ],
+        grid=(hidden_width // chunk,),
+        in_specs=[
+            rows_spec,
+            rows_spec,
+            pl.BlockSpec((width, chunk), lambda j: (0, j)),
+            pl.BlockSpec((width, chunk), lambda j: (0, j)),
+            pl.BlockSpec((chunk, width), lambda j: (j, 0)),
+        ],
+        out_specs=[rows_spec, rows_spec, pl.BlockSpec((3, width, chunk), lambda j: (0, 0, j))],
         out_shape=[
             jax.ShapeDtypeStruct((rows, width), jnp.bfloat16),
             jax.ShapeDtypeStruct((rows, width), jnp.bfloat16),
             jax.ShapeDtypeStruct((3, width, hidden_width), jnp.bfloat16),
         ],
         scratch_shapes=[
-            pltpu.VMEM((width, hidden_width), jnp.float32),
-            pltpu.VMEM((width, hidden_width), jnp.float32),
-            pltpu.VMEM((width, hidden_width), jnp.float32),
+            pltpu.VMEM((rows, width), jnp.float32),
+            pltpu.VMEM((rows, width), jnp.float32),
         ],
         compiler_params=pltpu.CompilerParams(
             dimension_semantics=("arbitrary",), vmem_limit_bytes=48 * 1024 * 1024
@@ -151,7 +148,6 @@
             flops=flops, bytes_accessed=2 * (4 * rows * width + 6 * width * hidden_width), transcendentals=rows * hidden_width
         ),
     )(tokens, cot, wg, wu, wd)
-
 
 def on_device(tokens, codes, cotangent, w_gate, w_up, w_down):
     token_count, feature_width = tokens.shape

time: 121 us -> 123 us (1.017)
  Pallas kernels: 7.01 us -> 8.28 us
    pallas_call x1, Pallas kernels: 7.01 us -> 8.28 us  [arm_math(): pl.pallas_call(arm_kernel, grid=(hidden_width // chunk,), in_specs=[rows_...]
where the time goes in v10:
time: 123 us; the launch traced here: 122 us
  blocking collectives  85.8 us (70%)
  between operations  14.1 us (11%)
  local copies, waits for them, and re-layouts  8.8 us (7%)
  Pallas kernels  8.28 us (7%)
  other arithmetic  2.71 us (2%)
  matrix products  2.45 us (2%)
    all_to_all x1, blocking collectives, on_device(): got = lax.all_to_all(send, 'expert', 0, 0, tiled=True)  48.7 us
    all_to_all x1, blocking collectives, on_device(): lax.all_to_all(ret, 'expert', 0, 0, tiled=True).reshape(-1, feature_width)  37.2 us
    pallas_call x1, Pallas kernels, arm_math(): pl.pallas_call(arm_kernel, grid=(hidden_width // chunk,), in_specs=[rows_...  8.28 us
    unnamed x9, local copies, waits for them, and re-layouts  4.7 us
  transfers between devices with their start and end apart: 1, of which 0 were waited for; matrix products, arithmetic and copies ran while one was open for 2% of the time, Pallas kernels for 0%

profile of v10, /device:TPU:1, one launch (start us, length us, event | category | flops | bytes accessed | tf_op | source)
XLA Modules:
  0.0 122.3 jit_solution(13095315797481375073)
XLA Ops:
  7.2 0.0 reduce-scatter.2.cloned.1.call-start
  7.2 0.8 copy.12
  8.0 0.1 reshape.52
  8.1 0.1 eq.34
  8.3 0.1 copy.14
  8.4 0.2 fusion.19
  8.7 0.2 fusion.21
  8.9 0.2 slice.54
  9.1 0.2 slice.53
  9.3 0.2 slice.52
  9.6 0.2 slice.51
  9.8 0.9 fusion.14
  10.8 1.7 %fusion.3 = bf16[128,8,512]{2,1,0:T(8,128)(2,1)S(1)} fusion(s32[512]{0:T(512)S(1)} %pad_add_fusion, bf16[128,512]{1,0:T(8,128)(2,1)S(1)} %get-tuple-element.31, bf16[128,512]{1,0:T(8,128)(2,1)S(1)} %get-tuple-element.30, bf16[128,512]{1,0:T(8,128)(2,1)} %param.6), kind=kOutput, calls=%fused_computation.4 | convolution fusion | flops 540016640 | bytes 1443840 | tf_op jit(solution)/shard_map/dot_general | solution.py:173
  12.5 48.7 %all_to_all.10 = bf16[128,8,512]{2,1,0:T(8,128)(2,1)S(1)} all-to-all(bf16[128,8,512]{2,1,0:T(8,128)(2,1)S(1)} %fusion.3), channel_id=1, replica_groups=mesh['dp'=4,'expert'=128] {'expert'}, dimensions={0} | all-to-all | bytes 2097152 | tf_op jit(solution)/shard_map/all_to_all | solution.py:177
  61.1 0.0 copy-start
  61.1 0.3 fusion.25
  61.5 0.1 squeeze_reshape.7.cot_ref
  61.6 0.1 squeeze_reshape.6.tok_ref
  61.7 0.6 copy-done
  62.4 0.0 copy-start.1
  62.4 1.2 %copy-done.1 = bf16[1,512,1024]{2,1,0:T(8,128)(2,1)S(1)} copy-done((bf16[1,512,1024]{2,1,0:T(8,128)(2,1)S(1)}, bf16[1,512,1024]{2,1,0:T(8,128)(2,1)}, u32[]{:S(2)}) %copy-start.1) | copy-done | bytes 1048600
  63.6 0.0 copy-start.2
  63.6 1.2 %copy-done.2 = bf16[1,1024,512]{2,1,0:T(8,128)(2,1)S(1)} copy-done((bf16[1,1024,512]{2,1,0:T(8,128)(2,1)S(1)}, bf16[1,1024,512]{2,1,0:T(8,128)(2,1)}, u32[]{:S(2)}) %copy-start.2) | copy-done | bytes 1048600
  64.8 8.3 %shard_map.101 = (bf16[512,512]{1,0:T(8,128)(2,1)S(1)}, bf16[512,512]{1,0:T(8,128)(2,1)S(1)}, bf16[3,512,1024]{2,1,0:T(8,128)(2,1)}) custom-call(bf16[512,512]{1,0:T(8,128)(2,1)S(1)} %squeeze_reshape.6.tok_ref, bf16[512,512]{1,0:T(8,128)(2,1)S(1)} %squeeze_reshape.7.cot_ref, bf16[512,1024]{1,0:T(8,128)(2,1)S(1)} %bitcast.27, bf16[512,1024]{1,0:T(8,128)(2,1)S(1)} %bitcast.28, ...), custom_call_target="tpu_custom_call" | custom-call | flops 4831838208 | bytes 8388608 | tf_op jit(solution)/shard_map/pallas_call | solution.py:124
  73.1 0.0 reduce-scatter.2.cloned.1.call-update
  73.1 0.1 reshape.55
  73.2 0.1 reshape.56
  73.4 0.5 pad_maximum_fusion
  73.9 37.2 %all_to_all.11 = bf16[128,8,512]{2,1,0:T(8,128)(2,1)S(1)} all-to-all(bf16[128,8,512]{2,1,0:T(8,128)(2,1)S(1)} %pad_maximum_fusion), channel_id=1, replica_groups=mesh['dp'=4,'expert'=128] {'expert'}, dimensions={0} | all-to-all | bytes 2097152 | tf_op jit(solution)/shard_map/all_to_all | solution.py:191
  111.1 0.8 fusion
  111.8 0.8 fusion.16
  112.6 0.0 reduce-scatter.2.cloned.1.call-done
  112.6 1.9 %slice_bitcast_fusion = (bf16[1,256,512]{1,2,0:T(8,128)(2,1)S(1)}, bf16[1,512,256]{2,1,0:T(8,128)(2,1)}, bf16[1,512,256]{2,1,0:T(8,128)(2,1)}) fusion(bf16[3,512,256]{2,1,0:T(8,128)(2,1)} %reduce-scatter.2.cloned.1.call-done), kind=kLoop, calls=%fused_computation.20 | loop fusion | bytes 1572864 | tf_op jit(solution)/shard_map/broadcast_in_dim | solution.py:201
  114.6 0.8 copy.16
  (8 shorter events, 0.1 us)
Async XLA Ops:
  7.2 105.5 %reduce-scatter.2.cloned.1.call-start = ((), (), s32[]{:S(2)}) async-start(), calls=%async_computation.3 | async-start | bytes 3932160 | tf_op jit(solution)/shard_map/reduce_scatter | solution.py:198
  61.1 1.2 %copy-start = (bf16[1,512,1024]{2,1,0:T(8,128)(2,1)S(1)}, bf16[1,512,1024]{2,1,0:T(8,128)(2,1)}, u32[]{:S(2)}) copy-start(bf16[1,512,1024]{2,1,0:T(8,128)(2,1)} %param.9) | copy-start | bytes 3145732
  62.4 1.2 %copy-start.1 = (bf16[1,512,1024]{2,1,0:T(8,128)(2,1)S(1)}, bf16[1,512,1024]{2,1,0:T(8,128)(2,1)}, u32[]{:S(2)}) copy-start(bf16[1,512,1024]{2,1,0:T(8,128)(2,1)} %param.10) | copy-start | bytes 3145732
  63.6 1.2 %copy-start.2 = (bf16[1,1024,512]{2,1,0:T(8,128)(2,1)S(1)}, bf16[1,1024,512]{2,1,0:T(8,128)(2,1)}, u32[]{:S(2)}) copy-start(bf16[1,1024,512]{2,1,0:T(8,128)(2,1)} %param.11) | copy-start | bytes 3145732
Sparse Core Ops, SparseCore 0:
  73.2 37.5 reduce-scatter.1

commit v11 on v8

--- a/solution.py
+++ b/solution.py
@@ -153,6 +153,27 @@
     )(tokens, cot, wg, wu, wd)
 
 
+def split_kernel(summed_ref, gate_ref, up_ref, down_ref):
+    gate_ref[...] = summed_ref[0]
+    up_ref[...] = summed_ref[1]
+    down_ref[...] = summed_ref[2].astype(jnp.float32).T.astype(down_ref.dtype)
+
+
+def split_grads(summed):
+    _, width, part = summed.shape
+    vmem = pl.BlockSpec(memory_space=pltpu.VMEM)
+    return pl.pallas_call(
+        split_kernel,
+        in_specs=[vmem],
+        out_specs=[vmem, vmem, vmem],
+        out_shape=[
+            jax.ShapeDtypeStruct((width, part), summed.dtype),
+            jax.ShapeDtypeStruct((width, part), summed.dtype),
+            jax.ShapeDtypeStruct((part, width), summed.dtype),
+        ],
+    )(summed)
+
+
 def on_device(tokens, codes, cotangent, w_gate, w_up, w_down):
     token_count, feature_width = tokens.shape
     local_arms = w_gate.shape[0]
@@ -200,9 +221,7 @@
     grad_tokens = (picked[2] + picked[3]).astype(jnp.bfloat16)
 
     summed = lax.psum_scatter(partials, "dp", scatter_dimension=2, tiled=True)
-    grad_gate = summed[0:1]
-    grad_up = summed[1:2]
-    grad_down = summed[2].T[None]
+    grad_gate, grad_up, grad_down = (g[None] for g in split_grads(summed))
     return (head_output, grad_tokens, grad_gate, grad_up, grad_down)
 
 

time: 121 us -> 121 us (level)
  local copies, waits for them, and re-layouts: 8.8 us -> 6.01 us
  Pallas kernels: 7.01 us -> 9.1 us
    pallas_call x0 -> x1, Pallas kernels: none -> 2.08 us  [split_grads(): pl.pallas_call(split_kernel, in_specs=[vmem], out_specs=[vmem, vmem, vmem...]
    broadcast_in_dim x1 -> x0, local copies, waits for them, and re-layouts: 1.95 us -> none  [on_device(): grad_down = summed[2].T[None]]
    unnamed x9 -> x8, local copies, waits for them, and re-layouts: 4.7 us -> 3.86 us
where the time goes in v11:
time: 121 us; the launch traced here: 120 us
  blocking collectives  85.8 us (71%)
  between operations  14.1 us (12%)
  Pallas kernels  9.1 us (8%)
  local copies, waits for them, and re-layouts  6.01 us (5%)
  other arithmetic  2.71 us (2%)
  matrix products  2.45 us (2%)
    all_to_all x1, blocking collectives, on_device(): got = lax.all_to_all(send, 'expert', 0, 0, tiled=True)  48.7 us
    all_to_all x1, blocking collectives, on_device(): lax.all_to_all(ret, 'expert', 0, 0, tiled=True).reshape(-1, feature_width)  37.2 us
    pallas_call x1, Pallas kernels, arm_math(): pl.pallas_call(arm_kernel, grid=(rows // block,), in_specs=[row_spec, row...  7.01 us
    unnamed x8, local copies, waits for them, and re-layouts  3.86 us
  transfers between devices with their start and end apart: 1, of which 0 were waited for; matrix products, arithmetic and copies ran while one was open for 2% of the time, Pallas kernels for 0%

profile of v11, /device:TPU:1, one launch (start us, length us, event | category | flops | bytes accessed | tf_op | source)
XLA Modules:
  0.0 120.3 jit_solution(14403913718701797727)
XLA Ops:
  7.2 0.0 reduce-scatter.2.cloned.1.call-start
  7.2 0.8 copy.11
  8.0 0.1 reshape.52
  8.1 0.1 eq.34
  8.3 0.1 copy.13
  8.4 0.2 fusion.19
  8.7 0.2 fusion.21
  8.9 0.2 slice.45
  9.1 0.2 slice.44
  9.3 0.2 slice.43
  9.6 0.2 slice.42
  9.8 0.9 fusion.14
  10.8 1.7 %fusion.3 = bf16[128,8,512]{2,1,0:T(8,128)(2,1)S(1)} fusion(s32[512]{0:T(512)S(1)} %pad_add_fusion, bf16[128,512]{1,0:T(8,128)(2,1)S(1)} %get-tuple-element.24, bf16[128,512]{1,0:T(8,128)(2,1)S(1)} %get-tuple-element.23, bf16[128,512]{1,0:T(8,128)(2,1)} %param.6), kind=kOutput, calls=%fused_computation.4 | convolution fusion | flops 540016640 | bytes 1443840 | tf_op jit(solution)/shard_map/dot_general | solution.py:198
  12.5 48.7 %all_to_all.10 = bf16[128,8,512]{2,1,0:T(8,128)(2,1)S(1)} all-to-all(bf16[128,8,512]{2,1,0:T(8,128)(2,1)S(1)} %fusion.3), channel_id=1, replica_groups=mesh['dp'=4,'expert'=128] {'expert'}, dimensions={0} | all-to-all | bytes 2097152 | tf_op jit(solution)/shard_map/all_to_all | solution.py:202
  61.1 0.0 copy-start
  61.1 0.3 fusion.25
  61.5 0.1 squeeze_reshape.7.cot_ref
  61.6 0.1 squeeze_reshape.6.tok_ref
  61.7 0.6 copy-done
  62.4 0.0 copy-start.1
  62.4 1.2 %copy-done.1 = bf16[1,512,1024]{2,1,0:T(8,128)(2,1)S(1)} copy-done((bf16[1,512,1024]{2,1,0:T(8,128)(2,1)S(1)}, bf16[1,512,1024]{2,1,0:T(8,128)(2,1)}, u32[]{:S(2)}) %copy-start.1) | copy-done | bytes 1048600
  63.6 0.0 copy-start.2
  63.6 1.2 %copy-done.2 = bf16[1,1024,512]{2,1,0:T(8,128)(2,1)S(1)} copy-done((bf16[1,1024,512]{2,1,0:T(8,128)(2,1)S(1)}, bf16[1,1024,512]{2,1,0:T(8,128)(2,1)}, u32[]{:S(2)}) %copy-start.2) | copy-done | bytes 1048600
  64.8 7.0 %shard_map.101 = (bf16[512,512]{1,0:T(8,128)(2,1)S(1)}, bf16[512,512]{1,0:T(8,128)(2,1)S(1)}, bf16[3,512,1024]{2,1,0:T(8,128)(2,1)}) custom-call(bf16[512,512]{1,0:T(8,128)(2,1)S(1)} %squeeze_reshape.6.tok_ref, bf16[512,512]{1,0:T(8,128)(2,1)S(1)} %squeeze_reshape.7.cot_ref, bf16[512,1024]{1,0:T(8,128)(2,1)S(1)} %bitcast.24, bf16[512,1024]{1,0:T(8,128)(2,1)S(1)} %bitcast.25, ...), custom_call_target="tpu_custom_call" | custom-call | flops 4831838208 | bytes 8388608 | tf_op jit(solution)/shard_map/pallas_call | solution.py:128
  71.8 0.0 reduce-scatter.2.cloned.1.call-update
  71.8 0.1 reshape.55
  72.0 0.1 reshape.56
  72.1 0.5 pad_maximum_fusion
  72.6 37.2 %all_to_all.11 = bf16[128,8,512]{2,1,0:T(8,128)(2,1)S(1)} all-to-all(bf16[128,8,512]{2,1,0:T(8,128)(2,1)S(1)} %pad_maximum_fusion), channel_id=1, replica_groups=mesh['dp'=4,'expert'=128] {'expert'}, dimensions={0} | all-to-all | bytes 2097152 | tf_op jit(solution)/shard_map/all_to_all | solution.py:216
  109.8 0.8 fusion
  110.6 0.8 fusion.16
  111.3 0.0 reduce-scatter.2.cloned.1.call-done.summed_ref
  111.3 2.1 %shard_map.102 = (bf16[512,256]{1,0:T(8,128)(2,1)}, bf16[512,256]{1,0:T(8,128)(2,1)}, bf16[256,512]{1,0:T(8,128)(2,1)}) custom-call(bf16[3,512,256]{2,1,0:T(8,128)(2,1)} %reduce-scatter.2.cloned.1.call-done.summed_ref), custom_call_target="tpu_custom_call" | custom-call | tf_op jit(solution)/shard_map/pallas_call | solution.py:165
  (8 shorter events, 0.1 us)
Async XLA Ops:
  7.2 104.2 %reduce-scatter.2.cloned.1.call-start = ((), (), s32[]{:S(2)}) async-start(), calls=%async_computation.3 | async-start | bytes 3932160 | tf_op jit(solution)/shard_map/reduce_scatter | solution.py:223
  61.1 1.2 %copy-start = (bf16[1,512,1024]{2,1,0:T(8,128)(2,1)S(1)}, bf16[1,512,1024]{2,1,0:T(8,128)(2,1)}, u32[]{:S(2)}) copy-start(bf16[1,512,1024]{2,1,0:T(8,128)(2,1)} %param.9) | copy-start | bytes 3145732
  62.4 1.2 %copy-start.1 = (bf16[1,512,1024]{2,1,0:T(8,128)(2,1)S(1)}, bf16[1,512,1024]{2,1,0:T(8,128)(2,1)}, u32[]{:S(2)}) copy-start(bf16[1,512,1024]{2,1,0:T(8,128)(2,1)} %param.10) | copy-start | bytes 3145732
  63.6 1.2 %copy-start.2 = (bf16[1,1024,512]{2,1,0:T(8,128)(2,1)S(1)}, bf16[1,1024,512]{2,1,0:T(8,128)(2,1)}, u32[]{:S(2)}) copy-start(bf16[1,1024,512]{2,1,0:T(8,128)(2,1)} %param.11) | copy-start | bytes 3145732
Sparse Core Ops, SparseCore 0:
  72.0 37.6 reduce-scatter.1

commit v12 on v11

--- a/solution.py
+++ b/solution.py
@@ -179,7 +179,7 @@
     local_arms = w_gate.shape[0]
     arm_count = local_arms * lax.axis_size("expert")
     capacity = 4 * token_count // arm_count
-    flat_codes = codes.reshape(-1)
+    flat_codes = codes.T.reshape(-1)
     arm_ids = jnp.arange(arm_count, dtype=jnp.int32)
     onehot = (flat_codes[:, None] == arm_ids[None, :]).astype(jnp.int32)
     earlier = jnp.cumsum(onehot, axis=0) - onehot
@@ -190,7 +190,7 @@
     sources = jnp.concatenate(
         [tokens, tokens, (cot_f * fact_share).astype(jnp.bfloat16), (cot_f * counter_share).astype(jnp.bfloat16)]
     )
-    dest = jnp.concatenate([tok_dest[0::2], tok_dest[1::2], cot_dest[0::2], cot_dest[1::2]])
+    dest = jnp.concatenate([tok_dest, cot_dest])
     place = (
         lax.broadcasted_iota(jnp.int32, (arm_count * 2 * capacity, dest.shape[0]), 0) == dest[None, :]
     ).astype(jnp.bfloat16)

time: 121 us -> 121 us (level)
  other arithmetic: 2.71 us -> 4.06 us
  local copies, waits for them, and re-layouts: 6.01 us -> 4.72 us
    unnamed x8 -> x7, local copies, waits for them, and re-layouts: 3.86 us -> 3.07 us
where the time goes in v12:
time: 121 us; the launch traced here: 120 us
  blocking collectives  85.8 us (71%)
  between operations  14.1 us (12%)
  Pallas kernels  9.1 us (8%)
  local copies, waits for them, and re-layouts  4.72 us (4%)
  other arithmetic  4.06 us (3%)
  matrix products  2.46 us (2%)
    all_to_all x1, blocking collectives, on_device(): got = lax.all_to_all(send, 'expert', 0, 0, tiled=True)  48.7 us
    all_to_all x1, blocking collectives, on_device(): lax.all_to_all(ret, 'expert', 0, 0, tiled=True).reshape(-1, feature_width)  37.2 us
    pallas_call x1, Pallas kernels, arm_math(): pl.pallas_call(arm_kernel, grid=(rows // block,), in_specs=[row_spec, row...  7.01 us
    unnamed x7, local copies, waits for them, and re-layouts  3.07 us
  transfers between devices with their start and end apart: 1, of which 0 were waited for; matrix products, arithmetic and copies ran while one was open for 2% of the time, Pallas kernels for 0%

profile of v12, /device:TPU:1, one launch (start us, length us, event | category | flops | bytes accessed | tf_op | source)
XLA Modules:
  0.0 120.3 jit_solution(5335547515405879594)
XLA Ops:
  7.2 0.0 reduce-scatter.2.cloned.1.call-start
  7.2 0.8 copy.12
  8.0 0.2 fusion.19
  8.3 0.9 fusion.21
  9.2 0.7 broadcast_add_fusion.1
  9.9 0.9 fusion.14
  10.8 1.7 %fusion.3 = bf16[128,8,512]{2,1,0:T(8,128)(2,1)S(1)} fusion(s32[512]{0:T(512)S(1)} %pad_add_fusion, bf16[128,512]{1,0:T(8,128)(2,1)S(1)} %get-tuple-element.24, bf16[128,512]{1,0:T(8,128)(2,1)S(1)} %get-tuple-element.23, bf16[128,512]{1,0:T(8,128)(2,1)} %param.6), kind=kOutput, calls=%fused_computation.4 | convolution fusion | flops 540016640 | bytes 1443840 | tf_op jit(solution)/shard_map/dot_general | solution.py:198
  12.5 48.7 %all_to_all.10 = bf16[128,8,512]{2,1,0:T(8,128)(2,1)S(1)} all-to-all(bf16[128,8,512]{2,1,0:T(8,128)(2,1)S(1)} %fusion.3), channel_id=1, replica_groups=mesh['dp'=4,'expert'=128] {'expert'}, dimensions={0} | all-to-all | bytes 2097152 | tf_op jit(solution)/shard_map/all_to_all | solution.py:202
  61.2 0.0 copy-start
  61.2 0.3 fusion.25
  61.5 0.1 squeeze_reshape.7.cot_ref
  61.6 0.1 squeeze_reshape.6.tok_ref
  61.8 0.6 copy-done
  62.4 0.0 copy-start.1
  62.4 1.2 %copy-done.1 = bf16[1,512,1024]{2,1,0:T(8,128)(2,1)S(1)} copy-done((bf16[1,512,1024]{2,1,0:T(8,128)(2,1)S(1)}, bf16[1,512,1024]{2,1,0:T(8,128)(2,1)}, u32[]{:S(2)}) %copy-start.1) | copy-done | bytes 1048600
  63.6 0.0 copy-start.2
  63.6 1.2 %copy-done.2 = bf16[1,1024,512]{2,1,0:T(8,128)(2,1)S(1)} copy-done((bf16[1,1024,512]{2,1,0:T(8,128)(2,1)S(1)}, bf16[1,1024,512]{2,1,0:T(8,128)(2,1)}, u32[]{:S(2)}) %copy-start.2) | copy-done | bytes 1048600
  64.8 7.0 %shard_map.101 = (bf16[512,512]{1,0:T(8,128)(2,1)S(1)}, bf16[512,512]{1,0:T(8,128)(2,1)S(1)}, bf16[3,512,1024]{2,1,0:T(8,128)(2,1)}) custom-call(bf16[512,512]{1,0:T(8,128)(2,1)S(1)} %squeeze_reshape.6.tok_ref, bf16[512,512]{1,0:T(8,128)(2,1)S(1)} %squeeze_reshape.7.cot_ref, bf16[512,1024]{1,0:T(8,128)(2,1)S(1)} %bitcast.29, bf16[512,1024]{1,0:T(8,128)(2,1)S(1)} %bitcast.30, ...), custom_call_target="tpu_custom_call" | custom-call | flops 4831838208 | bytes 8388608 | tf_op jit(solution)/shard_map/pallas_call | solution.py:128
  71.9 0.0 reduce-scatter.2.cloned.1.call-update
  71.9 0.1 reshape.55
  72.0 0.1 reshape.56
  72.1 0.5 pad_maximum_fusion
  72.7 37.2 %all_to_all.11 = bf16[128,8,512]{2,1,0:T(8,128)(2,1)S(1)} all-to-all(bf16[128,8,512]{2,1,0:T(8,128)(2,1)S(1)} %pad_maximum_fusion), channel_id=1, replica_groups=mesh['dp'=4,'expert'=128] {'expert'}, dimensions={0} | all-to-all | bytes 2097152 | tf_op jit(solution)/shard_map/all_to_all | solution.py:216
  109.8 0.8 fusion
  110.6 0.8 fusion.16
  111.4 0.0 reduce-scatter.2.cloned.1.call-done.summed_ref
  111.4 2.1 %shard_map.102 = (bf16[512,256]{1,0:T(8,128)(2,1)}, bf16[512,256]{1,0:T(8,128)(2,1)}, bf16[256,512]{1,0:T(8,128)(2,1)}) custom-call(bf16[3,512,256]{2,1,0:T(8,128)(2,1)} %reduce-scatter.2.cloned.1.call-done.summed_ref), custom_call_target="tpu_custom_call" | custom-call | tf_op jit(solution)/shard_map/pallas_call | solution.py:165
  (7 shorter events, 0.1 us)
Async XLA Ops:
  7.2 104.2 %reduce-scatter.2.cloned.1.call-start = ((), (), s32[]{:S(2)}) async-start(), calls=%async_computation.3 | async-start | bytes 3932160 | tf_op jit(solution)/shard_map/reduce_scatter | solution.py:223
  61.2 1.2 %copy-start = (bf16[1,512,1024]{2,1,0:T(8,128)(2,1)S(1)}, bf16[1,512,1024]{2,1,0:T(8,128)(2,1)}, u32[]{:S(2)}) copy-start(bf16[1,512,1024]{2,1,0:T(8,128)(2,1)} %param.9) | copy-start | bytes 3145732
  62.4 1.2 %copy-start.1 = (bf16[1,512,1024]{2,1,0:T(8,128)(2,1)S(1)}, bf16[1,512,1024]{2,1,0:T(8,128)(2,1)}, u32[]{:S(2)}) copy-start(bf16[1,512,1024]{2,1,0:T(8,128)(2,1)} %param.10) | copy-start | bytes 3145732
  63.6 1.2 %copy-start.2 = (bf16[1,1024,512]{2,1,0:T(8,128)(2,1)S(1)}, bf16[1,1024,512]{2,1,0:T(8,128)(2,1)}, u32[]{:S(2)}) copy-start(bf16[1,1024,512]{2,1,0:T(8,128)(2,1)} %param.11) | copy-start | bytes 3145732
Sparse Core Ops, SparseCore 0:
  72.0 37.6 reduce-scatter.1

commit v13 on v12

--- a/solution.py
+++ b/solution.py
@@ -181,9 +181,14 @@
     capacity = 4 * token_count // arm_count
     flat_codes = codes.T.reshape(-1)
     arm_ids = jnp.arange(arm_count, dtype=jnp.int32)
-    onehot = (flat_codes[:, None] == arm_ids[None, :]).astype(jnp.int32)
-    earlier = jnp.cumsum(onehot, axis=0) - onehot
-    slot = jnp.sum(earlier * onehot, axis=1)
+    onehot = (flat_codes[:, None] == arm_ids[None, :]).astype(jnp.bfloat16)
+    count = flat_codes.shape[0]
+    before = (
+        lax.broadcasted_iota(jnp.int32, (count, count), 1)
+        < lax.broadcasted_iota(jnp.int32, (count, count), 0)
+    ).astype(jnp.bfloat16)
+    earlier = jnp.dot(before, onehot, preferred_element_type=jnp.float32)
+    slot = jnp.sum(earlier * onehot.astype(jnp.float32), axis=1).astype(jnp.int32)
     tok_dest = flat_codes * (2 * capacity) + slot
     cot_dest = tok_dest + capacity
     cot_f = cotangent.astype(jnp.float32)

time: 121 us -> 120 us (level)
    unnamed x7 -> x6, local copies, waits for them, and re-layouts: 3.07 us -> 3.07 us
where the time goes in v13:
time: 120 us; the launch traced here: 119 us
  blocking collectives  85.8 us (72%)
  between operations  14.1 us (12%)
  Pallas kernels  9.09 us (8%)
  local copies, waits for them, and re-layouts  3.91 us (3%)
  matrix products  3.44 us (3%)
  other arithmetic  2.94 us (2%)
    all_to_all x1, blocking collectives, on_device(): got = lax.all_to_all(send, 'expert', 0, 0, tiled=True)  48.7 us
    all_to_all x1, blocking collectives, on_device(): lax.all_to_all(ret, 'expert', 0, 0, tiled=True).reshape(-1, feature_width)  37.2 us
    pallas_call x1, Pallas kernels, arm_math(): pl.pallas_call(arm_kernel, grid=(rows // block,), in_specs=[row_spec, row...  7.01 us
    unnamed x6, local copies, waits for them, and re-layouts  3.07 us
  transfers between devices with their start and end apart: 1, of which 0 were waited for; matrix products, arithmetic and copies ran while one was open for 2% of the time, Pallas kernels for 0%

profile of v13, /device:TPU:1, one launch (start us, length us, event | category | flops | bytes accessed | tf_op | source)
XLA Modules:
  0.0 119.4 jit_solution(144039506498980851)
XLA Ops:
  7.2 0.0 reduce-scatter.2.cloned.1.call-start
  7.2 1.0 fusion.4
  8.2 0.7 broadcast_add_fusion
  8.9 0.9 fusion.15
  9.8 1.7 %fusion.3 = bf16[128,8,512]{2,1,0:T(8,128)(2,1)S(1)} fusion(s32[512]{0:T(512)S(1)} %pad_add_fusion, bf16[128,512]{1,0:T(8,128)(2,1)S(1)} %get-tuple-element.24, bf16[128,512]{1,0:T(8,128)(2,1)S(1)} %get-tuple-element.23, bf16[128,512]{1,0:T(8,128)(2,1)} %param.6), kind=kOutput, calls=%fused_computation.4 | convolution fusion | flops 540016640 | bytes 1443840 | tf_op jit(solution)/shard_map/dot_general | solution.py:203
  11.5 48.7 %all_to_all.10 = bf16[128,8,512]{2,1,0:T(8,128)(2,1)S(1)} all-to-all(bf16[128,8,512]{2,1,0:T(8,128)(2,1)S(1)} %fusion.3), channel_id=1, replica_groups=mesh['dp'=4,'expert'=128] {'expert'}, dimensions={0} | all-to-all | bytes 2097152 | tf_op jit(solution)/shard_map/all_to_all | solution.py:207
  60.2 0.0 copy-start
  60.2 0.3 fusion.23
  60.6 0.1 squeeze_reshape.7.cot_ref
  60.7 0.1 squeeze_reshape.6.tok_ref
  60.8 0.6 copy-done
  61.4 0.0 copy-start.1
  61.4 1.2 %copy-done.1 = bf16[1,512,1024]{2,1,0:T(8,128)(2,1)S(1)} copy-done((bf16[1,512,1024]{2,1,0:T(8,128)(2,1)S(1)}, bf16[1,512,1024]{2,1,0:T(8,128)(2,1)}, u32[]{:S(2)}) %copy-start.1) | copy-done | bytes 1048600
  62.7 0.0 copy-start.2
  62.7 1.2 %copy-done.2 = bf16[1,1024,512]{2,1,0:T(8,128)(2,1)S(1)} copy-done((bf16[1,1024,512]{2,1,0:T(8,128)(2,1)S(1)}, bf16[1,1024,512]{2,1,0:T(8,128)(2,1)}, u32[]{:S(2)}) %copy-start.2) | copy-done | bytes 1048600
  63.9 7.0 %shard_map.101 = (bf16[512,512]{1,0:T(8,128)(2,1)S(1)}, bf16[512,512]{1,0:T(8,128)(2,1)S(1)}, bf16[3,512,1024]{2,1,0:T(8,128)(2,1)}) custom-call(bf16[512,512]{1,0:T(8,128)(2,1)S(1)} %squeeze_reshape.6.tok_ref, bf16[512,512]{1,0:T(8,128)(2,1)S(1)} %squeeze_reshape.7.cot_ref, bf16[512,1024]{1,0:T(8,128)(2,1)S(1)} %bitcast.16, bf16[512,1024]{1,0:T(8,128)(2,1)S(1)} %bitcast.17, ...), custom_call_target="tpu_custom_call" | custom-call | flops 4831838208 | bytes 8388608 | tf_op jit(solution)/shard_map/pallas_call | solution.py:128
  70.9 0.0 reduce-scatter.2.cloned.1.call-update
  70.9 0.1 reshape.38
  71.0 0.1 reshape.39
  71.2 0.5 pad_maximum_fusion
  71.7 37.2 %all_to_all.11 = bf16[128,8,512]{2,1,0:T(8,128)(2,1)S(1)} all-to-all(bf16[128,8,512]{2,1,0:T(8,128)(2,1)S(1)} %pad_maximum_fusion), channel_id=1, replica_groups=mesh['dp'=4,'expert'=128] {'expert'}, dimensions={0} | all-to-all | bytes 2097152 | tf_op jit(solution)/shard_map/all_to_all | solution.py:221
  108.9 0.8 fusion
  109.6 0.8 fusion.17
  110.4 0.0 reduce-scatter.2.cloned.1.call-done.summed_ref
  110.4 2.1 %shard_map.102 = (bf16[512,256]{1,0:T(8,128)(2,1)}, bf16[512,256]{1,0:T(8,128)(2,1)}, bf16[256,512]{1,0:T(8,128)(2,1)}) custom-call(bf16[3,512,256]{2,1,0:T(8,128)(2,1)} %reduce-scatter.2.cloned.1.call-done.summed_ref), custom_call_target="tpu_custom_call" | custom-call | tf_op jit(solution)/shard_map/pallas_call | solution.py:165
  (1 shorter events, 0.0 us)
Async XLA Ops:
  7.2 103.3 %reduce-scatter.2.cloned.1.call-start = ((), (), s32[]{:S(2)}) async-start(), calls=%async_computation.3 | async-start | bytes 3932160 | tf_op jit(solution)/shard_map/reduce_scatter | solution.py:228
  60.2 1.2 %copy-start = (bf16[1,512,1024]{2,1,0:T(8,128)(2,1)S(1)}, bf16[1,512,1024]{2,1,0:T(8,128)(2,1)}, u32[]{:S(2)}) copy-start(bf16[1,512,1024]{2,1,0:T(8,128)(2,1)} %param.9) | copy-start | bytes 3145732
  61.4 1.2 %copy-start.1 = (bf16[1,512,1024]{2,1,0:T(8,128)(2,1)S(1)}, bf16[1,512,1024]{2,1,0:T(8,128)(2,1)}, u32[]{:S(2)}) copy-start(bf16[1,512,1024]{2,1,0:T(8,128)(2,1)} %param.10) | copy-start | bytes 3145732
  62.7 1.2 %copy-start.2 = (bf16[1,1024,512]{2,1,0:T(8,128)(2,1)S(1)}, bf16[1,1024,512]{2,1,0:T(8,128)(2,1)}, u32[]{:S(2)}) copy-start(bf16[1,1024,512]{2,1,0:T(8,128)(2,1)} %param.11) | copy-start | bytes 3145732
Sparse Core Ops, SparseCore 0:
  71.0 37.5 reduce-scatter.1

commit v14 on v13

--- a/solution.py
+++ b/solution.py
@@ -193,14 +193,17 @@
     cot_dest = tok_dest + capacity
     cot_f = cotangent.astype(jnp.float32)
     sources = jnp.concatenate(
-        [tokens, tokens, (cot_f * fact_share).astype(jnp.bfloat16), (cot_f * counter_share).astype(jnp.bfloat16)]
+        [tokens, (cot_f * fact_share).astype(jnp.bfloat16), (cot_f * counter_share).astype(jnp.bfloat16)]
     )
     dest = jnp.concatenate([tok_dest, cot_dest])
     place = (
         lax.broadcasted_iota(jnp.int32, (arm_count * 2 * capacity, dest.shape[0]), 0) == dest[None, :]
     ).astype(jnp.bfloat16)
+    place_in = jnp.concatenate(
+        [place[:, :token_count] + place[:, token_count : 2 * token_count], place[:, 2 * token_count :]], axis=1
+    )
     send = (
-        jnp.dot(place, sources, preferred_element_type=jnp.float32)
+        jnp.dot(place_in, sources, preferred_element_type=jnp.float32)
         .astype(jnp.bfloat16)
         .reshape(arm_count, 2 * capacity, feature_width)
     )

time: 120 us -> 118 us (0.983)
    unnamed x6 -> x10, local copies, waits for them, and re-layouts: 3.07 us -> 3.07 us
where the time goes in v14:
time: 118 us
  blocking collectives  85.8 us (73%)
  between operations  14.1 us (12%)
  Pallas kernels  9.08 us (8%)
  local copies, waits for them, and re-layouts  3.95 us (3%)
  other arithmetic  2.51 us (2%)
  matrix products  2.44 us (2%)
    all_to_all x1, blocking collectives, on_device(): got = lax.all_to_all(send, 'expert', 0, 0, tiled=True)  48.7 us
    all_to_all x1, blocking collectives, on_device(): lax.all_to_all(ret, 'expert', 0, 0, tiled=True).reshape(-1, feature_width)  37.2 us
    pallas_call x1, Pallas kernels, arm_math(): pl.pallas_call(arm_kernel, grid=(rows // block,), in_specs=[row_spec, row...  7 us
    unnamed x10, local copies, waits for them, and re-layouts  3.07 us
  transfers between devices with their start and end apart: 1, of which 0 were waited for; matrix products, arithmetic and copies ran while one was open for 2% of the time, Pallas kernels for 0%

profile of v14, /device:TPU:1, one launch (start us, length us, event | category | flops | bytes accessed | tf_op | source)
XLA Modules:
  0.0 118.0 jit_solution(14781128324918193595)
XLA Ops:
  7.2 0.0 copy-start.3
  7.2 0.0 copy-start.4
  7.2 0.0 reduce-scatter.2.cloned.1.call-start
  7.2 1.0 fusion.3
  8.2 0.7 broadcast_add_fusion
  8.9 0.4 fusion.1
  9.4 0.0 copy-done.3
  9.5 0.0 copy-done.4
  9.5 0.7 fusion.2
  10.2 48.7 %all_to_all.10 = bf16[128,8,512]{2,1,0:T(8,128)(2,1)S(1)} all-to-all(bf16[128,8,512]{2,1,0:T(8,128)(2,1)S(1)} %fusion.2), channel_id=1, replica_groups=mesh['dp'=4,'expert'=128] {'expert'}, dimensions={0} | all-to-all | bytes 2097152 | tf_op jit(solution)/shard_map/all_to_all | solution.py:210
  58.9 0.0 copy-start
  58.9 0.3 fusion.22
  59.2 0.1 squeeze_reshape.7.cot_ref
  59.3 0.1 squeeze_reshape.6.tok_ref
  59.5 0.6 copy-done
  60.1 0.0 copy-start.1
  60.1 1.2 %copy-done.1 = bf16[1,512,1024]{2,1,0:T(8,128)(2,1)S(1)} copy-done((bf16[1,512,1024]{2,1,0:T(8,128)(2,1)S(1)}, bf16[1,512,1024]{2,1,0:T(8,128)(2,1)}, u32[]{:S(2)}) %copy-start.1) | copy-done | bytes 1048600
  61.3 0.0 copy-start.2
  61.3 1.2 %copy-done.2 = bf16[1,1024,512]{2,1,0:T(8,128)(2,1)S(1)} copy-done((bf16[1,1024,512]{2,1,0:T(8,128)(2,1)S(1)}, bf16[1,1024,512]{2,1,0:T(8,128)(2,1)}, u32[]{:S(2)}) %copy-start.2) | copy-done | bytes 1048600
  62.5 7.0 %shard_map.101 = (bf16[512,512]{1,0:T(8,128)(2,1)S(1)}, bf16[512,512]{1,0:T(8,128)(2,1)S(1)}, bf16[3,512,1024]{2,1,0:T(8,128)(2,1)}) custom-call(bf16[512,512]{1,0:T(8,128)(2,1)S(1)} %squeeze_reshape.6.tok_ref, bf16[512,512]{1,0:T(8,128)(2,1)S(1)} %squeeze_reshape.7.cot_ref, bf16[512,1024]{1,0:T(8,128)(2,1)S(1)} %bitcast.16, bf16[512,1024]{1,0:T(8,128)(2,1)S(1)} %bitcast.17, ...), custom_call_target="tpu_custom_call" | custom-call | flops 4831838208 | bytes 8388608 | tf_op jit(solution)/shard_map/pallas_call | solution.py:128
  69.5 0.0 reduce-scatter.2.cloned.1.call-update
  69.6 0.1 reshape.38
  69.7 0.1 reshape.39
  69.8 0.5 pad_maximum_fusion
  70.3 37.2 %all_to_all.11 = bf16[128,8,512]{2,1,0:T(8,128)(2,1)S(1)} all-to-all(bf16[128,8,512]{2,1,0:T(8,128)(2,1)S(1)} %pad_maximum_fusion), channel_id=1, replica_groups=mesh['dp'=4,'expert'=128] {'expert'}, dimensions={0} | all-to-all | bytes 2097152 | tf_op jit(solution)/shard_map/all_to_all | solution.py:224
  107.5 0.8 fusion
  108.3 0.8 fusion.16
  109.1 0.0 reduce-scatter.2.cloned.1.call-done.summed_ref
  109.1 2.1 %shard_map.102 = (bf16[512,256]{1,0:T(8,128)(2,1)}, bf16[512,256]{1,0:T(8,128)(2,1)}, bf16[256,512]{1,0:T(8,128)(2,1)}) custom-call(bf16[3,512,256]{2,1,0:T(8,128)(2,1)} %reduce-scatter.2.cloned.1.call-done.summed_ref), custom_call_target="tpu_custom_call" | custom-call | tf_op jit(solution)/shard_map/pallas_call | solution.py:165
  (4 shorter events, 0.1 us)
Async XLA Ops:
  7.2 2.3 %copy-start.3 = (bf16[128,512]{1,0:T(8,128)(2,1)S(1)}, bf16[128,512]{1,0:T(8,128)(2,1)}, u32[]{:S(2)}) copy-start(bf16[128,512]{1,0:T(8,128)(2,1)} %param.8) | copy-start | bytes 393220
  7.2 2.3 %copy-start.4 = (bf16[128,512]{1,0:T(8,128)(2,1)S(1)}, bf16[128,512]{1,0:T(8,128)(2,1)}, u32[]{:S(2)}) copy-start(bf16[128,512]{1,0:T(8,128)(2,1)} %param.6) | copy-start | bytes 393220
  7.2 101.9 %reduce-scatter.2.cloned.1.call-start = ((), (), s32[]{:S(2)}) async-start(), calls=%async_computation.3 | async-start | bytes 3932160 | tf_op jit(solution)/shard_map/reduce_scatter | solution.py:231
  58.9 1.2 %copy-start = (bf16[1,512,1024]{2,1,0:T(8,128)(2,1)S(1)}, bf16[1,512,1024]{2,1,0:T(8,128)(2,1)}, u32[]{:S(2)}) copy-start(bf16[1,512,1024]{2,1,0:T(8,128)(2,1)} %param.9) | copy-start | bytes 3145732
  60.1 1.2 %copy-start.1 = (bf16[1,512,1024]{2,1,0:T(8,128)(2,1)S(1)}, bf16[1,512,1024]{2,1,0:T(8,128)(2,1)}, u32[]{:S(2)}) copy-start(bf16[1,512,1024]{2,1,0:T(8,128)(2,1)} %param.10) | copy-start | bytes 3145732
  61.3 1.2 %copy-start.2 = (bf16[1,1024,512]{2,1,0:T(8,128)(2,1)S(1)}, bf16[1,1024,512]{2,1,0:T(8,128)(2,1)}, u32[]{:S(2)}) copy-start(bf16[1,1024,512]{2,1,0:T(8,128)(2,1)} %param.11) | copy-start | bytes 3145732
Sparse Core Ops, SparseCore 0:
  69.7 37.5 reduce-scatter.1

commit v15 on v14

--- a/solution.py
+++ b/solution.py
@@ -172,6 +172,25 @@
             jax.ShapeDtypeStruct((part, width), summed.dtype),
         ],
     )(summed)
+
+
+def pick_kernel(tokens, place_ref, back_ref, head_ref, grad_ref):
+    picked = contract_rows(place_ref[...], back_ref[...])
+    head_ref[...] = (
+        fact_share * picked[:tokens] + counter_share * picked[tokens : 2 * tokens]
+    ).astype(head_ref.dtype)
+    grad_ref[...] = (picked[2 * tokens : 3 * tokens] + picked[3 * tokens :]).astype(grad_ref.dtype)
+
+
+def pick_back(place, back, tokens):
+    vmem = pl.BlockSpec(memory_space=pltpu.VMEM)
+    row = jax.ShapeDtypeStruct((tokens, back.shape[1]), jnp.bfloat16)
+    return pl.pallas_call(
+        functools.partial(pick_kernel, tokens),
+        in_specs=[vmem, vmem],
+        out_specs=[vmem, vmem],
+        out_shape=[row, row],
+    )(place, back)
 
 
 def on_device(tokens, codes, cotangent, w_gate, w_up, w_down):
@@ -222,11 +241,7 @@
         axis=1,
     )
     back = lax.all_to_all(ret, "expert", 0, 0, tiled=True).reshape(-1, feature_width)
-    picked = lax.dot_general(
-        place, back, (((0,), (0,)), ((), ())), preferred_element_type=jnp.float32
-    ).reshape(4, token_count, feature_width)
-    head_output = (fact_share * picked[0] + counter_share * picked[1]).astype(jnp.bfloat16)
-    grad_tokens = (picked[2] + picked[3]).astype(jnp.bfloat16)
+    head_output, grad_tokens = pick_back(place, back, token_count)
 
     summed = lax.psum_scatter(partials, "dp", scatter_dimension=2, tiled=True)
     grad_gate, grad_up, grad_down = (g[None] for g in split_grads(summed))

time: 118 us -> 121 us (1.025)
  Pallas kernels: 9.08 us -> 12 us
    pallas_call x0 -> x1, Pallas kernels: none -> 2.93 us  [pick_back(): pl.pallas_call(functools.partial(pick_kernel, tokens), in_specs=[vmem, vm...]
    unnamed x10 -> x12, local copies, waits for them, and re-layouts: 3.07 us -> 4.02 us
  transfers between devices with their start and end apart: 1 -> 1, of which waited for: 0 -> 0; matrix products, arithmetic and copies ran while one was open for 2% -> 1% of each run, Pallas kernels for 0% -> 2%
where the time goes in v15:
time: 121 us; the launch traced here: 120 us
  blocking collectives  85.9 us (71%)
  between operations  14.1 us (12%)
  Pallas kernels  12 us (10%)
  local copies, waits for them, and re-layouts  4.89 us (4%)
  other arithmetic  1.71 us (1%)
  matrix products  1.69 us (1%)
    all_to_all x1, blocking collectives, on_device(): got = lax.all_to_all(send, 'expert', 0, 0, tiled=True)  48.7 us
    all_to_all x1, blocking collectives, on_device(): lax.all_to_all(ret, 'expert', 0, 0, tiled=True).reshape(-1, feature_width)  37.3 us
    pallas_call x1, Pallas kernels, arm_math(): pl.pallas_call(arm_kernel, grid=(rows // block,), in_specs=[row_spec, row...  6.99 us
    unnamed x12, local copies, waits for them, and re-layouts  4.02 us
    pallas_call x1, Pallas kernels, pick_back(): pl.pallas_call(functools.partial(pick_kernel, tokens), in_specs=[vmem, vm...  2.93 us
  transfers between devices with their start and end apart: 1, of which 0 were waited for; matrix products, arithmetic and copies ran while one was open for 1% of the time, Pallas kernels for 2%

profile of v15, /device:TPU:1, one launch (start us, length us, event | category | flops | bytes accessed | tf_op | source)
XLA Modules:
  0.0 120.4 jit_solution(10245834383031135704)
XLA Ops:
  7.2 0.0 copy-start.4
  7.2 0.0 copy-start.5
  7.2 0.0 reduce-scatter.2.cloned.1.call-start
  7.2 1.0 fusion.2
  8.2 0.7 broadcast_add_fusion
  8.9 0.4 fusion.place_ref
  9.3 0.0 copy-start.3
  9.4 0.9 copy-done.3
  10.4 0.0 copy-done.4
  10.4 0.0 copy-done.5
  10.4 0.7 fusion.1
  11.2 48.7 %all_to_all.10 = bf16[128,8,512]{2,1,0:T(8,128)(2,1)S(1)} all-to-all(bf16[128,8,512]{2,1,0:T(8,128)(2,1)S(1)} %fusion.1), channel_id=1, replica_groups=mesh['dp'=4,'expert'=128] {'expert'}, dimensions={0} | all-to-all | bytes 2097152 | tf_op jit(solution)/shard_map/all_to_all | solution.py:229
  59.8 0.0 copy-start
  59.8 0.3 fusion.16
  60.2 0.1 squeeze_reshape.7.cot_ref
  60.3 0.1 squeeze_reshape.6.tok_ref
  60.4 0.6 copy-done
  61.0 0.0 copy-start.1
  61.0 1.2 %copy-done.1 = bf16[1,512,1024]{2,1,0:T(8,128)(2,1)S(1)} copy-done((bf16[1,512,1024]{2,1,0:T(8,128)(2,1)S(1)}, bf16[1,512,1024]{2,1,0:T(8,128)(2,1)}, u32[]{:S(2)}) %copy-start.1) | copy-done | bytes 1048600
  62.3 0.0 copy-start.2
  62.3 1.2 %copy-done.2 = bf16[1,1024,512]{2,1,0:T(8,128)(2,1)S(1)} copy-done((bf16[1,1024,512]{2,1,0:T(8,128)(2,1)S(1)}, bf16[1,1024,512]{2,1,0:T(8,128)(2,1)}, u32[]{:S(2)}) %copy-start.2) | copy-done | bytes 1048600
  63.5 7.0 %shard_map.101 = (bf16[512,512]{1,0:T(8,128)(2,1)S(1)}, bf16[512,512]{1,0:T(8,128)(2,1)S(1)}, bf16[3,512,1024]{2,1,0:T(8,128)(2,1)}) custom-call(bf16[512,512]{1,0:T(8,128)(2,1)S(1)} %squeeze_reshape.6.tok_ref, bf16[512,512]{1,0:T(8,128)(2,1)S(1)} %squeeze_reshape.7.cot_ref, bf16[512,1024]{1,0:T(8,128)(2,1)S(1)} %bitcast.14, bf16[512,1024]{1,0:T(8,128)(2,1)S(1)} %bitcast.15, ...), custom_call_target="tpu_custom_call" | custom-call | flops 4831838208 | bytes 8388608 | tf_op jit(solution)/shard_map/pallas_call | solution.py:128
  70.5 0.0 reduce-scatter.2.cloned.1.call-update
  70.5 0.1 reshape.29
  70.6 0.1 reshape.30
  70.8 0.5 pad_maximum_fusion
  71.3 37.3 %all_to_all.11 = bf16[128,8,512]{2,1,0:T(8,128)(2,1)} all-to-all(bf16[128,8,512]{2,1,0:T(8,128)(2,1)S(1)} %pad_maximum_fusion), channel_id=1, replica_groups=mesh['dp'=4,'expert'=128] {'expert'}, dimensions={0} | all-to-all | bytes 2097152 | tf_op jit(solution)/shard_map/all_to_all | solution.py:243
  108.6 2.9 %shard_map.102 = (bf16[128,512]{1,0:T(8,128)(2,1)}, bf16[128,512]{1,0:T(8,128)(2,1)}) custom-call(bf16[1024,512]{1,0:T(8,128)(2,1)} %copy-done.3, bf16[1024,512]{1,0:T(8,128)(2,1)} %bitcast.17), custom_call_target="tpu_custom_call" | custom-call | tf_op jit(solution)/shard_map/pallas_call | solution.py:188
  111.5 0.0 reduce-scatter.2.cloned.1.call-done.summed_ref
  111.5 2.1 %shard_map.103 = (bf16[512,256]{1,0:T(8,128)(2,1)}, bf16[512,256]{1,0:T(8,128)(2,1)}, bf16[256,512]{1,0:T(8,128)(2,1)}) custom-call(bf16[3,512,256]{2,1,0:T(8,128)(2,1)} %reduce-scatter.2.cloned.1.call-done.summed_ref), custom_call_target="tpu_custom_call" | custom-call | tf_op jit(solution)/shard_map/pallas_call | solution.py:165
  (4 shorter events, 0.1 us)
Async XLA Ops:
  7.2 3.2 %copy-start.4 = (bf16[128,512]{1,0:T(8,128)(2,1)S(1)}, bf16[128,512]{1,0:T(8,128)(2,1)}, u32[]{:S(2)}) copy-start(bf16[128,512]{1,0:T(8,128)(2,1)} %param.8) | copy-start | bytes 393220
  7.2 3.3 %copy-start.5 = (bf16[128,512]{1,0:T(8,128)(2,1)S(1)}, bf16[128,512]{1,0:T(8,128)(2,1)}, u32[]{:S(2)}) copy-start(bf16[128,512]{1,0:T(8,128)(2,1)} %param.6) | copy-start | bytes 393220
  7.2 104.3 %reduce-scatter.2.cloned.1.call-start = ((), (), s32[]{:S(2)}) async-start(), calls=%async_computation.3 | async-start | bytes 3932160 | tf_op jit(solution)/shard_map/reduce_scatter | solution.py:246
  9.3 1.0 copy-start.3
  59.8 1.2 %copy-start = (bf16[1,512,1024]{2,1,0:T(8,128)(2,1)S(1)}, bf16[1,512,1024]{2,1,0:T(8,128)(2,1)}, u32[]{:S(2)}) copy-start(bf16[1,512,1024]{2,1,0:T(8,128)(2,1)} %param.9) | copy-start | bytes 3145732
  61.0 1.2 %copy-start.1 = (bf16[1,512,1024]{2,1,0:T(8,128)(2,1)S(1)}, bf16[1,512,1024]{2,1,0:T(8,128)(2,1)}, u32[]{:S(2)}) copy-start(bf16[1,512,1024]{2,1,0:T(8,128)(2,1)} %param.10) | copy-start | bytes 3145732
  62.3 1.2 %copy-start.2 = (bf16[1,1024,512]{2,1,0:T(8,128)(2,1)S(1)}, bf16[1,1024,512]{2,1,0:T(8,128)(2,1)}, u32[]{:S(2)}) copy-start(bf16[1,1024,512]{2,1,0:T(8,128)(2,1)} %param.11) | copy-start | bytes 3145732
Sparse Core Ops, SparseCore 0:
  70.6 37.6 reduce-scatter.1

commit v16 on v14

--- a/solution.py
+++ b/solution.py
@@ -83,16 +83,7 @@
     return lax.dot_general(a, b, (((1,), (1,)), ((), ())), preferred_element_type=jnp.float32)
 
 
-def arm_kernel(tok_ref, cot_ref, wg_ref, wu_ref, wd_ref, out_ref, inp_ref, part_ref, acc_g, acc_u, acc_d):
-    step = pl.program_id(0)
-    hidden_width = wg_ref.shape[1]
-
-    @pl.when(step == 0)
-    def _():
-        acc_g[...] = jnp.zeros_like(acc_g)
-        acc_u[...] = jnp.zeros_like(acc_u)
-        acc_d[...] = jnp.zeros_like(acc_d)
-
+def arm_kernel(tok_ref, cot_ref, wg_ref, wu_ref, wd_ref, out_ref, inp_ref, part_ref):
     x = tok_ref[...]
     c = cot_ref[...]
     wg = wg_ref[...]
@@ -107,21 +98,15 @@
     d_up = (d_hidden * activated).astype(jnp.bfloat16)
     d_gate = (d_hidden * up_pre * silu_slope).astype(jnp.bfloat16)
     inp_ref[...] = (contract_cols(d_gate, wg) + contract_cols(d_up, wu)).astype(inp_ref.dtype)
-    acc_g[...] += contract_rows(x, d_gate)
-    acc_u[...] += contract_rows(x, d_up)
-    acc_d[...] += contract_rows(c, hidden)
-
-    @pl.when(step == pl.num_programs(0) - 1)
-    def _():
-        part_ref[0] = acc_g[...].astype(part_ref.dtype)
-        part_ref[1] = acc_u[...].astype(part_ref.dtype)
-        part_ref[2] = acc_d[...].astype(part_ref.dtype)
+    part_ref[0] = contract_rows(x, d_gate).astype(part_ref.dtype)
+    part_ref[1] = contract_rows(x, d_up).astype(part_ref.dtype)
+    part_ref[2] = contract_rows(c, hidden).astype(part_ref.dtype)
 
 
 def arm_math(tokens, cot, wg, wu, wd):
     rows, width = tokens.shape
     hidden_width = wg.shape[1]
-    block = 512
+    block = rows
     row_spec = pl.BlockSpec((block, width), lambda i: (i, 0))
     whole = lambda shape: pl.BlockSpec(shape, lambda i: (0, 0))
     flops = 2 * rows * width * hidden_width * 9
@@ -138,11 +123,6 @@
             jax.ShapeDtypeStruct((rows, width), jnp.bfloat16),
             jax.ShapeDtypeStruct((rows, width), jnp.bfloat16),
             jax.ShapeDtypeStruct((3, width, hidden_width), jnp.bfloat16),
-        ],
-        scratch_shapes=[
-            pltpu.VMEM((width, hidden_width), jnp.float32),
-            pltpu.VMEM((width, hidden_width), jnp.float32),
-            pltpu.VMEM((width, hidden_width), jnp.float32),
         ],
         compiler_params=pltpu.CompilerParams(
             dimension_semantics=("arbitrary",), vmem_limit_bytes=48 * 1024 * 1024

time: 118 us -> 118 us (level)
  no operation moved by 1% of the time
where the time goes in v16:
time: 118 us
  blocking collectives  85.8 us (73%)
  between operations  14.1 us (12%)
  Pallas kernels  9.08 us (8%)
  local copies, waits for them, and re-layouts  3.95 us (3%)
  other arithmetic  2.51 us (2%)
  matrix products  2.44 us (2%)
    all_to_all x1, blocking collectives, on_device(): got = lax.all_to_all(send, 'expert', 0, 0, tiled=True)  48.7 us
    all_to_all x1, blocking collectives, on_device(): lax.all_to_all(ret, 'expert', 0, 0, tiled=True).reshape(-1, feature_width)  37.2 us
    pallas_call x1, Pallas kernels, arm_math(): pl.pallas_call(arm_kernel, grid=(rows // block,), in_specs=[row_spec, row...  7 us
    unnamed x10, local copies, waits for them, and re-layouts  3.07 us
  transfers between devices with their start and end apart: 1, of which 0 were waited for; matrix products, arithmetic and copies ran while one was open for 2% of the time, Pallas kernels for 0%

profile of v16, /device:TPU:1, one launch (start us, length us, event | category | flops | bytes accessed | tf_op | source)
XLA Modules:
  0.0 118.0 jit_solution(14781128324918193595)
XLA Ops:
  7.2 0.0 copy-start.3
  7.2 0.0 copy-start.4
  7.2 0.0 reduce-scatter.2.cloned.1.call-start
  7.2 1.0 fusion.3
  8.2 0.7 broadcast_add_fusion
  8.9 0.4 fusion.1
  9.4 0.0 copy-done.3
  9.5 0.0 copy-done.4
  9.5 0.7 fusion.2
  10.2 48.7 %all_to_all.10 = bf16[128,8,512]{2,1,0:T(8,128)(2,1)S(1)} all-to-all(bf16[128,8,512]{2,1,0:T(8,128)(2,1)S(1)} %fusion.2), channel_id=1, replica_groups=mesh['dp'=4,'expert'=128] {'expert'}, dimensions={0} | all-to-all | bytes 2097152 | tf_op jit(solution)/shard_map/all_to_all | solution.py:190
  58.9 0.0 copy-start
  58.9 0.3 fusion.22
  59.2 0.1 squeeze_reshape.7.cot_ref
  59.3 0.1 squeeze_reshape.6.tok_ref
  59.5 0.6 copy-done
  60.1 0.0 copy-start.1
  60.1 1.2 %copy-done.1 = bf16[1,512,1024]{2,1,0:T(8,128)(2,1)S(1)} copy-done((bf16[1,512,1024]{2,1,0:T(8,128)(2,1)S(1)}, bf16[1,512,1024]{2,1,0:T(8,128)(2,1)}, u32[]{:S(2)}) %copy-start.1) | copy-done | bytes 1048600
  61.3 0.0 copy-start.2
  61.3 1.2 %copy-done.2 = bf16[1,1024,512]{2,1,0:T(8,128)(2,1)S(1)} copy-done((bf16[1,1024,512]{2,1,0:T(8,128)(2,1)S(1)}, bf16[1,1024,512]{2,1,0:T(8,128)(2,1)}, u32[]{:S(2)}) %copy-start.2) | copy-done | bytes 1048600
  62.5 7.0 %shard_map.101 = (bf16[512,512]{1,0:T(8,128)(2,1)S(1)}, bf16[512,512]{1,0:T(8,128)(2,1)S(1)}, bf16[3,512,1024]{2,1,0:T(8,128)(2,1)}) custom-call(bf16[512,512]{1,0:T(8,128)(2,1)S(1)} %squeeze_reshape.6.tok_ref, bf16[512,512]{1,0:T(8,128)(2,1)S(1)} %squeeze_reshape.7.cot_ref, bf16[512,1024]{1,0:T(8,128)(2,1)S(1)} %bitcast.16, bf16[512,1024]{1,0:T(8,128)(2,1)S(1)} %bitcast.17, ...), custom_call_target="tpu_custom_call" | custom-call | flops 4831838208 | bytes 8388608 | tf_op jit(solution)/shard_map/pallas_call | solution.py:113
  69.5 0.0 reduce-scatter.2.cloned.1.call-update
  69.6 0.1 reshape.38
  69.7 0.1 reshape.39
  69.8 0.5 pad_maximum_fusion
  70.3 37.2 %all_to_all.11 = bf16[128,8,512]{2,1,0:T(8,128)(2,1)S(1)} all-to-all(bf16[128,8,512]{2,1,0:T(8,128)(2,1)S(1)} %pad_maximum_fusion), channel_id=1, replica_groups=mesh['dp'=4,'expert'=128] {'expert'}, dimensions={0} | all-to-all | bytes 2097152 | tf_op jit(solution)/shard_map/all_to_all | solution.py:204
  107.5 0.8 fusion
  108.3 0.8 fusion.16
  109.1 0.0 reduce-scatter.2.cloned.1.call-done.summed_ref
  109.1 2.1 %shard_map.102 = (bf16[512,256]{1,0:T(8,128)(2,1)}, bf16[512,256]{1,0:T(8,128)(2,1)}, bf16[256,512]{1,0:T(8,128)(2,1)}) custom-call(bf16[3,512,256]{2,1,0:T(8,128)(2,1)} %reduce-scatter.2.cloned.1.call-done.summed_ref), custom_call_target="tpu_custom_call" | custom-call | tf_op jit(solution)/shard_map/pallas_call | solution.py:145
  (4 shorter events, 0.1 us)
Async XLA Ops:
  7.2 2.3 %copy-start.3 = (bf16[128,512]{1,0:T(8,128)(2,1)S(1)}, bf16[128,512]{1,0:T(8,128)(2,1)}, u32[]{:S(2)}) copy-start(bf16[128,512]{1,0:T(8,128)(2,1)} %param.8) | copy-start | bytes 393220
  7.2 2.3 %copy-start.4 = (bf16[128,512]{1,0:T(8,128)(2,1)S(1)}, bf16[128,512]{1,0:T(8,128)(2,1)}, u32[]{:S(2)}) copy-start(bf16[128,512]{1,0:T(8,128)(2,1)} %param.6) | copy-start | bytes 393220
  7.2 101.9 %reduce-scatter.2.cloned.1.call-start = ((), (), s32[]{:S(2)}) async-start(), calls=%async_computation.3 | async-start | bytes 3932160 | tf_op jit(solution)/shard_map/reduce_scatter | solution.py:211
  58.9 1.2 %copy-start = (bf16[1,512,1024]{2,1,0:T(8,128)(2,1)S(1)}, bf16[1,512,1024]{2,1,0:T(8,128)(2,1)}, u32[]{:S(2)}) copy-start(bf16[1,512,1024]{2,1,0:T(8,128)(2,1)} %param.9) | copy-start | bytes 3145732
  60.1 1.2 %copy-start.1 = (bf16[1,512,1024]{2,1,0:T(8,128)(2,1)S(1)}, bf16[1,512,1024]{2,1,0:T(8,128)(2,1)}, u32[]{:S(2)}) copy-start(bf16[1,512,1024]{2,1,0:T(8,128)(2,1)} %param.10) | copy-start | bytes 3145732
  61.3 1.2 %copy-start.2 = (bf16[1,1024,512]{2,1,0:T(8,128)(2,1)S(1)}, bf16[1,1024,512]{2,1,0:T(8,128)(2,1)}, u32[]{:S(2)}) copy-start(bf16[1,1024,512]{2,1,0:T(8,128)(2,1)} %param.11) | copy-start | bytes 3145732
Sparse Core Ops, SparseCore 0:
  69.7 37.5 reduce-scatter.1
